TPU v7x, 32 devices: a whole 2x2x4 slice. The times are simulated.
32 devices in a mesh: frag: 16 (over z, y, core), band: 2 (over x).
Axes of the slice: x: 2, y: 2, z: 4, core: 2. Of those that a mesh axis runs over, the one named last changes fastest.
Arguments:
- orbitals: bfloat16 [4096, 32768], P(('frag', 'band')), parts along dimension 0, may hold values from -40 to 40
- potential: float32 [524288], P('frag'), parts along dimension 0, may hold values from 0.5 to 3
Outputs:
- margin: float32 [4096, 256], P(('frag', 'band')), parts along dimension 0
- projected: float32 [4096, 256], P(('frag', 'band')), parts along dimension 0
- residuals: bfloat16 [4096, 32768], P(('frag', 'band')), parts along dimension 0
There are 16 independent parts, one for each index of `frag`. A program takes and returns all parts, laid end to end along the dimension named above; each array names one. Nothing has to cross between parts.
All inputs are finite; a program needn't handle non-finite values.
Results may differ from a plain program's by a relative error of at most 0.034.
Values may be sent and summed in bfloat16 or wider, within the bound.
No kernel may reach another device: no remote copies, remote signals or barrier semaphores. Data moves between devices by JAX's collectives and lax.ppermute only.
A program may use at most 192 MiB of HBM per device.

v0:
```python
import functools

import jax
import jax.numpy as jnp
from jax import lax
from jax.experimental import pallas as pl
from jax.experimental.pallas import tpu as pltpu
from jax.sharding import PartitionSpec as P


ROWS = 16
F32 = jnp.float32
BF16 = jnp.bfloat16
ANY = pl.ANY


def call(kernel, grid, in_specs, out_specs, out_shape, args, scratch=(), aliases={}, flops=0, limit=58):
    touched = sum(a.size * a.dtype.itemsize for a in args)
    return pl.pallas_call(
        kernel,
        out_shape=out_shape,
        grid_spec=pltpu.PrefetchScalarGridSpec(
            num_scalar_prefetch=1, grid=grid, in_specs=in_specs, out_specs=out_specs, scratch_shapes=scratch
        ),
        input_output_aliases=aliases,
        compiler_params=pltpu.CompilerParams(
            dimension_semantics=("arbitrary",), vmem_limit_bytes=limit * 2**20
        ),
        cost_estimate=pl.CostEstimate(flops=flops, bytes_accessed=touched, transcendentals=0),
    )(*args)


def near(ctr, left, right, pot, side):
    size = side * side
    z = lax.broadcasted_iota(jnp.int32, ctr.shape, 1) % side
    low = jnp.where(z == 0, pltpu.roll(ctr, size - side + 1, 1), pltpu.roll(ctr, 1, 1))
    high = jnp.where(z == side - 1, pltpu.roll(ctr, side - 1, 1), pltpu.roll(ctr, size - 1, 1))
    beside = (left + right) + (pltpu.roll(ctr, side, 1) + pltpu.roll(ctr, size - side, 1)) + (low + high)
    return (3.0 + pot) * ctr - 0.5 * beside


def rowdot(a, b):
    return lax.dot_general(a, b, (((1,), (1,)), ((), ())), preferred_element_type=F32)


def pack_body(at, src, dst):
    dst[...] = src[...]


def pack(orbitals, start, width, side):
    own, size = orbitals.shape[0], side * side
    return call(
        pack_body,
        (width,),
        [pl.BlockSpec((own, size), lambda i, at: (0, lax.rem(at[0] + i, side)))],
        pl.BlockSpec((own, size), lambda i, at: (0, i)),
        jax.ShapeDtypeStruct((own, width * size), BF16),
        (start, orbitals),
    )


def apply_body(side, at, left, ctr, right, pot, out, sums, both):
    own = ctr.shape[0]

    def some(r, _):
        rows = pl.ds(r * ROWS, ROWS)
        value = near(
            ctr[rows, :].astype(F32), left[rows, :].astype(F32), right[rows, :].astype(F32), pot[...], side
        )
        out[rows, :] = value.astype(BF16)
        return 0

    lax.fori_loop(0, own // ROWS, some, 0)
    both[:own, :] = out[...]
    both[own:, :] = ctr[...]

    @pl.when(pl.program_id(0) == 0)
    def _():
        sums[...] = jnp.zeros_like(sums)

    sums[...] += rowdot(both[...], ctr[...])


def apply_own(orbitals, potential, token, side):
    own, grid, size = orbitals.shape[0], orbitals.shape[1], side * side

    def plane(shift):
        return pl.BlockSpec((own, size), lambda i, at: (0, lax.rem(i + shift + side, side)))

    return call(
        functools.partial(apply_body, side),
        (side,),
        [plane(-1), plane(0), plane(1), pl.BlockSpec((1, size), lambda i, at: (0, i))],
        [plane(0), pl.BlockSpec((2 * own, own), lambda i, at: (0, 0))],
        [jax.ShapeDtypeStruct((own, grid), BF16), jax.ShapeDtypeStruct((2 * own, own), F32)],
        (token, orbitals, orbitals, orbitals, potential),
        scratch=[pltpu.VMEM((2 * own, size), BF16)],
        flops=4 * own * own * grid,
    )


def part_body(side, n, q0, first, last, at, own_ref, applied, pot, *refs):
    refs = list(refs)
    rems, olds, recent = refs[: n - 1], refs[n - 1 : 2 * n - 2], refs[2 * n - 2 : 3 * n - 3]
    refs = refs[3 * n - 3 :]
    before = None if first else refs.pop(0)
    outs, (ring, every, moved, total) = refs[:-4], refs[-4:]
    own = own_ref.shape[0]
    i = pl.program_id(0)

    @pl.when(i == 0)
    def _():
        for j in range(n - 1):
            rows = pl.ds(j * own, own)
            ring[(q0 - 2) % 3, rows, :] = olds[j][...]
            ring[(q0 - 1) % 3, rows, :] = recent[j][...]
        total[...] = jnp.zeros_like(total) if first else before[...]

    slot = lax.rem(q0 + i, 3)
    here = lax.rem(q0 + i + 2, 3)
    back = lax.rem(q0 + i + 1, 3)
    for j in range(n - 1):
        ring[slot, pl.ds(j * own, own), :] = rems[j][...]
    every[:own, :] = own_ref[...]
    moved[:own, :] = applied[...]

    def some(r, _):
        rows = pl.ds(r * ROWS, ROWS)
        ctr = ring[here, rows, :]
        value = near(
            ctr.astype(F32), ring[back, rows, :].astype(F32), ring[slot, rows, :].astype(F32), pot[...], side
        )
        there = pl.ds(pl.multiple_of(own + r * ROWS, ROWS), ROWS)
        every[there, :] = ctr
        moved[there, :] = value.astype(BF16)
        return 0

    lax.fori_loop(0, (n - 1) * own // ROWS, some, 0)
    total[...] += rowdot(moved[...], every[...])

    @pl.when(i == pl.num_programs(0) - 1)
    def _():
        if not last:
            outs[0][...] = total[...]
        else:
            for j in range(n):
                rows = total[((n - j) % n) * own : ((n - j) % n) * own + own, :]
                outs[j][...] = pltpu.roll(rows, j * own, 1) if j else rows


def part(orbitals, applied, potential, at, rems, previous, before, q0, width, last, side):
    own, size, n = orbitals.shape[0], side * side, len(rems) + 1
    total = n * own
    held = previous[0].shape[1] // size

    def plane():
        return pl.BlockSpec((own, size), lambda i, at: (0, lax.rem(at[0] + q0 + i - 2 + side, side)))

    def fixed(shape, column=0):
        return pl.BlockSpec(shape, lambda i, at: (0, column))

    first = before is None
    args = [at, orbitals, applied, potential, *rems, *previous, *previous] + ([] if first else [before])
    specs = [plane(), plane(), pl.BlockSpec((1, size), lambda i, at: (0, lax.rem(at[0] + q0 + i - 2 + side, side)))]
    specs += [pl.BlockSpec((own, size), lambda i, at: (0, i))] * (n - 1)
    specs += [fixed((own, size), held - 2)] * (n - 1) + [fixed((own, size), held - 1)] * (n - 1)
    specs += [] if first else [fixed((total, total))]
    shapes = [(own, total)] * n if last else [(total, total)]
    return call(
        functools.partial(part_body, side, n, q0, first, last),
        (width,),
        specs,
        [fixed(s) for s in shapes],
        [jax.ShapeDtypeStruct(s, F32) for s in shapes],
        tuple(args),
        scratch=[
            pltpu.VMEM((3, (n - 1) * own, size), BF16),
            pltpu.VMEM((total, size), BF16),
            pltpu.VMEM((total, size), BF16),
            pltpu.VMEM((total, total), F32),
        ],
        flops=2 * total * total * size * width,
        limit=32,
    )


def coef_body(n, at, sums, mine, *refs):
    got, (projected, coef, work) = refs[: n - 1], refs[n - 1 :]
    own = mine.shape[0]
    other = mine[:, own:]
    for g in got:
        other = other + g[...]
    work[:, :own] = sums[:own, :]
    work[:, own:] = other
    gram = sums[own:, :]
    same = lax.broadcasted_iota(jnp.int32, gram.shape, 0) == lax.broadcasted_iota(jnp.int32, gram.shape, 1)
    diagonal = jnp.sum(jnp.where(same, gram, 0.0), axis=1, keepdims=True)
    value = work[...]
    coef[...] = (value / diagonal).astype(BF16)
    projected[...] = pltpu.roll(value, at[0] * own, 1)


def coefficients(at, sums, mine, got):
    own, total = mine.shape
    n = total // own

    def whole(x):
        return pl.BlockSpec(x.shape, lambda i, at: (0, 0))

    shape = jax.ShapeDtypeStruct((own, total), F32)
    return call(
        functools.partial(coef_body, n),
        (1,),
        [whole(sums), whole(mine)] + [whole(g) for g in got],
        [whole(shape), whole(shape)],
        [shape, jax.ShapeDtypeStruct((own, total), BF16)],
        (at, sums, mine, *got),
        scratch=[pltpu.VMEM((own, total), F32)],
        limit=16,
    )


def rest_body(n, first, last, at, coef, own_ref, applied, *refs):
    refs = list(refs)
    rems, refs = refs[: n - 1], refs[n - 1 :]
    if not first:
        before, refs = refs[1], refs[2:]
    out, gram, every = refs
    own = own_ref.shape[0]
    i = pl.program_id(0)
    every[:own, :] = own_ref[...]
    for j in range(n - 1):
        every[(j + 1) * own : (j + 2) * own, :] = rems[j][...]
    mixed = jnp.dot(coef[...], every[...], preferred_element_type=F32)
    out[...] = (applied[...].astype(F32) - mixed).astype(BF16)

    @pl.when(i == 0)
    def _():
        gram[...] = jnp.zeros_like(gram) if first else before[...]

    gram[...] += rowdot(own_ref[...], every[...])
    if last:

        @pl.when(i == pl.num_programs(0) - 1)
        def _():
            gram[...] = pltpu.roll(gram[...], at[1] * own, 1)


def rest(at, coef, orbitals, applied, rems, carry, q0, width, last, side):
    own, grid, size, n = orbitals.shape[0], orbitals.shape[1], side * side, len(rems) + 1
    total = n * own

    def plane():
        return pl.BlockSpec((own, size), lambda i, at: (0, lax.rem(at[0] + q0 + i - 1 + side, side)))

    def fixed(shape):
        return pl.BlockSpec(shape, lambda i, at: (0, 0))

    first = carry is None
    args = [at, coef, orbitals, applied, *rems]
    specs = [fixed((own, total)), plane(), plane()]
    specs += [pl.BlockSpec((own, size), lambda i, at: (0, i))] * (n - 1)
    aliases = {}
    if not first:
        aliases = {len(args): 0}
        args += list(carry)
        specs += [pl.BlockSpec(memory_space=ANY), fixed((own, total))]
    return call(
        functools.partial(rest_body, n, first, last),
        (width,),
        specs,
        [plane(), fixed((own, total))],
        [jax.ShapeDtypeStruct((own, grid), BF16), jax.ShapeDtypeStruct((own, total), F32)],
        tuple(args),
        scratch=[pltpu.VMEM((total, size), BF16)],
        aliases=aliases,
        flops=4 * own * total * size * width,
        limit=16,
    )


def cuts(count):
    out = []
    while count:
        out.append(max(1, count // 2))
        count -= out[-1]
    return out


def plan(n, side):
    share = side // n
    widths = [2] + ([share - share // 2, share // 2] if share >= 4 else [share])
    widths.append((side - share - 2) // 4)
    after = cuts(side - sum(widths))
    starts = [sum((widths + after)[:c]) for c in range(len(widths + after))]
    both = list(zip(starts, widths + after))
    return both[: len(widths)], both[len(widths) :]


def shards(n, orbitals, potential):
    own, grid = orbitals.shape
    side = round(grid ** (1 / 3))
    share = side // n
    me = lax.axis_index("band")
    potential = potential.reshape(1, grid)

    def sent(q0, width):
        got = []
        for j in range(1, n):
            dest = lax.rem(me + n - j, n)
            start = lax.rem(dest * share + q0 - 1 + side, side).astype(jnp.int32).reshape(1)
            chunk = pack(orbitals, start, width, side)
            got.append(lax.ppermute(chunk, "band", [(k, (k - j) % n) for k in range(n)]))
        return got

    early, late = plan(n, side)
    at = jnp.stack([me * share, me]).astype(jnp.int32)
    chunks = [(q0, w, sent(q0, w)) for q0, w in early]
    applied, sums = apply_own(orbitals, potential, at, side)
    before = None
    for c in range(1, len(early) - 1):
        q0, w, rems = chunks[c]
        before = part(
            orbitals, applied, potential, at, rems, chunks[c - 1][2],
            None if before is None else before[0], q0, w, c == len(early) - 2, side,
        )
    mine, others = before[0], before[1:]
    got = []
    for j in range(1, n):
        perm = [(k, (k - j) % n) for k in range(n)]
        got.append(lax.ppermute(others[j - 1][:, own:], "band", perm))
    chunks += [(q0, w, sent(q0, w)) for q0, w in late]
    projected, coef = coefficients(at[1:], sums, mine, got)
    carry = None
    for c, (q0, w, rems) in enumerate(chunks):
        carry = rest(at, coef, orbitals, applied, rems, carry, q0, w, c == len(chunks) - 1, side)
    residuals, margin = carry
    return margin, projected, residuals


def solution(mesh):
    n, spec = mesh.shape["band"], P(("frag", "band"), None)

    def body(orbitals, potential):
        return shards(n, orbitals, potential)

    return jax.shard_map(
        body,
        mesh=mesh,
        in_specs=(spec, P("frag")),
        out_specs=(spec, spec, spec),
        check_vma=False,
    )
```

profile of v0, /device:TPU:0, one launch (start us, length us, event | category | flops | bytes accessed | tf_op | source)
XLA Modules:
  0.0 283.3 jit_solution(12227337006887794414)
XLA Ops:
  0.6 5.7 %shard_map.51 = bf16[128,8192]{1,0:T(8,128)(2,1)} custom-call(s32[1]{0:T(128)} %bitcast.4.at, bf16[128,32768]{1,0:T(8,128)(2,1)} %own_ref.21), custom_call_target="tpu_custom_call" | custom-call | bytes 8388612 | tf_op jit(solution)/shard_map/pallas_call | solution.py:19
  6.3 3.0 %collective-permute-start.1 = (bf16[128,8192]{1,0:T(8,128)(2,1)}, bf16[128,8192]{1,0:T(8,128)(2,1)S(1)}, u32[]{:S(2)}, u32[]{:S(2)}) collective-permute-start(bf16[128,8192]{1,0:T(8,128)(2,1)} %shard_map.51), channel_id=1, source_target_pairs={{0,1},{1,0},{2,3},{3,2},{4,5},{5,4},{6,7},{7,6},{8,9},{9,8},{10,11... | collective-permute-start | bytes 6291464 | tf_op jit(solution)/shard_map/ppermute | solution.py:313
  9.3 5.7 %shard_map.50 = bf16[128,8192]{1,0:T(8,128)(2,1)} custom-call(s32[1]{0:T(128)} %bitcast.3.at, bf16[128,32768]{1,0:T(8,128)(2,1)} %own_ref.21), custom_call_target="tpu_custom_call" | custom-call | bytes 8388612 | tf_op jit(solution)/shard_map/pallas_call | solution.py:19
  15.0 0.0 collective-permute-start
  15.0 4.0 %shard_map.60 = bf16[128,5120]{1,0:T(8,128)(2,1)} custom-call(s32[1]{0:T(128)} %bitcast.10.at, bf16[128,32768]{1,0:T(8,128)(2,1)} %own_ref.21), custom_call_target="tpu_custom_call" | custom-call | bytes 8388612 | tf_op jit(solution)/shard_map/pallas_call | solution.py:19
  19.0 2.0 collective-permute-start.8
  21.0 1.8 shard_map.52
  22.8 0.0 collective-permute-start.2
  22.8 2.9 %shard_map.61 = bf16[128,3072]{1,0:T(8,128)(2,1)} custom-call(s32[1]{0:T(128)} %bitcast.11.at, bf16[128,32768]{1,0:T(8,128)(2,1)} %own_ref.21), custom_call_target="tpu_custom_call" | custom-call | bytes 8388612 | tf_op jit(solution)/shard_map/pallas_call | solution.py:19
  25.6 2.0 collective-permute-start.9
  27.7 2.9 %shard_map.59 = bf16[128,3072]{1,0:T(8,128)(2,1)} custom-call(s32[1]{0:T(128)} %bitcast.9.at, bf16[128,32768]{1,0:T(8,128)(2,1)} %own_ref.21), custom_call_target="tpu_custom_call" | custom-call | bytes 8388612 | tf_op jit(solution)/shard_map/pallas_call | solution.py:19
  30.5 0.6 pad_add_fusion.at
  31.1 109.1 %collective-permute-done.2.refs_1_.refs_2_.refs_0_ = bf16[128,2048]{1,0:T(8,128)(2,1)S(1)} collective-permute-done((bf16[128,2048]{1,0:T(8,128)(2,1)}, bf16[128,2048]{1,0:T(8,128)(2,1)S(1)}, u32[]{:S(2)}, u32[]{:S(2)}) %collective-permute-start.2) | collective-permute-done | bytes 524320 | tf_op jit(solution)/shard_map/ppermute | solution.py:313
  140.2 2.0 collective-permute-start.7
  142.3 51.3 %shard_map.49 = (bf16[128,32768]{1,0:T(8,128)(2,1)}, f32[256,128]{1,0:T(8,128)}) custom-call(s32[2]{0:T(128)} %pad_add_fusion.at, bf16[128,32768]{1,0:T(8,128)(2,1)} %own_ref.21, bf16[128,32768]{1,0:T(8,128)(2,1)} %own_ref.21, bf16[128,32768]{1,0:T(8,128)(2,1)} %own_ref.21, f32[1,32768]{1,0:T(1,128)} %bitcast.12), custom_call_target="tpu_custom_call" | custom-call | flops 2147483648 | bytes 25296904 | tf_op jit(solution)/shard_map/pallas_call | solution.py:19
  193.6 0.0 collective-permute-done.1.refs_0_.refs_1_.refs_2_
  193.6 0.0 copy-start
  193.6 3.4 %copy-done = bf16[128,32768]{1,0:T(8,128)(2,1)S(1)} copy-done((bf16[128,32768]{1,0:T(8,128)(2,1)S(1)}, bf16[128,32768]{1,0:T(8,128)(2,1)}, u32[]{:S(2)}) %copy-start) | copy-done | bytes 8388632
  197.0 3.4 %copy-done.2 = bf16[128,32768]{1,0:T(8,128)(2,1)S(1)} copy-done((bf16[128,32768]{1,0:T(8,128)(2,1)S(1)}, bf16[128,32768]{1,0:T(8,128)(2,1)}, u32[]{:S(2)}) %copy-start.2) | copy-done | bytes 8388632
  200.4 13.8 %shard_map.53.refs_3_ = f32[256,256]{1,0:T(8,128)S(1)} custom-call(s32[2]{0:T(128)S(1)} %copy-done.8, bf16[128,32768]{1,0:T(8,128)(2,1)S(1)} %copy-done, bf16[128,32768]{1,0:T(8,128)(2,1)S(1)} %copy-done.2, f32[1,32768]{1,0:T(1,128)S(1)} %bitcast.13, bf16[128,8192]{1,0:T(8,128)(2,1)S(1)} %collective-permute-done.1.refs_0_.refs_1_.refs_2_, ...), custom_call_target="tpu_custom_call" | custom-call | flops 1073741824 | bytes 20054024 | tf_op jit(solution)/shard_map/pallas_call | solution.py:19
  214.2 0.0 collective-permute-done.refs_0_
  214.2 14.5 %shard_map.54 = (f32[128,256]{1,0:T(8,128)S(1)}, f32[128,256]{1,0:T(8,128)S(1)}) custom-call(s32[2]{0:T(128)S(1)} %copy-done.8, bf16[128,32768]{1,0:T(8,128)(2,1)S(1)} %copy-done, bf16[128,32768]{1,0:T(8,128)(2,1)S(1)} %copy-done.2, f32[1,32768]{1,0:T(1,128)S(1)} %bitcast.14, bf16[128,8192]{1,0:T(8,128)(2,1)} %collective-permute-done.refs_0_, ...), custom_call_target="tpu_custom_call" | custom-call | flops 1073741824 | bytes 23461896 | tf_op jit(solution)/shard_map/pallas_call | solution.py:19
  228.7 0.0 copy-start.6
  228.7 0.6 copy-done.6
  229.4 0.6 slice.3
  230.0 0.0 collective-permute-start.3
  230.0 1.7 shard_map.58
  231.7 2.0 collective-permute-start.6
  233.7 1.7 shard_map.57
  235.4 1.7 shard_map.56
  237.2 0.0 collective-permute-done.3.refs_0_
  237.2 0.0 collective-permute-start.5
  237.2 1.6 shard_map.55
  238.8 3.4 %copy-done.1 = bf16[128,32768]{1,0:T(8,128)(2,1)S(1)} copy-done((bf16[128,32768]{1,0:T(8,128)(2,1)S(1)}, bf16[128,32768]{1,0:T(8,128)(2,1)}, u32[]{:S(2)}) %copy-start.1) | copy-done | bytes 8388632
  242.2 3.4 %copy-done.3 = bf16[128,32768]{1,0:T(8,128)(2,1)S(1)} copy-done((bf16[128,32768]{1,0:T(8,128)(2,1)S(1)}, bf16[128,32768]{1,0:T(8,128)(2,1)}, u32[]{:S(2)}) %copy-start.3) | copy-done | bytes 8388632
  245.6 2.4 shard_map.62
  248.0 6.4 %shard_map.63 = (bf16[128,32768]{1,0:T(8,128)(2,1)}, f32[128,256]{1,0:T(8,128)S(1)}) custom-call(s32[2]{0:T(128)S(1)} %copy-done.8, bf16[128,256]{1,0:T(8,128)(2,1)S(1)} %get-tuple-element.31.coef, bf16[128,32768]{1,0:T(8,128)(2,1)S(1)} %copy-done.1, bf16[128,32768]{1,0:T(8,128)(2,1)S(1)} %copy-done.3, ...), custom_call_target="tpu_custom_call", output_to_operand_aliasing={{0}: (5, {})} | custom-call | flops 1073741824 | bytes 27459592 | tf_op jit(solution)/shard_map/pallas_call | solution.py:19
  254.4 0.0 collective-permute-done.9.refs_0_
  254.4 2.0 collective-permute-start.4
  256.4 8.1 %shard_map.64 = (bf16[128,32768]{1,0:T(8,128)(2,1)}, f32[128,256]{1,0:T(8,128)S(1)}) custom-call(s32[2]{0:T(128)S(1)} %copy-done.8, bf16[128,256]{1,0:T(8,128)(2,1)S(1)} %get-tuple-element.31.coef, bf16[128,32768]{1,0:T(8,128)(2,1)S(1)} %copy-done.1, bf16[128,32768]{1,0:T(8,128)(2,1)S(1)} %copy-done.3, ...), custom_call_target="tpu_custom_call", output_to_operand_aliasing={{0}: (5, {})} | custom-call | flops 1073741824 | bytes 27459592 | tf_op jit(solution)/shard_map/pallas_call | solution.py:19
  264.5 3.1 %shard_map.65 = (bf16[128,32768]{1,0:T(8,128)(2,1)}, f32[128,256]{1,0:T(8,128)S(1)}) custom-call(s32[2]{0:T(128)S(1)} %copy-done.8, bf16[128,256]{1,0:T(8,128)(2,1)S(1)} %get-tuple-element.31.coef, bf16[128,32768]{1,0:T(8,128)(2,1)S(1)} %copy-done.1, bf16[128,32768]{1,0:T(8,128)(2,1)S(1)} %copy-done.3, ...), custom_call_target="tpu_custom_call", output_to_operand_aliasing={{0}: (5, {})} | custom-call | flops 402653184 | bytes 26148872 | tf_op jit(solution)/shard_map/pallas_call | solution.py:19
  267.5 5.8 %shard_map.66 = (bf16[128,32768]{1,0:T(8,128)(2,1)}, f32[128,256]{1,0:T(8,128)S(1)}) custom-call(s32[2]{0:T(128)S(1)} %copy-done.8, bf16[128,256]{1,0:T(8,128)(2,1)S(1)} %get-tuple-element.31.coef, bf16[128,32768]{1,0:T(8,128)(2,1)S(1)} %copy-done.1, bf16[128,32768]{1,0:T(8,128)(2,1)S(1)} %copy-done.3, ...), custom_call_target="tpu_custom_call", output_to_operand_aliasing={{0}: (5, {})} | custom-call | flops 671088640 | bytes 26673160 | tf_op jit(solution)/shard_map/pallas_call | solution.py:19
  273.4 4.2 %shard_map.67 = (bf16[128,32768]{1,0:T(8,128)(2,1)}, f32[128,256]{1,0:T(8,128)S(1)}) custom-call(s32[2]{0:T(128)S(1)} %copy-done.8, bf16[128,256]{1,0:T(8,128)(2,1)S(1)} %get-tuple-element.31.coef, bf16[128,32768]{1,0:T(8,128)(2,1)S(1)} %copy-done.1, bf16[128,32768]{1,0:T(8,128)(2,1)S(1)} %copy-done.3, ...), custom_call_target="tpu_custom_call", output_to_operand_aliasing={{0}: (5, {})} | custom-call | flops 402653184 | bytes 26148872 | tf_op jit(solution)/shard_map/pallas_call | solution.py:19
  277.6 0.0 collective-permute-done.6.refs_0_
  277.6 2.5 shard_map.68
  280.1 1.5 shard_map.69
  281.6 0.0 collective-permute-done.4.refs_0_
  281.6 1.7 shard_map.70
  (18 shorter events, 0.0 us)
Async XLA Ops:
  6.3 187.3 %collective-permute-start.1 = (bf16[128,8192]{1,0:T(8,128)(2,1)}, bf16[128,8192]{1,0:T(8,128)(2,1)S(1)}, u32[]{:S(2)}, u32[]{:S(2)}) collective-permute-start(bf16[128,8192]{1,0:T(8,128)(2,1)} %shard_map.51), channel_id=1, source_target_pairs={{0,1},{1,0},{2,3},{3,2},{4,5},{5,4},{6,7},{7,6},{8,9},{9,8},{10,11... | collective-permute-start | bytes 6291464 | tf_op jit(solution)/shard_map/ppermute | solution.py:313
  15.0 199.2 %collective-permute-start = (bf16[128,8192]{1,0:T(8,128)(2,1)}, bf16[128,8192]{1,0:T(8,128)(2,1)}, u32[]{:S(2)}, u32[]{:S(2)}) collective-permute-start(bf16[128,8192]{1,0:T(8,128)(2,1)} %shard_map.50), channel_id=1, source_target_pairs={{0,1},{1,0},{2,3},{3,2},{4,5},{5,4},{6,7},{7,6},{8,9},{9,8},{10,11... | collective-permute-start | bytes 6291464 | tf_op jit(solution)/shard_map/ppermute | solution.py:313
  19.0 248.6 %collective-permute-start.8 = (bf16[128,5120]{1,0:T(8,128)(2,1)}, bf16[128,5120]{1,0:T(8,128)(2,1)}, u32[]{:S(2)}, u32[]{:S(2)}) collective-permute-start(bf16[128,5120]{1,0:T(8,128)(2,1)} %shard_map.60), channel_id=1, source_target_pairs={{0,1},{1,0},{2,3},{3,2},{4,5},{5,4},{6,7},{7,6},{8,9},{9,8},{10,11... | collective-permute-start | bytes 3932168 | tf_op jit(solution)/shard_map/ppermute | solution.py:313
  22.8 117.5 %collective-permute-start.2 = (bf16[128,2048]{1,0:T(8,128)(2,1)}, bf16[128,2048]{1,0:T(8,128)(2,1)S(1)}, u32[]{:S(2)}, u32[]{:S(2)}) collective-permute-start(bf16[128,2048]{1,0:T(8,128)(2,1)} %shard_map.52), channel_id=1, source_target_pairs={{0,1},{1,0},{2,3},{3,2},{4,5},{5,4},{6,7},{7,6},{8,9},{9,8},{10,11... | collective-permute-start | bytes 1572872 | tf_op jit(solution)/shard_map/ppermute | solution.py:313
  25.6 228.7 %collective-permute-start.9 = (bf16[128,3072]{1,0:T(8,128)(2,1)}, bf16[128,3072]{1,0:T(8,128)(2,1)S(1)}, u32[]{:S(2)}, u32[]{:S(2)}) collective-permute-start(bf16[128,3072]{1,0:T(8,128)(2,1)} %shard_map.61), channel_id=1, source_target_pairs={{0,1},{1,0},{2,3},{3,2},{4,5},{5,4},{6,7},{7,6},{8,9},{9,8},{10,11... | collective-permute-start | bytes 2359304 | tf_op jit(solution)/shard_map/ppermute | solution.py:313
  140.2 133.1 %collective-permute-start.7 = (bf16[128,3072]{1,0:T(8,128)(2,1)}, bf16[128,3072]{1,0:T(8,128)(2,1)}, u32[]{:S(2)}, u32[]{:S(2)}) collective-permute-start(bf16[128,3072]{1,0:T(8,128)(2,1)} %shard_map.59), channel_id=1, source_target_pairs={{0,1},{1,0},{2,3},{3,2},{4,5},{5,4},{6,7},{7,6},{8,9},{9,8},{10,11... | collective-permute-start | bytes 2359304 | tf_op jit(solution)/shard_map/ppermute | solution.py:313
  142.3 51.3 %copy-start.4 = (f32[32768]{0:T(1024)S(1)}, f32[32768]{0:T(1024)}, u32[]{:S(2)}) copy-start(f32[32768]{0:T(1024)} %param.3) | copy-start | bytes 393220
  142.3 51.3 %copy-start.8 = (s32[2]{0:T(128)S(1)}, s32[2]{0:T(128)}, u32[]{:S(2)}) copy-start(s32[2]{0:T(128)} %pad_add_fusion.at) | copy-start | bytes 28
  193.6 3.4 %copy-start = (bf16[128,32768]{1,0:T(8,128)(2,1)S(1)}, bf16[128,32768]{1,0:T(8,128)(2,1)}, u32[]{:S(2)}) copy-start(bf16[128,32768]{1,0:T(8,128)(2,1)} %own_ref.21) | copy-start | bytes 25165828
  197.0 3.4 %copy-start.2 = (bf16[128,32768]{1,0:T(8,128)(2,1)S(1)}, bf16[128,32768]{1,0:T(8,128)(2,1)}, u32[]{:S(2)}) copy-start(bf16[128,32768]{1,0:T(8,128)(2,1)} %get-tuple-element.28.applied) | copy-start | bytes 25165828
  228.7 0.7 copy-start.6
  230.0 7.2 %collective-permute-start.3 = (f32[128,128]{1,0:T(8,128)}, f32[128,128]{1,0:T(8,128)}, u32[]{:S(2)}, u32[]{:S(2)}) collective-permute-start(f32[128,128]{1,0:T(8,128)} %slice.3), channel_id=1, source_target_pairs={{0,1},{1,0},{2,3},{3,2},{4,5},{5,4},{6,7},{7,6},{8,9},{9,8},{10,11... | collective-permute-start | bytes 196616 | tf_op jit(solution)/shard_map/ppermute | solution.py:331
  231.7 45.9 %collective-permute-start.6 = (bf16[128,1024]{1,0:T(8,128)(2,1)}, bf16[128,1024]{1,0:T(8,128)(2,1)}, u32[]{:S(2)}, u32[]{:S(2)}) collective-permute-start(bf16[128,1024]{1,0:T(8,128)(2,1)} %shard_map.58), channel_id=1, source_target_pairs={{0,1},{1,0},{2,3},{3,2},{4,5},{5,4},{6,7},{7,6},{8,9},{9,8},{10,11... | collective-permute-start | bytes 786440 | tf_op jit(solution)/shard_map/ppermute | solution.py:313
  233.7 3.5 %copy-start.5 = (f32[256,128]{1,0:T(8,128)S(1)}, f32[256,128]{1,0:T(8,128)}, u32[]{:S(2)}) copy-start(f32[256,128]{1,0:T(8,128)} %get-tuple-element.27.sums) | copy-start | bytes 393220
  235.4 1.7 copy-start.9
  235.4 1.8 copy-start.7
  237.2 42.9 %collective-permute-start.5 = (bf16[128,1024]{1,0:T(8,128)(2,1)S(1)}, bf16[128,1024]{1,0:T(8,128)(2,1)S(1)}, u32[]{:S(2)}, u32[]{:S(2)}) collective-permute-start(bf16[128,1024]{1,0:T(8,128)(2,1)S(1)} %copy-done.9), channel_id=1, source_target_pairs={{0,1},{1,0},{2,3},{3,2},{4,5},{5,4},{6,7},{7,6},{8,9},{9,8},{10,11... | collective-permute-start | bytes 786440 | tf_op jit(solution)/shard_map/ppermute | solution.py:313
  238.8 3.4 %copy-start.1 = (bf16[128,32768]{1,0:T(8,128)(2,1)S(1)}, bf16[128,32768]{1,0:T(8,128)(2,1)}, u32[]{:S(2)}) copy-start(bf16[128,32768]{1,0:T(8,128)(2,1)} %own_ref.21) | copy-start | bytes 25165828
  242.2 3.4 %copy-start.3 = (bf16[128,32768]{1,0:T(8,128)(2,1)S(1)}, bf16[128,32768]{1,0:T(8,128)(2,1)}, u32[]{:S(2)}) copy-start(bf16[128,32768]{1,0:T(8,128)(2,1)} %get-tuple-element.28.applied) | copy-start | bytes 25165828
  248.0 6.4 %copy-start.10 = (bf16[128,1024]{1,0:T(8,128)(2,1)S(1)}, bf16[128,1024]{1,0:T(8,128)(2,1)}, u32[]{:S(2)}) copy-start(bf16[128,1024]{1,0:T(8,128)(2,1)} %shard_map.56) | copy-start | bytes 786436
  254.4 27.2 %collective-permute-start.4 = (bf16[128,1024]{1,0:T(8,128)(2,1)S(1)}, bf16[128,1024]{1,0:T(8,128)(2,1)S(1)}, u32[]{:S(2)}, u32[]{:S(2)}) collective-permute-start(bf16[128,1024]{1,0:T(8,128)(2,1)S(1)} %copy-done.10), channel_id=1, source_target_pairs={{0,1},{1,0},{2,3},{3,2},{4,5},{5,4},{6,7},{7,6},{8,9},{9,8},{10,11... | collective-permute-start | bytes 786440 | tf_op jit(solution)/shard_map/ppermute | solution.py:313
where the time goes:
time: 284 us; the launch traced here: 283 us
  Pallas kernels  145 us (51%)
  waiting for transfers between devices  109 us (38%)
  local copies, waits for them, and re-layouts  14.8 us (5%)
  starting transfers between devices  13 us (5%)
    pallas_call x22, Pallas kernels, call(): pl.pallas_call(kernel, out_shape=out_shape, grid_spec=pltpu.PrefetchScala...  145 us
    ppermute x9, waiting for transfers between devices, sent(): lax.ppermute(chunk, 'band', [(k, (k - j) % n) for k in range(n)])  109 us
    unnamed x22, local copies, waits for them, and re-layouts  14.2 us
    ppermute x9, starting transfers between devices, sent(): lax.ppermute(chunk, 'band', [(k, (k - j) % n) for k in range(n)])  13 us
  transfers between devices with their start and end apart: 10, of which 1 were waited for; matrix products, arithmetic and copies ran while one was open for 0% of the time, Pallas kernels for 49%

commit v1 on v0

--- a/solution.py
+++ b/solution.py
@@ -9,12 +9,14 @@
 
 
 ROWS = 16
+WHOLE = 2**20
 F32 = jnp.float32
 BF16 = jnp.bfloat16
 ANY = pl.ANY
 
 
 def call(kernel, grid, in_specs, out_specs, out_shape, args, scratch=(), aliases={}, flops=0, limit=58):
+    args = [pltpu.with_memory_space_constraint(a, pltpu.HBM) if a.size >= WHOLE else a for a in args]
     touched = sum(a.size * a.dtype.itemsize for a in args)
     return pl.pallas_call(
         kernel,
@@ -56,6 +58,32 @@
         pl.BlockSpec((own, size), lambda i, at: (0, i)),
         jax.ShapeDtypeStruct((own, width * size), BF16),
         (start, orbitals),
+    )
+
+
+def grab_body(width, size, side, at, src, dst, sems):
+    copies = []
+    for i in range(width):
+        column = pl.multiple_of(lax.rem(at[0] + i, side) * size, size)
+        copies.append(
+            pltpu.make_async_copy(src.at[:, pl.ds(column, size)], dst.at[:, pl.ds(i * size, size)], sems.at[i])
+        )
+    for copy in copies:
+        copy.start()
+    for copy in copies:
+        copy.wait()
+
+
+def grab(orbitals, start, width, side):
+    own, size = orbitals.shape[0], side * side
+    return call(
+        functools.partial(grab_body, width, size, side),
+        (1,),
+        [pl.BlockSpec(memory_space=ANY)],
+        pl.BlockSpec(memory_space=pltpu.VMEM),
+        pltpu.VMEM((own, width * size), BF16),
+        (start, orbitals),
+        scratch=[pltpu.SemaphoreType.DMA((width,))],
     )
 
 
@@ -289,8 +317,9 @@
 
 def plan(n, side):
     share = side // n
-    widths = [2] + ([share - share // 2, share // 2] if share >= 4 else [share])
-    widths.append((side - share - 2) // 4)
+    short = max(2, share // 4)
+    widths = [2] + ([share - short, short] if share >= 4 else [share])
+    widths.append((side - share - 2) // 3)
     after = cuts(side - sum(widths))
     starts = [sum((widths + after)[:c]) for c in range(len(widths + after))]
     both = list(zip(starts, widths + after))
@@ -304,18 +333,18 @@
     me = lax.axis_index("band")
     potential = potential.reshape(1, grid)
 
-    def sent(q0, width):
+    def sent(c, q0, width):
         got = []
         for j in range(1, n):
             dest = lax.rem(me + n - j, n)
             start = lax.rem(dest * share + q0 - 1 + side, side).astype(jnp.int32).reshape(1)
-            chunk = pack(orbitals, start, width, side)
+            chunk = (pack if c else grab)(orbitals, start, width, side)
             got.append(lax.ppermute(chunk, "band", [(k, (k - j) % n) for k in range(n)]))
         return got
 
     early, late = plan(n, side)
     at = jnp.stack([me * share, me]).astype(jnp.int32)
-    chunks = [(q0, w, sent(q0, w)) for q0, w in early]
+    chunks = [(q0, w, sent(c, q0, w)) for c, (q0, w) in enumerate(early)]
     applied, sums = apply_own(orbitals, potential, at, side)
     before = None
     for c in range(1, len(early) - 1):
@@ -329,7 +358,7 @@
     for j in range(1, n):
         perm = [(k, (k - j) % n) for k in range(n)]
         got.append(lax.ppermute(others[j - 1][:, own:], "band", perm))
-    chunks += [(q0, w, sent(q0, w)) for q0, w in late]
+    chunks += [(q0, w, sent(len(early) + c, q0, w)) for c, (q0, w) in enumerate(late)]
     projected, coef = coefficients(at[1:], sums, mine, got)
     carry = None
     for c, (q0, w, rems) in enumerate(chunks):

time: 284 us -> 251 us (0.88)
  waiting for transfers between devices: 109 us -> 83 us
  local copies, waits for them, and re-layouts: 14.8 us -> 1.29 us
  Pallas kernels: 145 us -> 151 us
    ppermute x9, waiting for transfers between devices: 109 us -> 83 us  [sent(): lax.ppermute(chunk, 'band', [(k, (k - j) % n) for k in range(n)])]
    unnamed x22 -> x14, local copies, waits for them, and re-layouts: 14.2 us -> 0.67 us
    pallas_call x22, Pallas kernels: 145 us -> 151 us  [call(): pl.pallas_call(kernel, out_shape=out_shape, grid_spec=pltpu.PrefetchScala...]
  transfers between devices with their start and end apart: 10 -> 10, of which waited for: 1 -> 1; matrix products, arithmetic and copies ran while one was open for 0% -> 0% of each run, Pallas kernels for 49% -> 56%
where the time goes in v1:
time: 251 us; the launch traced here: 250 us
  Pallas kernels  151 us (60%)
  waiting for transfers between devices  83 us (33%)
  starting transfers between devices  12.9 us (5%)
    pallas_call x22, Pallas kernels, call(): pl.pallas_call(kernel, out_shape=out_shape, grid_spec=pltpu.PrefetchScala...  151 us
    ppermute x9, waiting for transfers between devices, sent(): lax.ppermute(chunk, 'band', [(k, (k - j) % n) for k in range(n)])  83 us
    ppermute x9, starting transfers between devices, sent(): lax.ppermute(chunk, 'band', [(k, (k - j) % n) for k in range(n)])  12.7 us
  transfers between devices with their start and end apart: 10, of which 1 were waited for; matrix products, arithmetic and copies ran while one was open for 0% of the time, Pallas kernels for 56%

profile of v1, /device:TPU:0, one launch (start us, length us, event | category | flops | bytes accessed | tf_op | source)
XLA Modules:
  0.0 249.7 jit_solution(11544099512117765687)
XLA Ops:
  0.6 7.9 %shard_map.51 = bf16[128,12288]{1,0:T(8,128)(2,1)} custom-call(s32[1]{0:T(128)} %bitcast.4.at, bf16[128,32768]{1,0:T(8,128)(2,1)} %own_ref.21), custom_call_target="tpu_custom_call" | custom-call | bytes 8388612 | tf_op jit(solution)/shard_map/pallas_call | solution.py:21
  8.6 3.0 %collective-permute-start.1 = (bf16[128,12288]{1,0:T(8,128)(2,1)}, bf16[128,12288]{1,0:T(8,128)(2,1)}, u32[]{:S(2)}, u32[]{:S(2)}) collective-permute-start(bf16[128,12288]{1,0:T(8,128)(2,1)} %shard_map.51), channel_id=1, source_target_pairs={{0,1},{1,0},{2,3},{3,2},{4,5},{5,4},{6,7},{7,6},{8,9},{9,8},{10,11... | collective-permute-start | bytes 9437192 | tf_op jit(solution)/shard_map/ppermute | solution.py:342
  11.5 3.4 %shard_map.50 = bf16[128,4096]{1,0:T(8,128)(2,1)} custom-call(s32[1]{0:T(128)} %bitcast.3.at, bf16[128,32768]{1,0:T(8,128)(2,1)} %own_ref.21), custom_call_target="tpu_custom_call" | custom-call | bytes 8388612 | tf_op jit(solution)/shard_map/pallas_call | solution.py:21
  14.9 0.0 collective-permute-start
  14.9 4.0 %shard_map.60 = bf16[128,5120]{1,0:T(8,128)(2,1)} custom-call(s32[1]{0:T(128)} %bitcast.10.at, bf16[128,32768]{1,0:T(8,128)(2,1)} %own_ref.21), custom_call_target="tpu_custom_call" | custom-call | bytes 8388612 | tf_op jit(solution)/shard_map/pallas_call | solution.py:21
  18.9 2.0 collective-permute-start.8
  20.9 3.4 %shard_map.61 = bf16[128,4096]{1,0:T(8,128)(2,1)} custom-call(s32[1]{0:T(128)} %bitcast.11.at, bf16[128,32768]{1,0:T(8,128)(2,1)} %own_ref.21), custom_call_target="tpu_custom_call" | custom-call | bytes 8388612 | tf_op jit(solution)/shard_map/pallas_call | solution.py:21
  24.3 0.0 collective-permute-start.9
  24.3 1.0 shard_map.52
  25.4 2.1 collective-permute-start.2
  27.4 1.8 shard_map.59
  29.2 0.6 pad_add_fusion.at
  29.8 51.3 %shard_map.49 = (bf16[128,32768]{1,0:T(8,128)(2,1)}, f32[256,128]{1,0:T(8,128)}) custom-call(s32[2]{0:T(128)} %pad_add_fusion.at, bf16[128,32768]{1,0:T(8,128)(2,1)} %own_ref.21, bf16[128,32768]{1,0:T(8,128)(2,1)} %own_ref.21, bf16[128,32768]{1,0:T(8,128)(2,1)} %own_ref.21, f32[1,32768]{1,0:T(1,128)} %bitcast.12), custom_call_target="tpu_custom_call" | custom-call | flops 2147483648 | bytes 25296904 | tf_op jit(solution)/shard_map/pallas_call | solution.py:21
  81.1 83.0 %collective-permute-done.2.refs_1_.refs_2_.refs_0_ = bf16[128,2048]{1,0:T(8,128)(2,1)S(1)} collective-permute-done((bf16[128,2048]{1,0:T(8,128)(2,1)S(1)}, bf16[128,2048]{1,0:T(8,128)(2,1)S(1)}, u32[]{:S(2)}, u32[]{:S(2)}) %collective-permute-start.2) | collective-permute-done | bytes 524320 | tf_op jit(solution)/shard_map/ppermute | solution.py:342
  164.1 1.7 collective-permute-start.7
  165.9 0.0 collective-permute-done.1.refs_0_.refs_1_.refs_2_
  165.9 0.0 copy-done
  165.9 20.9 %shard_map.53.refs_3_ = f32[256,256]{1,0:T(8,128)S(1)} custom-call(s32[2]{0:T(128)S(1)} %copy-done.4, bf16[128,32768]{1,0:T(8,128)(2,1)} %own_ref.21, bf16[128,32768]{1,0:T(8,128)(2,1)} %get-tuple-element.28.applied, f32[1,32768]{1,0:T(1,128)S(1)} %bitcast.13, bf16[128,12288]{1,0:T(8,128)(2,1)} %collective-permute-done.1.refs_0_.refs_1_.refs_2_, ...), custom_call_target="tpu_custom_call" | custom-call | flops 1610612736 | bytes 21102600 | tf_op jit(solution)/shard_map/pallas_call | solution.py:21
  186.7 0.0 collective-permute-done.refs_0_
  186.8 8.2 %shard_map.54 = (f32[128,256]{1,0:T(8,128)S(1)}, f32[128,256]{1,0:T(8,128)S(1)}) custom-call(s32[2]{0:T(128)S(1)} %copy-done.4, bf16[128,32768]{1,0:T(8,128)(2,1)} %own_ref.21, bf16[128,32768]{1,0:T(8,128)(2,1)} %get-tuple-element.28.applied, f32[1,32768]{1,0:T(1,128)S(1)} %bitcast.14, bf16[128,4096]{1,0:T(8,128)(2,1)S(1)} %collective-permute-done.refs_0_, ...), custom_call_target="tpu_custom_call" | custom-call | flops 536870912 | bytes 24510472 | tf_op jit(solution)/shard_map/pallas_call | solution.py:21
  195.0 0.0 copy-start.2
  195.0 0.6 copy-done.2
  195.6 0.6 slice.3
  196.2 0.3 collective-permute-start.3
  196.5 1.7 shard_map.58
  198.2 1.7 collective-permute-start.6
  200.0 1.7 shard_map.57
  201.7 1.7 shard_map.56
  203.4 0.0 collective-permute-done.3.refs_0_
  203.4 0.3 collective-permute-start.5
  203.7 0.0 copy-done.1
  203.7 1.6 shard_map.55
  205.3 3.3 %shard_map.62 = (bf16[128,32768]{1,0:T(8,128)(2,1)}, f32[128,256]{1,0:T(8,128)S(1)}) custom-call(s32[2]{0:T(128)S(1)} %copy-done.4, bf16[128,256]{1,0:T(8,128)(2,1)S(1)} %get-tuple-element.31.coef, bf16[128,32768]{1,0:T(8,128)(2,1)} %own_ref.21, bf16[128,32768]{1,0:T(8,128)(2,1)} %get-tuple-element.28.applied, ...), custom_call_target="tpu_custom_call" | custom-call | flops 268435456 | bytes 17367048 | tf_op jit(solution)/shard_map/pallas_call | solution.py:21
  208.6 0.0 collective-permute-done.9.refs_0_
  208.6 1.8 collective-permute-start.4
  210.4 12.1 %shard_map.63 = (bf16[128,32768]{1,0:T(8,128)(2,1)}, f32[128,256]{1,0:T(8,128)S(1)}) custom-call(s32[2]{0:T(128)S(1)} %copy-done.4, bf16[128,256]{1,0:T(8,128)(2,1)S(1)} %get-tuple-element.31.coef, bf16[128,32768]{1,0:T(8,128)(2,1)} %own_ref.21, bf16[128,32768]{1,0:T(8,128)(2,1)} %get-tuple-element.28.applied, ...), custom_call_target="tpu_custom_call", output_to_operand_aliasing={{0}: (5, {})} | custom-call | flops 1610612736 | bytes 28508168 | tf_op jit(solution)/shard_map/pallas_call | solution.py:21
  222.5 5.0 %shard_map.64 = (bf16[128,32768]{1,0:T(8,128)(2,1)}, f32[128,256]{1,0:T(8,128)S(1)}) custom-call(s32[2]{0:T(128)S(1)} %copy-done.4, bf16[128,256]{1,0:T(8,128)(2,1)S(1)} %get-tuple-element.31.coef, bf16[128,32768]{1,0:T(8,128)(2,1)} %own_ref.21, bf16[128,32768]{1,0:T(8,128)(2,1)} %get-tuple-element.28.applied, ...), custom_call_target="tpu_custom_call", output_to_operand_aliasing={{0}: (5, {})} | custom-call | flops 536870912 | bytes 26411016 | tf_op jit(solution)/shard_map/pallas_call | solution.py:21
  227.5 5.1 %shard_map.65 = (bf16[128,32768]{1,0:T(8,128)(2,1)}, f32[128,256]{1,0:T(8,128)S(1)}) custom-call(s32[2]{0:T(128)S(1)} %copy-done.4, bf16[128,256]{1,0:T(8,128)(2,1)S(1)} %get-tuple-element.31.coef, bf16[128,32768]{1,0:T(8,128)(2,1)} %own_ref.21, bf16[128,32768]{1,0:T(8,128)(2,1)} %get-tuple-element.28.applied, ...), custom_call_target="tpu_custom_call", output_to_operand_aliasing={{0}: (5, {})} | custom-call | flops 536870912 | bytes 26411016 | tf_op jit(solution)/shard_map/pallas_call | solution.py:21
  232.6 0.0 collective-permute-done.8.refs_0_
  232.6 5.9 %shard_map.66 = (bf16[128,32768]{1,0:T(8,128)(2,1)}, f32[128,256]{1,0:T(8,128)S(1)}) custom-call(s32[2]{0:T(128)S(1)} %copy-done.4, bf16[128,256]{1,0:T(8,128)(2,1)S(1)} %get-tuple-element.31.coef, bf16[128,32768]{1,0:T(8,128)(2,1)} %own_ref.21, bf16[128,32768]{1,0:T(8,128)(2,1)} %get-tuple-element.28.applied, ...), custom_call_target="tpu_custom_call", output_to_operand_aliasing={{0}: (5, {})} | custom-call | flops 671088640 | bytes 26673160 | tf_op jit(solution)/shard_map/pallas_call | solution.py:21
  238.5 0.0 collective-permute-done.7.refs_0_
  238.5 3.3 %shard_map.67 = (bf16[128,32768]{1,0:T(8,128)(2,1)}, f32[128,256]{1,0:T(8,128)S(1)}) custom-call(s32[2]{0:T(128)S(1)} %copy-done.4, bf16[128,256]{1,0:T(8,128)(2,1)S(1)} %get-tuple-element.31.coef, bf16[128,32768]{1,0:T(8,128)(2,1)} %own_ref.21, bf16[128,32768]{1,0:T(8,128)(2,1)} %get-tuple-element.28.applied, ...), custom_call_target="tpu_custom_call", output_to_operand_aliasing={{0}: (5, {})} | custom-call | flops 268435456 | bytes 25886728 | tf_op jit(solution)/shard_map/pallas_call | solution.py:21
  241.8 0.0 collective-permute-done.6.refs_0_
  241.8 2.6 %shard_map.68 = (bf16[128,32768]{1,0:T(8,128)(2,1)}, f32[128,256]{1,0:T(8,128)S(1)}) custom-call(s32[2]{0:T(128)S(1)} %copy-done.4, bf16[128,256]{1,0:T(8,128)(2,1)S(1)} %get-tuple-element.31.coef, bf16[128,32768]{1,0:T(8,128)(2,1)} %own_ref.21, bf16[128,32768]{1,0:T(8,128)(2,1)} %get-tuple-element.28.applied, ...), custom_call_target="tpu_custom_call", output_to_operand_aliasing={{0}: (5, {})} | custom-call | flops 134217728 | bytes 25624584 | tf_op jit(solution)/shard_map/pallas_call | solution.py:21
  244.4 0.0 collective-permute-done.5.refs_0_
  244.4 2.5 %shard_map.69 = (bf16[128,32768]{1,0:T(8,128)(2,1)}, f32[128,256]{1,0:T(8,128)S(1)}) custom-call(s32[2]{0:T(128)S(1)} %copy-done.4, bf16[128,256]{1,0:T(8,128)(2,1)S(1)} %get-tuple-element.31.coef, bf16[128,32768]{1,0:T(8,128)(2,1)} %own_ref.21, bf16[128,32768]{1,0:T(8,128)(2,1)} %get-tuple-element.28.applied, ...), custom_call_target="tpu_custom_call", output_to_operand_aliasing={{0}: (5, {})} | custom-call | flops 134217728 | bytes 25624584 | tf_op jit(solution)/shard_map/pallas_call | solution.py:21
  247.0 0.0 collective-permute-done.4.refs_0_
  247.0 2.7 %shard_map.70 = (bf16[128,32768]{1,0:T(8,128)(2,1)}, f32[128,256]{1,0:T(8,128)}) custom-call(s32[2]{0:T(128)S(1)} %copy-done.4, bf16[128,256]{1,0:T(8,128)(2,1)S(1)} %get-tuple-element.31.coef, bf16[128,32768]{1,0:T(8,128)(2,1)} %own_ref.21, bf16[128,32768]{1,0:T(8,128)(2,1)} %get-tuple-element.28.applied, ...), custom_call_target="tpu_custom_call", output_to_operand_aliasing={{0}: (5, {})} | custom-call | flops 134217728 | bytes 25624584 | tf_op jit(solution)/shard_map/pallas_call | solution.py:21
  (10 shorter events, 0.0 us)
Async XLA Ops:
  8.6 157.3 %collective-permute-start.1 = (bf16[128,12288]{1,0:T(8,128)(2,1)}, bf16[128,12288]{1,0:T(8,128)(2,1)}, u32[]{:S(2)}, u32[]{:S(2)}) collective-permute-start(bf16[128,12288]{1,0:T(8,128)(2,1)} %shard_map.51), channel_id=1, source_target_pairs={{0,1},{1,0},{2,3},{3,2},{4,5},{5,4},{6,7},{7,6},{8,9},{9,8},{10,11... | collective-permute-start | bytes 9437192 | tf_op jit(solution)/shard_map/ppermute | solution.py:342
  14.9 171.8 %collective-permute-start = (bf16[128,4096]{1,0:T(8,128)(2,1)}, bf16[128,4096]{1,0:T(8,128)(2,1)S(1)}, u32[]{:S(2)}, u32[]{:S(2)}) collective-permute-start(bf16[128,4096]{1,0:T(8,128)(2,1)} %shard_map.50), channel_id=1, source_target_pairs={{0,1},{1,0},{2,3},{3,2},{4,5},{5,4},{6,7},{7,6},{8,9},{9,8},{10,11... | collective-permute-start | bytes 3145736 | tf_op jit(solution)/shard_map/ppermute | solution.py:342
  18.9 213.7 %collective-permute-start.8 = (bf16[128,5120]{1,0:T(8,128)(2,1)}, bf16[128,5120]{1,0:T(8,128)(2,1)S(1)}, u32[]{:S(2)}, u32[]{:S(2)}) collective-permute-start(bf16[128,5120]{1,0:T(8,128)(2,1)} %shard_map.60), channel_id=1, source_target_pairs={{0,1},{1,0},{2,3},{3,2},{4,5},{5,4},{6,7},{7,6},{8,9},{9,8},{10,11... | collective-permute-start | bytes 3932168 | tf_op jit(solution)/shard_map/ppermute | solution.py:342
  24.3 184.3 %collective-permute-start.9 = (bf16[128,4096]{1,0:T(8,128)(2,1)}, bf16[128,4096]{1,0:T(8,128)(2,1)}, u32[]{:S(2)}, u32[]{:S(2)}) collective-permute-start(bf16[128,4096]{1,0:T(8,128)(2,1)} %shard_map.61), channel_id=1, source_target_pairs={{0,1},{1,0},{2,3},{3,2},{4,5},{5,4},{6,7},{7,6},{8,9},{9,8},{10,11... | collective-permute-start | bytes 3145736 | tf_op jit(solution)/shard_map/ppermute | solution.py:342
  25.4 138.8 %collective-permute-start.2 = (bf16[128,2048]{1,0:T(8,128)(2,1)S(1)}, bf16[128,2048]{1,0:T(8,128)(2,1)S(1)}, u32[]{:S(2)}, u32[]{:S(2)}) collective-permute-start(bf16[128,2048]{1,0:T(8,128)(2,1)S(1)} %shard_map.52), channel_id=1, source_target_pairs={{0,1},{1,0},{2,3},{3,2},{4,5},{5,4},{6,7},{7,6},{8,9},{9,8},{10,11... | collective-permute-start | bytes 1572872 | tf_op jit(solution)/shard_map/ppermute | solution.py:342
  29.8 136.0 %copy-start = (f32[32768]{0:T(1024)S(1)}, f32[32768]{0:T(1024)}, u32[]{:S(2)}) copy-start(f32[32768]{0:T(1024)} %param.3) | copy-start | bytes 393220
  29.8 136.0 %copy-start.4 = (s32[2]{0:T(128)S(1)}, s32[2]{0:T(128)}, u32[]{:S(2)}) copy-start(s32[2]{0:T(128)} %pad_add_fusion.at) | copy-start | bytes 28
  164.1 74.4 %collective-permute-start.7 = (bf16[128,2048]{1,0:T(8,128)(2,1)}, bf16[128,2048]{1,0:T(8,128)(2,1)S(1)}, u32[]{:S(2)}, u32[]{:S(2)}) collective-permute-start(bf16[128,2048]{1,0:T(8,128)(2,1)} %shard_map.59), channel_id=1, source_target_pairs={{0,1},{1,0},{2,3},{3,2},{4,5},{5,4},{6,7},{7,6},{8,9},{9,8},{10,11... | collective-permute-start | bytes 1572872 | tf_op jit(solution)/shard_map/ppermute | solution.py:342
  195.0 0.7 copy-start.2
  196.2 7.1 %collective-permute-start.3 = (f32[128,128]{1,0:T(8,128)}, f32[128,128]{1,0:T(8,128)}, u32[]{:S(2)}, u32[]{:S(2)}) collective-permute-start(f32[128,128]{1,0:T(8,128)} %slice.3), channel_id=1, source_target_pairs={{0,1},{1,0},{2,3},{3,2},{4,5},{5,4},{6,7},{7,6},{8,9},{9,8},{10,11... | collective-permute-start | bytes 196616 | tf_op jit(solution)/shard_map/ppermute | solution.py:360
  198.2 43.6 %collective-permute-start.6 = (bf16[128,1024]{1,0:T(8,128)(2,1)}, bf16[128,1024]{1,0:T(8,128)(2,1)}, u32[]{:S(2)}, u32[]{:S(2)}) collective-permute-start(bf16[128,1024]{1,0:T(8,128)(2,1)} %shard_map.58), channel_id=1, source_target_pairs={{0,1},{1,0},{2,3},{3,2},{4,5},{5,4},{6,7},{7,6},{8,9},{9,8},{10,11... | collective-permute-start | bytes 786440 | tf_op jit(solution)/shard_map/ppermute | solution.py:342
  199.9 3.7 %copy-start.1 = (f32[256,128]{1,0:T(8,128)S(1)}, f32[256,128]{1,0:T(8,128)}, u32[]{:S(2)}) copy-start(f32[256,128]{1,0:T(8,128)} %get-tuple-element.27.sums) | copy-start | bytes 393220
  201.7 1.7 copy-start.5
  201.7 2.0 copy-start.3
  203.4 41.0 %collective-permute-start.5 = (bf16[128,1024]{1,0:T(8,128)(2,1)S(1)}, bf16[128,1024]{1,0:T(8,128)(2,1)S(1)}, u32[]{:S(2)}, u32[]{:S(2)}) collective-permute-start(bf16[128,1024]{1,0:T(8,128)(2,1)S(1)} %copy-done.5), channel_id=1, source_target_pairs={{0,1},{1,0},{2,3},{3,2},{4,5},{5,4},{6,7},{7,6},{8,9},{9,8},{10,11... | collective-permute-start | bytes 786440 | tf_op jit(solution)/shard_map/ppermute | solution.py:342
  205.3 3.3 %copy-start.6 = (bf16[128,1024]{1,0:T(8,128)(2,1)S(1)}, bf16[128,1024]{1,0:T(8,128)(2,1)}, u32[]{:S(2)}) copy-start(bf16[128,1024]{1,0:T(8,128)(2,1)} %shard_map.56) | copy-start | bytes 786436
  208.6 38.4 %collective-permute-start.4 = (bf16[128,1024]{1,0:T(8,128)(2,1)S(1)}, bf16[128,1024]{1,0:T(8,128)(2,1)S(1)}, u32[]{:S(2)}, u32[]{:S(2)}) collective-permute-start(bf16[128,1024]{1,0:T(8,128)(2,1)S(1)} %copy-done.6), channel_id=1, source_target_pairs={{0,1},{1,0},{2,3},{3,2},{4,5},{5,4},{6,7},{7,6},{8,9},{9,8},{10,11... | collective-permute-start | bytes 786440 | tf_op jit(solution)/shard_map/ppermute | solution.py:342

commit v2 on v1

--- a/solution.py
+++ b/solution.py
@@ -10,13 +10,15 @@
 
 ROWS = 16
 WHOLE = 2**20
+PARTS = 2
 F32 = jnp.float32
 BF16 = jnp.bfloat16
 ANY = pl.ANY
 
 
-def call(kernel, grid, in_specs, out_specs, out_shape, args, scratch=(), aliases={}, flops=0, limit=58):
-    args = [pltpu.with_memory_space_constraint(a, pltpu.HBM) if a.size >= WHOLE else a for a in args]
+def call(kernel, grid, in_specs, out_specs, out_shape, args, scratch=(), aliases={}, flops=0, limit=58, keep=True):
+    if keep:
+        args = [pltpu.with_memory_space_constraint(a, pltpu.HBM) if a.size >= WHOLE else a for a in args]
     touched = sum(a.size * a.dtype.itemsize for a in args)
     return pl.pallas_call(
         kernel,
@@ -49,22 +51,22 @@
     dst[...] = src[...]
 
 
-def pack(orbitals, start, width, side):
-    own, size = orbitals.shape[0], side * side
+def pack(orbitals, start, width, size):
+    own, count = orbitals.shape[0], orbitals.shape[1] // size
     return call(
         pack_body,
         (width,),
-        [pl.BlockSpec((own, size), lambda i, at: (0, lax.rem(at[0] + i, side)))],
+        [pl.BlockSpec((own, size), lambda i, at: (0, lax.rem(at[0] + i, count)))],
         pl.BlockSpec((own, size), lambda i, at: (0, i)),
         jax.ShapeDtypeStruct((own, width * size), BF16),
         (start, orbitals),
     )
 
 
-def grab_body(width, size, side, at, src, dst, sems):
+def grab_body(width, size, count, at, src, dst, sems):
     copies = []
     for i in range(width):
-        column = pl.multiple_of(lax.rem(at[0] + i, side) * size, size)
+        column = pl.multiple_of(lax.rem(at[0] + i, count) * size, size)
         copies.append(
             pltpu.make_async_copy(src.at[:, pl.ds(column, size)], dst.at[:, pl.ds(i * size, size)], sems.at[i])
         )
@@ -74,10 +76,10 @@
         copy.wait()
 
 
-def grab(orbitals, start, width, side):
-    own, size = orbitals.shape[0], side * side
-    return call(
-        functools.partial(grab_body, width, size, side),
+def grab(orbitals, start, width, size):
+    own, count = orbitals.shape[0], orbitals.shape[1] // size
+    return call(
+        functools.partial(grab_body, width, size, count),
         (1,),
         [pl.BlockSpec(memory_space=ANY)],
         pl.BlockSpec(memory_space=pltpu.VMEM),
@@ -274,12 +276,12 @@
             gram[...] = pltpu.roll(gram[...], at[1] * own, 1)
 
 
-def rest(at, coef, orbitals, applied, rems, carry, q0, width, last, side):
-    own, grid, size, n = orbitals.shape[0], orbitals.shape[1], side * side, len(rems) + 1
-    total = n * own
+def rest(at, coef, orbitals, applied, rems, carry, q0, width, last, size, ratio):
+    own, grid, n = orbitals.shape[0], orbitals.shape[1], len(rems) + 1
+    total, count = n * own, grid // size
 
     def plane():
-        return pl.BlockSpec((own, size), lambda i, at: (0, lax.rem(at[0] + q0 + i - 1 + side, side)))
+        return pl.BlockSpec((own, size), lambda i, at: (0, lax.rem((at[0] - 1) * ratio + q0 + i + count, count)))
 
     def fixed(shape):
         return pl.BlockSpec(shape, lambda i, at: (0, 0))
@@ -303,6 +305,7 @@
         scratch=[pltpu.VMEM((total, size), BF16)],
         aliases=aliases,
         flops=4 * own * total * size * width,
+        keep=False,
         limit=16,
     )
 
@@ -320,10 +323,10 @@
     short = max(2, share // 4)
     widths = [2] + ([share - short, short] if share >= 4 else [share])
     widths.append((side - share - 2) // 3)
-    after = cuts(side - sum(widths))
-    starts = [sum((widths + after)[:c]) for c in range(len(widths + after))]
-    both = list(zip(starts, widths + after))
-    return both[: len(widths)], both[len(widths) :]
+    after = cuts(PARTS * (side - sum(widths)))
+    early = [(sum(widths[:c]), w, 1) for c, w in enumerate(widths)]
+    late = [(PARTS * sum(widths) + sum(after[:c]), w, PARTS) for c, w in enumerate(after)]
+    return early, late
 
 
 def shards(n, orbitals, potential):
@@ -333,24 +336,24 @@
     me = lax.axis_index("band")
     potential = potential.reshape(1, grid)
 
-    def sent(c, q0, width):
-        got = []
+    def sent(c, q0, width, ratio):
+        got, count = [], side * ratio
         for j in range(1, n):
             dest = lax.rem(me + n - j, n)
-            start = lax.rem(dest * share + q0 - 1 + side, side).astype(jnp.int32).reshape(1)
-            chunk = (pack if c else grab)(orbitals, start, width, side)
+            start = lax.rem((dest * share - 1) * ratio + q0 + count, count).astype(jnp.int32).reshape(1)
+            chunk = (pack if c else grab)(orbitals, start, width, grid // count)
             got.append(lax.ppermute(chunk, "band", [(k, (k - j) % n) for k in range(n)]))
         return got
 
     early, late = plan(n, side)
     at = jnp.stack([me * share, me]).astype(jnp.int32)
-    chunks = [(q0, w, sent(c, q0, w)) for c, (q0, w) in enumerate(early)]
+    chunks = [(*block, sent(c, *block)) for c, block in enumerate(early)]
     applied, sums = apply_own(orbitals, potential, at, side)
     before = None
     for c in range(1, len(early) - 1):
-        q0, w, rems = chunks[c]
+        q0, w, _, rems = chunks[c]
         before = part(
-            orbitals, applied, potential, at, rems, chunks[c - 1][2],
+            orbitals, applied, potential, at, rems, chunks[c - 1][3],
             None if before is None else before[0], q0, w, c == len(early) - 2, side,
         )
     mine, others = before[0], before[1:]
@@ -358,11 +361,12 @@
     for j in range(1, n):
         perm = [(k, (k - j) % n) for k in range(n)]
         got.append(lax.ppermute(others[j - 1][:, own:], "band", perm))
-    chunks += [(q0, w, sent(len(early) + c, q0, w)) for c, (q0, w) in enumerate(late)]
+    chunks += [(*block, sent(len(early) + c, *block)) for c, block in enumerate(late)]
     projected, coef = coefficients(at[1:], sums, mine, got)
     carry = None
-    for c, (q0, w, rems) in enumerate(chunks):
-        carry = rest(at, coef, orbitals, applied, rems, carry, q0, w, c == len(chunks) - 1, side)
+    for c, (q0, w, ratio, rems) in enumerate(chunks):
+        last = c == len(chunks) - 1
+        carry = rest(at, coef, orbitals, applied, rems, carry, q0, w, last, grid // (side * ratio), ratio)
     residuals, margin = carry
     return margin, projected, residuals
 

time: 251 us -> 289 us (1.15)
  waiting for transfers between devices: 83 us -> 108 us
  local copies, waits for them, and re-layouts: 1.29 us -> 8.42 us
  Pallas kernels: 151 us -> 157 us
    ppermute x9 -> x10, waiting for transfers between devices: 83 us -> 108 us  [sent(): lax.ppermute(chunk, 'band', [(k, (k - j) % n) for k in range(n)])]
    unnamed x14 -> x20, local copies, waits for them, and re-layouts: 0.67 us -> 8.41 us
    pallas_call x22 -> x24, Pallas kernels: 151 us -> 157 us  [call(): pl.pallas_call(kernel, out_shape=out_shape, grid_spec=pltpu.PrefetchScala...]
    ppermute x9 -> x10, starting transfers between devices: 12.7 us -> 13.2 us  [sent(): lax.ppermute(chunk, 'band', [(k, (k - j) % n) for k in range(n)])]
  transfers between devices with their start and end apart: 10 -> 11, of which waited for: 1 -> 1; matrix products, arithmetic and copies ran while one was open for 0% -> 0% of each run, Pallas kernels for 56% -> 51%
where the time goes in v2:
time: 289 us; the launch traced here: 287 us
  Pallas kernels  157 us (54%)
  waiting for transfers between devices  108 us (37%)
  starting transfers between devices  13.2 us (5%)
  local copies, waits for them, and re-layouts  8.42 us (3%)
    pallas_call x24, Pallas kernels, call(): pl.pallas_call(kernel, out_shape=out_shape, grid_spec=pltpu.PrefetchScala...  157 us
    ppermute x10, waiting for transfers between devices, sent(): lax.ppermute(chunk, 'band', [(k, (k - j) % n) for k in range(n)])  108 us
    ppermute x10, starting transfers between devices, sent(): lax.ppermute(chunk, 'band', [(k, (k - j) % n) for k in range(n)])  13.2 us
    unnamed x20, local copies, waits for them, and re-layouts  8.41 us
  transfers between devices with their start and end apart: 11, of which 1 were waited for; matrix products, arithmetic and copies ran while one was open for 0% of the time, Pallas kernels for 51%

profile of v2, /device:TPU:0, one launch (start us, length us, event | category | flops | bytes accessed | tf_op | source)
XLA Modules:
  0.0 287.3 jit_solution(13988851189799200105)
XLA Ops:
  0.6 8.0 %shard_map.51 = bf16[128,12288]{1,0:T(8,128)(2,1)} custom-call(s32[1]{0:T(128)} %bitcast.4.at, bf16[128,32768]{1,0:T(8,128)(2,1)} %own_ref.23), custom_call_target="tpu_custom_call" | custom-call | bytes 8388612 | tf_op jit(solution)/shard_map/pallas_call | solution.py:23
  8.7 3.0 %collective-permute-start.1 = (bf16[128,12288]{1,0:T(8,128)(2,1)}, bf16[128,12288]{1,0:T(8,128)(2,1)S(1)}, u32[]{:S(2)}, u32[]{:S(2)}) collective-permute-start(bf16[128,12288]{1,0:T(8,128)(2,1)} %shard_map.51), channel_id=1, source_target_pairs={{0,1},{1,0},{2,3},{3,2},{4,5},{5,4},{6,7},{7,6},{8,9},{9,8},{10,11... | collective-permute-start | bytes 9437192 | tf_op jit(solution)/shard_map/ppermute | solution.py:345
  11.6 3.4 %shard_map.50 = bf16[128,4096]{1,0:T(8,128)(2,1)} custom-call(s32[1]{0:T(128)} %bitcast.3.at, bf16[128,32768]{1,0:T(8,128)(2,1)} %own_ref.23), custom_call_target="tpu_custom_call" | custom-call | bytes 8388612 | tf_op jit(solution)/shard_map/pallas_call | solution.py:23
  15.0 0.0 collective-permute-start
  15.0 6.4 %shard_map.61 = bf16[128,5120]{1,0:T(8,128)(2,1)} custom-call(s32[1]{0:T(128)} %bitcast.11.at, bf16[128,32768]{1,0:T(8,128)(2,1)} %own_ref.23), custom_call_target="tpu_custom_call" | custom-call | bytes 8388612 | tf_op jit(solution)/shard_map/pallas_call | solution.py:23
  21.4 2.0 collective-permute-start.9
  23.4 1.8 shard_map.52
  25.3 0.1 collective-permute-start.2
  25.4 3.4 %shard_map.62 = bf16[128,4096]{1,0:T(8,128)(2,1)} custom-call(s32[1]{0:T(128)} %bitcast.12.at, bf16[128,32768]{1,0:T(8,128)(2,1)} %own_ref.23), custom_call_target="tpu_custom_call" | custom-call | bytes 8388612 | tf_op jit(solution)/shard_map/pallas_call | solution.py:23
  28.7 2.0 collective-permute-start.10
  30.7 3.6 %shard_map.60 = bf16[128,2560]{1,0:T(8,128)(2,1)} custom-call(s32[1]{0:T(128)} %bitcast.10.at, bf16[128,32768]{1,0:T(8,128)(2,1)} %own_ref.23), custom_call_target="tpu_custom_call" | custom-call | bytes 8388612 | tf_op jit(solution)/shard_map/pallas_call | solution.py:23
  34.4 0.6 pad_add_fusion.at
  34.9 107.7 %collective-permute-done.2.refs_1_.refs_2_.refs_0_ = bf16[128,2048]{1,0:T(8,128)(2,1)} collective-permute-done((bf16[128,2048]{1,0:T(8,128)(2,1)}, bf16[128,2048]{1,0:T(8,128)(2,1)}, u32[]{:S(2)}, u32[]{:S(2)}) %collective-permute-start.2) | collective-permute-done | bytes 524320 | tf_op jit(solution)/shard_map/ppermute | solution.py:345
  142.7 2.0 collective-permute-start.8
  144.7 51.3 %shard_map.49 = (bf16[128,32768]{1,0:T(8,128)(2,1)}, f32[256,128]{1,0:T(8,128)}) custom-call(s32[2]{0:T(128)} %pad_add_fusion.at, bf16[128,32768]{1,0:T(8,128)(2,1)} %own_ref.23, bf16[128,32768]{1,0:T(8,128)(2,1)} %own_ref.23, bf16[128,32768]{1,0:T(8,128)(2,1)} %own_ref.23, f32[1,32768]{1,0:T(1,128)} %bitcast.13), custom_call_target="tpu_custom_call" | custom-call | flops 2147483648 | bytes 25296904 | tf_op jit(solution)/shard_map/pallas_call | solution.py:23
  196.0 0.0 collective-permute-done.1.refs_0_.refs_1_.refs_2_
  196.0 1.6 copy-done.2
  197.7 20.9 %shard_map.53.refs_3_ = f32[256,256]{1,0:T(8,128)S(1)} custom-call(s32[2]{0:T(128)S(1)} %copy-done.6, bf16[128,32768]{1,0:T(8,128)(2,1)} %own_ref.23, bf16[128,32768]{1,0:T(8,128)(2,1)} %get-tuple-element.30.applied, f32[1,32768]{1,0:T(1,128)S(1)} %bitcast.14, bf16[128,12288]{1,0:T(8,128)(2,1)} %copy-done.2, ...), custom_call_target="tpu_custom_call" | custom-call | flops 1610612736 | bytes 21102600 | tf_op jit(solution)/shard_map/pallas_call | solution.py:23
  218.6 0.0 collective-permute-done.refs_0_
  218.6 8.3 %shard_map.54 = (f32[128,256]{1,0:T(8,128)S(1)}, f32[128,256]{1,0:T(8,128)S(1)}) custom-call(s32[2]{0:T(128)S(1)} %copy-done.6, bf16[128,32768]{1,0:T(8,128)(2,1)} %own_ref.23, bf16[128,32768]{1,0:T(8,128)(2,1)} %get-tuple-element.30.applied, f32[1,32768]{1,0:T(1,128)S(1)} %bitcast.15, bf16[128,4096]{1,0:T(8,128)(2,1)} %collective-permute-done.refs_0_, ...), custom_call_target="tpu_custom_call" | custom-call | flops 536870912 | bytes 24510472 | tf_op jit(solution)/shard_map/pallas_call | solution.py:23
  226.9 0.1 collective-permute-start.3
  227.0 1.7 shard_map.59
  228.6 2.0 collective-permute-start.7
  230.6 1.6 shard_map.58
  232.2 1.6 shard_map.57
  233.8 1.6 shard_map.56
  235.4 0.0 collective-permute-done.3.refs_0_
  235.4 0.0 collective-permute-start.6
  235.4 0.8 shard_map.55
  236.2 3.4 %copy-done = bf16[128,32768]{1,0:T(8,128)(2,1)S(1)} copy-done((bf16[128,32768]{1,0:T(8,128)(2,1)S(1)}, bf16[128,32768]{1,0:T(8,128)(2,1)}, u32[]{:S(2)}) %copy-start) | copy-done | bytes 8388632
  239.6 3.4 %copy-done.1 = bf16[128,32768]{1,0:T(8,128)(2,1)S(1)} copy-done((bf16[128,32768]{1,0:T(8,128)(2,1)S(1)}, bf16[128,32768]{1,0:T(8,128)(2,1)}, u32[]{:S(2)}) %copy-start.1) | copy-done | bytes 8388632
  243.0 3.5 %shard_map.63 = (bf16[128,32768]{1,0:T(8,128)(2,1)}, f32[128,256]{1,0:T(8,128)S(1)}) custom-call(s32[2]{0:T(128)S(1)} %copy-done.6, bf16[128,256]{1,0:T(8,128)(2,1)S(1)} %get-tuple-element.33.coef, bf16[128,32768]{1,0:T(8,128)(2,1)S(1)} %copy-done, bf16[128,32768]{1,0:T(8,128)(2,1)S(1)} %copy-done.1, ...), custom_call_target="tpu_custom_call" | custom-call | flops 268435456 | bytes 17367048 | tf_op jit(solution)/shard_map/pallas_call | solution.py:23
  246.5 8.9 %shard_map.64 = (bf16[128,32768]{1,0:T(8,128)(2,1)}, f32[128,256]{1,0:T(8,128)S(1)}) custom-call(s32[2]{0:T(128)S(1)} %copy-done.6, bf16[128,256]{1,0:T(8,128)(2,1)S(1)} %get-tuple-element.33.coef, bf16[128,32768]{1,0:T(8,128)(2,1)S(1)} %copy-done, bf16[128,32768]{1,0:T(8,128)(2,1)S(1)} %copy-done.1, ...), custom_call_target="tpu_custom_call", output_to_operand_aliasing={{0}: (5, {})} | custom-call | flops 1610612736 | bytes 28508168 | tf_op jit(solution)/shard_map/pallas_call | solution.py:23
  255.5 4.9 %shard_map.65 = (bf16[128,32768]{1,0:T(8,128)(2,1)}, f32[128,256]{1,0:T(8,128)S(1)}) custom-call(s32[2]{0:T(128)S(1)} %copy-done.6, bf16[128,256]{1,0:T(8,128)(2,1)S(1)} %get-tuple-element.33.coef, bf16[128,32768]{1,0:T(8,128)(2,1)S(1)} %copy-done, bf16[128,32768]{1,0:T(8,128)(2,1)S(1)} %copy-done.1, ...), custom_call_target="tpu_custom_call", output_to_operand_aliasing={{0}: (5, {})} | custom-call | flops 536870912 | bytes 26411016 | tf_op jit(solution)/shard_map/pallas_call | solution.py:23
  260.4 0.0 collective-permute-done.10.refs_0_
  260.4 2.0 collective-permute-start.5
  262.3 0.0 collective-permute-done.9.refs_0_
  262.4 0.1 collective-permute-start.4
  262.4 4.9 %shard_map.66 = (bf16[128,32768]{1,0:T(8,128)(2,1)}, f32[128,256]{1,0:T(8,128)S(1)}) custom-call(s32[2]{0:T(128)S(1)} %copy-done.6, bf16[128,256]{1,0:T(8,128)(2,1)S(1)} %get-tuple-element.33.coef, bf16[128,32768]{1,0:T(8,128)(2,1)S(1)} %copy-done, bf16[128,32768]{1,0:T(8,128)(2,1)S(1)} %copy-done.1, ...), custom_call_target="tpu_custom_call", output_to_operand_aliasing={{0}: (5, {})} | custom-call | flops 536870912 | bytes 26411016 | tf_op jit(solution)/shard_map/pallas_call | solution.py:23
  267.3 8.5 %shard_map.67 = (bf16[128,32768]{1,0:T(8,128)(2,1)}, f32[128,256]{1,0:T(8,128)S(1)}) custom-call(s32[2]{0:T(128)S(1)} %copy-done.6, bf16[128,256]{1,0:T(8,128)(2,1)S(1)} %get-tuple-element.33.coef, bf16[128,32768]{1,0:T(8,128)(2,1)S(1)} %copy-done, bf16[128,32768]{1,0:T(8,128)(2,1)S(1)} %copy-done.1, ...), custom_call_target="tpu_custom_call", output_to_operand_aliasing={{0}: (5, {})} | custom-call | flops 671088640 | bytes 26673160 | tf_op jit(solution)/shard_map/pallas_call | solution.py:23
  275.8 0.0 collective-permute-done.8.refs_0_
  275.8 5.2 %shard_map.68 = (bf16[128,32768]{1,0:T(8,128)(2,1)}, f32[128,256]{1,0:T(8,128)S(1)}) custom-call(s32[2]{0:T(128)S(1)} %copy-done.6, bf16[128,256]{1,0:T(8,128)(2,1)S(1)} %get-tuple-element.33.coef, bf16[128,32768]{1,0:T(8,128)(2,1)S(1)} %copy-done, bf16[128,32768]{1,0:T(8,128)(2,1)S(1)} %copy-done.1, ...), custom_call_target="tpu_custom_call", output_to_operand_aliasing={{0}: (5, {})} | custom-call | flops 335544320 | bytes 26017800 | tf_op jit(solution)/shard_map/pallas_call | solution.py:23
  281.0 2.0 shard_map.69
  283.0 1.4 shard_map.70
  284.4 0.0 collective-permute-done.5.refs_0_
  284.4 1.4 shard_map.71
  285.8 0.0 collective-permute-done.4.refs_0_
  285.8 1.6 shard_map.72
  (20 shorter events, 0.0 us)
Async XLA Ops:
  8.7 187.4 %collective-permute-start.1 = (bf16[128,12288]{1,0:T(8,128)(2,1)}, bf16[128,12288]{1,0:T(8,128)(2,1)S(1)}, u32[]{:S(2)}, u32[]{:S(2)}) collective-permute-start(bf16[128,12288]{1,0:T(8,128)(2,1)} %shard_map.51), channel_id=1, source_target_pairs={{0,1},{1,0},{2,3},{3,2},{4,5},{5,4},{6,7},{7,6},{8,9},{9,8},{10,11... | collective-permute-start | bytes 9437192 | tf_op jit(solution)/shard_map/ppermute | solution.py:345
  15.0 203.6 %collective-permute-start = (bf16[128,4096]{1,0:T(8,128)(2,1)}, bf16[128,4096]{1,0:T(8,128)(2,1)}, u32[]{:S(2)}, u32[]{:S(2)}) collective-permute-start(bf16[128,4096]{1,0:T(8,128)(2,1)} %shard_map.50), channel_id=1, source_target_pairs={{0,1},{1,0},{2,3},{3,2},{4,5},{5,4},{6,7},{7,6},{8,9},{9,8},{10,11... | collective-permute-start | bytes 3145736 | tf_op jit(solution)/shard_map/ppermute | solution.py:345
  21.4 240.9 %collective-permute-start.9 = (bf16[128,5120]{1,0:T(8,128)(2,1)}, bf16[128,5120]{1,0:T(8,128)(2,1)}, u32[]{:S(2)}, u32[]{:S(2)}) collective-permute-start(bf16[128,5120]{1,0:T(8,128)(2,1)} %shard_map.61), channel_id=1, source_target_pairs={{0,1},{1,0},{2,3},{3,2},{4,5},{5,4},{6,7},{7,6},{8,9},{9,8},{10,11... | collective-permute-start | bytes 3932168 | tf_op jit(solution)/shard_map/ppermute | solution.py:345
  25.3 117.4 %collective-permute-start.2 = (bf16[128,2048]{1,0:T(8,128)(2,1)}, bf16[128,2048]{1,0:T(8,128)(2,1)}, u32[]{:S(2)}, u32[]{:S(2)}) collective-permute-start(bf16[128,2048]{1,0:T(8,128)(2,1)} %shard_map.52), channel_id=1, source_target_pairs={{0,1},{1,0},{2,3},{3,2},{4,5},{5,4},{6,7},{7,6},{8,9},{9,8},{10,11... | collective-permute-start | bytes 1572872 | tf_op jit(solution)/shard_map/ppermute | solution.py:345
  28.7 231.6 %collective-permute-start.10 = (bf16[128,4096]{1,0:T(8,128)(2,1)}, bf16[128,4096]{1,0:T(8,128)(2,1)}, u32[]{:S(2)}, u32[]{:S(2)}) collective-permute-start(bf16[128,4096]{1,0:T(8,128)(2,1)} %shard_map.62), channel_id=1, source_target_pairs={{0,1},{1,0},{2,3},{3,2},{4,5},{5,4},{6,7},{7,6},{8,9},{9,8},{10,11... | collective-permute-start | bytes 3145736 | tf_op jit(solution)/shard_map/ppermute | solution.py:345
  142.7 133.1 %collective-permute-start.8 = (bf16[128,2560]{1,0:T(8,128)(2,1)}, bf16[128,2560]{1,0:T(8,128)(2,1)}, u32[]{:S(2)}, u32[]{:S(2)}) collective-permute-start(bf16[128,2560]{1,0:T(8,128)(2,1)} %shard_map.60), channel_id=1, source_target_pairs={{0,1},{1,0},{2,3},{3,2},{4,5},{5,4},{6,7},{7,6},{8,9},{9,8},{10,11... | collective-permute-start | bytes 1966088 | tf_op jit(solution)/shard_map/ppermute | solution.py:345
  144.7 53.0 %copy-start.4 = (f32[32768]{0:T(1024)S(1)}, f32[32768]{0:T(1024)}, u32[]{:S(2)}) copy-start(f32[32768]{0:T(1024)} %param.3) | copy-start | bytes 393220
  144.7 53.0 %copy-start.6 = (s32[2]{0:T(128)S(1)}, s32[2]{0:T(128)}, u32[]{:S(2)}) copy-start(s32[2]{0:T(128)} %pad_add_fusion.at) | copy-start | bytes 28
  196.0 1.6 copy-start.2
  226.9 8.5 %collective-permute-start.3 = (f32[128,128]{1,0:T(8,128)S(1)}, f32[128,128]{1,0:T(8,128)S(1)}, u32[]{:S(2)}, u32[]{:S(2)}) collective-permute-start(f32[128,128]{1,0:T(8,128)S(1)} %slice.3), channel_id=1, source_target_pairs={{0,1},{1,0},{2,3},{3,2},{4,5},{5,4},{6,7},{7,6},{8,9},{9,8},{10,11... | collective-permute-start | bytes 196616 | tf_op jit(solution)/shard_map/ppermute | solution.py:363
  228.6 52.3 %collective-permute-start.7 = (bf16[128,1024]{1,0:T(8,128)(2,1)}, bf16[128,1024]{1,0:T(8,128)(2,1)S(1)}, u32[]{:S(2)}, u32[]{:S(2)}) collective-permute-start(bf16[128,1024]{1,0:T(8,128)(2,1)} %shard_map.59), channel_id=1, source_target_pairs={{0,1},{1,0},{2,3},{3,2},{4,5},{5,4},{6,7},{7,6},{8,9},{9,8},{10,11... | collective-permute-start | bytes 786440 | tf_op jit(solution)/shard_map/ppermute | solution.py:345
  232.2 3.2 %copy-start.7 = (bf16[128,512]{1,0:T(8,128)(2,1)S(1)}, bf16[128,512]{1,0:T(8,128)(2,1)}, u32[]{:S(2)}) copy-start(bf16[128,512]{1,0:T(8,128)(2,1)} %shard_map.58) | copy-start | bytes 393220
  232.2 3.2 %copy-start.5 = (f32[256,128]{1,0:T(8,128)S(1)}, f32[256,128]{1,0:T(8,128)}, u32[]{:S(2)}) copy-start(f32[256,128]{1,0:T(8,128)} %get-tuple-element.29.sums) | copy-start | bytes 393220
  235.4 47.6 %collective-permute-start.6 = (bf16[128,512]{1,0:T(8,128)(2,1)S(1)}, bf16[128,512]{1,0:T(8,128)(2,1)S(1)}, u32[]{:S(2)}, u32[]{:S(2)}) collective-permute-start(bf16[128,512]{1,0:T(8,128)(2,1)S(1)} %copy-done.7), channel_id=1, source_target_pairs={{0,1},{1,0},{2,3},{3,2},{4,5},{5,4},{6,7},{7,6},{8,9},{9,8},{10,11... | collective-permute-start | bytes 393224 | tf_op jit(solution)/shard_map/ppermute | solution.py:345
  236.2 3.4 %copy-start = (bf16[128,32768]{1,0:T(8,128)(2,1)S(1)}, bf16[128,32768]{1,0:T(8,128)(2,1)}, u32[]{:S(2)}) copy-start(bf16[128,32768]{1,0:T(8,128)(2,1)} %own_ref.23) | copy-start | bytes 25165828
  239.6 3.4 %copy-start.1 = (bf16[128,32768]{1,0:T(8,128)(2,1)S(1)}, bf16[128,32768]{1,0:T(8,128)(2,1)}, u32[]{:S(2)}) copy-start(bf16[128,32768]{1,0:T(8,128)(2,1)} %get-tuple-element.30.applied) | copy-start | bytes 25165828
  243.0 3.6 %copy-start.3 = (bf16[128,12288]{1,0:T(8,128)(2,1)S(1)}, bf16[128,12288]{1,0:T(8,128)(2,1)}, u32[]{:S(2)}) copy-start(bf16[128,12288]{1,0:T(8,128)(2,1)} %copy-done.2) | copy-start | bytes 9437188
  255.5 4.9 %copy-start.8 = (bf16[128,512]{1,0:T(8,128)(2,1)S(1)}, bf16[128,512]{1,0:T(8,128)(2,1)}, u32[]{:S(2)}) copy-start(bf16[128,512]{1,0:T(8,128)(2,1)} %shard_map.57) | copy-start | bytes 393220
  255.5 6.9 %copy-start.9 = (bf16[128,512]{1,0:T(8,128)(2,1)S(1)}, bf16[128,512]{1,0:T(8,128)(2,1)}, u32[]{:S(2)}) copy-start(bf16[128,512]{1,0:T(8,128)(2,1)} %shard_map.56) | copy-start | bytes 393220
  260.4 24.0 %collective-permute-start.5 = (bf16[128,512]{1,0:T(8,128)(2,1)S(1)}, bf16[128,512]{1,0:T(8,128)(2,1)S(1)}, u32[]{:S(2)}, u32[]{:S(2)}) collective-permute-start(bf16[128,512]{1,0:T(8,128)(2,1)S(1)} %copy-done.8), channel_id=1, source_target_pairs={{0,1},{1,0},{2,3},{3,2},{4,5},{5,4},{6,7},{7,6},{8,9},{9,8},{10,11... | collective-permute-start | bytes 393224 | tf_op jit(solution)/shard_map/ppermute | solution.py:345
  262.4 23.4 %collective-permute-start.4 = (bf16[128,512]{1,0:T(8,128)(2,1)S(1)}, bf16[128,512]{1,0:T(8,128)(2,1)S(1)}, u32[]{:S(2)}, u32[]{:S(2)}) collective-permute-start(bf16[128,512]{1,0:T(8,128)(2,1)S(1)} %copy-done.9), channel_id=1, source_target_pairs={{0,1},{1,0},{2,3},{3,2},{4,5},{5,4},{6,7},{7,6},{8,9},{9,8},{10,11... | collective-permute-start | bytes 393224 | tf_op jit(solution)/shard_map/ppermute | solution.py:345

commit v3 on v2

--- a/solution.py
+++ b/solution.py
@@ -16,9 +16,8 @@
 ANY = pl.ANY
 
 
-def call(kernel, grid, in_specs, out_specs, out_shape, args, scratch=(), aliases={}, flops=0, limit=58, keep=True):
-    if keep:
-        args = [pltpu.with_memory_space_constraint(a, pltpu.HBM) if a.size >= WHOLE else a for a in args]
+def call(kernel, grid, in_specs, out_specs, out_shape, args, scratch=(), aliases={}, flops=0, limit=16):
+    args = [pltpu.with_memory_space_constraint(a, pltpu.HBM) if a.size >= WHOLE else a for a in args]
     touched = sum(a.size * a.dtype.itemsize for a in args)
     return pl.pallas_call(
         kernel,
@@ -126,6 +125,7 @@
         (token, orbitals, orbitals, orbitals, potential),
         scratch=[pltpu.VMEM((2 * own, size), BF16)],
         flops=4 * own * own * grid,
+        limit=56,
     )
 
 
@@ -210,7 +210,6 @@
             pltpu.VMEM((total, total), F32),
         ],
         flops=2 * total * total * size * width,
-        limit=32,
     )
 
 
@@ -246,37 +245,30 @@
         [shape, jax.ShapeDtypeStruct((own, total), BF16)],
         (at, sums, mine, *got),
         scratch=[pltpu.VMEM((own, total), F32)],
-        limit=16,
-    )
-
-
-def rest_body(n, first, last, at, coef, own_ref, applied, *refs):
+    )
+
+
+def rest_body(n, first, at, coef, own_ref, applied, *refs):
     refs = list(refs)
     rems, refs = refs[: n - 1], refs[n - 1 :]
     if not first:
         before, refs = refs[1], refs[2:]
     out, gram, every = refs
     own = own_ref.shape[0]
-    i = pl.program_id(0)
     every[:own, :] = own_ref[...]
     for j in range(n - 1):
         every[(j + 1) * own : (j + 2) * own, :] = rems[j][...]
     mixed = jnp.dot(coef[...], every[...], preferred_element_type=F32)
     out[...] = (applied[...].astype(F32) - mixed).astype(BF16)
 
-    @pl.when(i == 0)
+    @pl.when(pl.program_id(0) == 0)
     def _():
         gram[...] = jnp.zeros_like(gram) if first else before[...]
 
-    gram[...] += rowdot(own_ref[...], every[...])
-    if last:
-
-        @pl.when(i == pl.num_programs(0) - 1)
-        def _():
-            gram[...] = pltpu.roll(gram[...], at[1] * own, 1)
-
-
-def rest(at, coef, orbitals, applied, rems, carry, q0, width, last, size, ratio):
+    gram[...] += rowdot(own_ref[...], every[own:, :])
+
+
+def rest(at, coef, orbitals, applied, rems, carry, q0, width, size, ratio):
     own, grid, n = orbitals.shape[0], orbitals.shape[1], len(rems) + 1
     total, count = n * own, grid // size
 
@@ -294,19 +286,83 @@
     if not first:
         aliases = {len(args): 0}
         args += list(carry)
-        specs += [pl.BlockSpec(memory_space=ANY), fixed((own, total))]
-    return call(
-        functools.partial(rest_body, n, first, last),
+        specs += [pl.BlockSpec(memory_space=ANY), fixed((own, total - own))]
+    return call(
+        functools.partial(rest_body, n, first),
         (width,),
         specs,
-        [plane(), fixed((own, total))],
-        [jax.ShapeDtypeStruct((own, grid), BF16), jax.ShapeDtypeStruct((own, total), F32)],
+        [plane(), fixed((own, total - own))],
+        [jax.ShapeDtypeStruct((own, grid), BF16), jax.ShapeDtypeStruct((own, total - own), F32)],
         tuple(args),
         scratch=[pltpu.VMEM((total, size), BF16)],
         aliases=aliases,
         flops=4 * own * total * size * width,
-        keep=False,
-        limit=16,
+    )
+
+
+def ready_body(at, coef, own_ref, applied, base, copied):
+    own = own_ref.shape[0]
+    copied[...] = own_ref[...]
+    base[...] = applied[...].astype(F32) - jnp.dot(coef[:, :own], own_ref[...], preferred_element_type=F32)
+
+
+def ready(at, coef, orbitals, applied, q0, size, ratio):
+    own, grid = orbitals.shape
+    count = grid // size
+    plane = pl.BlockSpec((own, size), lambda i, at: (0, lax.rem((at[0] - 1) * ratio + q0 + count, count)))
+    return call(
+        ready_body,
+        (1,),
+        [pl.BlockSpec(coef.shape, lambda i, at: (0, 0)), plane, plane],
+        [pl.BlockSpec(memory_space=pltpu.VMEM)] * 2,
+        [pltpu.VMEM((own, size), F32), pltpu.VMEM((own, size), BF16)],
+        (at, coef, orbitals, applied),
+    )
+
+
+def finish_body(n, size, count, q0, ratio, at, coef, base, copied, sums, gram, *refs):
+    rems, (_, out, margin, rows, block, others, sems) = refs[: n - 1], refs[n - 1 :]
+    own = copied.shape[0]
+    if n == 2:
+        other = rems[0][...]
+    else:
+        for j in range(n - 1):
+            others[j * own : (j + 1) * own, :] = rems[j][...]
+        other = others[...]
+    rows[:, :own] = sums[own:, :]
+    rows[:, own:] = gram[...] + rowdot(copied[...], other)
+    rows[...] = pltpu.roll(rows[...], at[1] * own, 1)
+    first = pltpu.make_async_copy(rows, margin, sems.at[0])
+    first.start()
+    mixed = jnp.dot(coef[:, own:], other, preferred_element_type=F32)
+    block[...] = (base[...] - mixed).astype(BF16)
+    column = pl.multiple_of(lax.rem((at[0] - 1) * ratio + q0 + count, count) * size, size)
+    second = pltpu.make_async_copy(block, out.at[:, pl.ds(column, size)], sems.at[1])
+    second.start()
+    first.wait()
+    second.wait()
+
+
+def finish(at, coef, base, copied, sums, rems, carry, q0, size, ratio):
+    out, gram = carry
+    own, grid = out.shape
+    n = len(rems) + 1
+    vmem, free = pl.BlockSpec(memory_space=pltpu.VMEM), pl.BlockSpec(memory_space=ANY)
+    held = [pltpu.with_memory_space_constraint(a, pltpu.VMEM) for a in (coef, base, copied, sums, gram, *rems)]
+    return call(
+        functools.partial(finish_body, n, size, grid // size, q0, ratio),
+        (1,),
+        [vmem] * len(held) + [free],
+        [free, free],
+        [jax.ShapeDtypeStruct(out.shape, BF16), jax.ShapeDtypeStruct((own, n * own), F32)],
+        (at, *held, out),
+        scratch=[
+            pltpu.VMEM((own, n * own), F32),
+            pltpu.VMEM((own, size), BF16),
+            pltpu.VMEM(((n - 1) * own, size), BF16),
+            pltpu.SemaphoreType.DMA((2,)),
+        ],
+        aliases={len(held) + 1: 0},
     )
 
 
@@ -364,9 +420,12 @@
     chunks += [(*block, sent(len(early) + c, *block)) for c, block in enumerate(late)]
     projected, coef = coefficients(at[1:], sums, mine, got)
     carry = None
-    for c, (q0, w, ratio, rems) in enumerate(chunks):
-        last = c == len(chunks) - 1
-        carry = rest(at, coef, orbitals, applied, rems, carry, q0, w, last, grid // (side * ratio), ratio)
+    q0, _, ratio, rems = chunks.pop()
+    size = grid // (side * ratio)
+    base, copied = ready(at, coef, orbitals, applied, q0, size, ratio)
+    for first, width, parts, block in chunks:
+        carry = rest(at, coef, orbitals, applied, block, carry, first, width, grid // (side * parts), parts)
+    carry = finish(at, coef, base, copied, sums, rems, carry, q0, size, ratio)
     residuals, margin = carry
     return margin, projected, residuals
 

time: 289 us -> 288 us (level)
  local copies, waits for them, and re-layouts: 8.42 us -> 2.6 us
  Pallas kernels: 157 us -> 161 us
    unnamed x20 -> x18, local copies, waits for them, and re-layouts: 8.41 us -> 1.99 us
    pallas_call x24 -> x25, Pallas kernels: 157 us -> 161 us  [call(): pl.pallas_call(kernel, out_shape=out_shape, grid_spec=pltpu.PrefetchScala...]
  transfers between devices with their start and end apart: 11 -> 11, of which waited for: 1 -> 1; matrix products, arithmetic and copies ran while one was open for 0% -> 0% of each run, Pallas kernels for 51% -> 53%
where the time goes in v3:
time: 288 us; the launch traced here: 287 us
  Pallas kernels  161 us (56%)
  waiting for transfers between devices  108 us (38%)
  starting transfers between devices  13.3 us (5%)
    pallas_call x25, Pallas kernels, call(): pl.pallas_call(kernel, out_shape=out_shape, grid_spec=pltpu.PrefetchScala...  161 us
    ppermute x10, waiting for transfers between devices, sent(): lax.ppermute(chunk, 'band', [(k, (k - j) % n) for k in range(n)])  108 us
    ppermute x10, starting transfers between devices, sent(): lax.ppermute(chunk, 'band', [(k, (k - j) % n) for k in range(n)])  13.3 us
  transfers between devices with their start and end apart: 11, of which 1 were waited for; matrix products, arithmetic and copies ran while one was open for 0% of the time, Pallas kernels for 53%

profile of v3, /device:TPU:0, one launch (start us, length us, event | category | flops | bytes accessed | tf_op | source)
XLA Modules:
  0.0 286.9 jit_solution(4824401912508610130)
XLA Ops:
  0.6 7.9 %shard_map.51 = bf16[128,12288]{1,0:T(8,128)(2,1)} custom-call(s32[1]{0:T(128)} %bitcast.4.at, bf16[128,32768]{1,0:T(8,128)(2,1)} %src.19), custom_call_target="tpu_custom_call" | custom-call | bytes 8388612 | tf_op jit(solution)/shard_map/pallas_call | solution.py:22
  8.6 3.0 %collective-permute-start.1 = (bf16[128,12288]{1,0:T(8,128)(2,1)}, bf16[128,12288]{1,0:T(8,128)(2,1)}, u32[]{:S(2)}, u32[]{:S(2)}) collective-permute-start(bf16[128,12288]{1,0:T(8,128)(2,1)} %shard_map.51), channel_id=1, source_target_pairs={{0,1},{1,0},{2,3},{3,2},{4,5},{5,4},{6,7},{7,6},{8,9},{9,8},{10,11... | collective-permute-start | bytes 9437192 | tf_op jit(solution)/shard_map/ppermute | solution.py:401
  11.5 3.4 %shard_map.50 = bf16[128,4096]{1,0:T(8,128)(2,1)} custom-call(s32[1]{0:T(128)} %bitcast.3.at, bf16[128,32768]{1,0:T(8,128)(2,1)} %src.19), custom_call_target="tpu_custom_call" | custom-call | bytes 8388612 | tf_op jit(solution)/shard_map/pallas_call | solution.py:22
  14.9 0.0 collective-permute-start
  14.9 6.4 %shard_map.61 = bf16[128,5120]{1,0:T(8,128)(2,1)} custom-call(s32[1]{0:T(128)} %bitcast.10.at, bf16[128,32768]{1,0:T(8,128)(2,1)} %src.19), custom_call_target="tpu_custom_call" | custom-call | bytes 8388612 | tf_op jit(solution)/shard_map/pallas_call | solution.py:22
  21.3 2.0 collective-permute-start.8
  23.3 1.8 shard_map.52
  25.2 0.1 collective-permute-start.2
  25.3 3.4 %shard_map.62 = bf16[128,4096]{1,0:T(8,128)(2,1)} custom-call(s32[1]{0:T(128)} %bitcast.11.at, bf16[128,32768]{1,0:T(8,128)(2,1)} %src.19), custom_call_target="tpu_custom_call" | custom-call | bytes 8388612 | tf_op jit(solution)/shard_map/pallas_call | solution.py:22
  28.7 2.0 collective-permute-start.9
  30.7 2.8 shard_map.60
  33.5 0.6 pad_add_fusion.at
  34.1 108.4 %collective-permute-done.2.refs_1_.refs_2_.refs_0_ = bf16[128,2048]{1,0:T(8,128)(2,1)S(1)} collective-permute-done((bf16[128,2048]{1,0:T(8,128)(2,1)}, bf16[128,2048]{1,0:T(8,128)(2,1)S(1)}, u32[]{:S(2)}, u32[]{:S(2)}) %collective-permute-start.2) | collective-permute-done | bytes 524320 | tf_op jit(solution)/shard_map/ppermute | solution.py:401
  142.5 2.0 collective-permute-start.7
  144.5 51.3 %shard_map.49 = (bf16[128,32768]{1,0:T(8,128)(2,1)}, f32[256,128]{1,0:T(8,128)}) custom-call(s32[2]{0:T(128)} %pad_add_fusion.at, bf16[128,32768]{1,0:T(8,128)(2,1)} %src.19, bf16[128,32768]{1,0:T(8,128)(2,1)} %src.19, bf16[128,32768]{1,0:T(8,128)(2,1)} %src.19, f32[1,32768]{1,0:T(1,128)} %bitcast.13), custom_call_target="tpu_custom_call" | custom-call | flops 2147483648 | bytes 25296904 | tf_op jit(solution)/shard_map/pallas_call | solution.py:22
  195.9 20.9 %shard_map.53.refs_3_ = f32[256,256]{1,0:T(8,128)S(1)} custom-call(s32[2]{0:T(128)S(1)} %copy-done.8, bf16[128,32768]{1,0:T(8,128)(2,1)} %src.19, bf16[128,32768]{1,0:T(8,128)(2,1)} %get-tuple-element.32.applied, f32[1,32768]{1,0:T(1,128)S(1)} %bitcast.14, bf16[128,12288]{1,0:T(8,128)(2,1)} %collective-permute-done.1.refs_0_.refs_1_.refs_2_, ...), custom_call_target="tpu_custom_call" | custom-call | flops 1610612736 | bytes 21102600 | tf_op jit(solution)/shard_map/pallas_call | solution.py:22
  216.7 0.0 collective-permute-done.refs_0_
  216.8 8.2 %shard_map.54 = (f32[128,256]{1,0:T(8,128)S(1)}, f32[128,256]{1,0:T(8,128)S(1)}) custom-call(s32[2]{0:T(128)S(1)} %copy-done.8, bf16[128,32768]{1,0:T(8,128)(2,1)} %src.19, bf16[128,32768]{1,0:T(8,128)(2,1)} %get-tuple-element.32.applied, f32[1,32768]{1,0:T(1,128)S(1)} %bitcast.15, bf16[128,4096]{1,0:T(8,128)(2,1)S(1)} %collective-permute-done.refs_0_, ...), custom_call_target="tpu_custom_call" | custom-call | flops 536870912 | bytes 24510472 | tf_op jit(solution)/shard_map/pallas_call | solution.py:22
  225.0 0.0 copy-start.6
  225.0 0.6 copy-done.6
  225.6 0.6 slice.3
  226.2 0.0 collective-permute-start.3
  226.2 1.6 shard_map.59
  227.9 2.0 collective-permute-start.6
  229.9 0.9 shard_map.58
  230.8 0.0 copy-start.2
  230.8 0.6 copy-done.2
  231.5 0.9 shard_map.57
  232.4 0.7 copy-done.4
  233.1 1.0 shard_map.72
  234.0 0.1 collective-permute-start.5
  234.1 0.0 copy-done.7
  234.2 1.6 shard_map.55
  235.8 3.1 %shard_map.63 = (bf16[128,32768]{1,0:T(8,128)(2,1)}, f32[128,128]{1,0:T(8,128)S(1)}) custom-call(s32[2]{0:T(128)S(1)} %copy-done.8, bf16[128,256]{1,0:T(8,128)(2,1)S(1)} %get-tuple-element.35.coef, bf16[128,32768]{1,0:T(8,128)(2,1)} %src.19, bf16[128,32768]{1,0:T(8,128)(2,1)} %get-tuple-element.32.applied, ...), custom_call_target="tpu_custom_call" | custom-call | flops 268435456 | bytes 17367048 | tf_op jit(solution)/shard_map/pallas_call | solution.py:22
  238.9 11.5 %shard_map.64 = (bf16[128,32768]{1,0:T(8,128)(2,1)}, f32[128,128]{1,0:T(8,128)S(1)}) custom-call(s32[2]{0:T(128)S(1)} %copy-done.8, bf16[128,256]{1,0:T(8,128)(2,1)S(1)} %get-tuple-element.35.coef, bf16[128,32768]{1,0:T(8,128)(2,1)} %src.19, bf16[128,32768]{1,0:T(8,128)(2,1)} %get-tuple-element.32.applied, ...), custom_call_target="tpu_custom_call", output_to_operand_aliasing={{0}: (5, {})} | custom-call | flops 1610612736 | bytes 28442632 | tf_op jit(solution)/shard_map/pallas_call | solution.py:22
  250.4 4.7 %shard_map.65 = (bf16[128,32768]{1,0:T(8,128)(2,1)}, f32[128,128]{1,0:T(8,128)S(1)}) custom-call(s32[2]{0:T(128)S(1)} %copy-done.8, bf16[128,256]{1,0:T(8,128)(2,1)S(1)} %get-tuple-element.35.coef, bf16[128,32768]{1,0:T(8,128)(2,1)} %src.19, bf16[128,32768]{1,0:T(8,128)(2,1)} %get-tuple-element.32.applied, ...), custom_call_target="tpu_custom_call", output_to_operand_aliasing={{0}: (5, {})} | custom-call | flops 536870912 | bytes 26345480 | tf_op jit(solution)/shard_map/pallas_call | solution.py:22
  255.1 0.0 collective-permute-done.9.refs_0_
  255.1 2.1 collective-permute-start.4
  257.2 0.0 collective-permute-done.8.refs_0_
  257.2 0.1 collective-permute-start.10
  257.3 4.9 %shard_map.66 = (bf16[128,32768]{1,0:T(8,128)(2,1)}, f32[128,128]{1,0:T(8,128)S(1)}) custom-call(s32[2]{0:T(128)S(1)} %copy-done.8, bf16[128,256]{1,0:T(8,128)(2,1)S(1)} %get-tuple-element.35.coef, bf16[128,32768]{1,0:T(8,128)(2,1)} %src.19, bf16[128,32768]{1,0:T(8,128)(2,1)} %get-tuple-element.32.applied, ...), custom_call_target="tpu_custom_call", output_to_operand_aliasing={{0}: (5, {})} | custom-call | flops 536870912 | bytes 26345480 | tf_op jit(solution)/shard_map/pallas_call | solution.py:22
  262.2 1.7 shard_map.56
  263.9 8.5 %shard_map.67 = (bf16[128,32768]{1,0:T(8,128)(2,1)}, f32[128,128]{1,0:T(8,128)S(1)}) custom-call(s32[2]{0:T(128)S(1)} %copy-done.8, bf16[128,256]{1,0:T(8,128)(2,1)S(1)} %get-tuple-element.35.coef, bf16[128,32768]{1,0:T(8,128)(2,1)} %src.19, bf16[128,32768]{1,0:T(8,128)(2,1)} %get-tuple-element.32.applied, ...), custom_call_target="tpu_custom_call", output_to_operand_aliasing={{0}: (5, {})} | custom-call | flops 671088640 | bytes 26607624 | tf_op jit(solution)/shard_map/pallas_call | solution.py:22
  272.4 5.4 %shard_map.68 = (bf16[128,32768]{1,0:T(8,128)(2,1)}, f32[128,128]{1,0:T(8,128)S(1)}) custom-call(s32[2]{0:T(128)S(1)} %copy-done.8, bf16[128,256]{1,0:T(8,128)(2,1)S(1)} %get-tuple-element.35.coef, bf16[128,32768]{1,0:T(8,128)(2,1)} %src.19, bf16[128,32768]{1,0:T(8,128)(2,1)} %get-tuple-element.32.applied, ...), custom_call_target="tpu_custom_call", output_to_operand_aliasing={{0}: (5, {})} | custom-call | flops 335544320 | bytes 25952264 | tf_op jit(solution)/shard_map/pallas_call | solution.py:22
  277.7 2.9 %shard_map.69 = (bf16[128,32768]{1,0:T(8,128)(2,1)}, f32[128,128]{1,0:T(8,128)S(1)}) custom-call(s32[2]{0:T(128)S(1)} %copy-done.8, bf16[128,256]{1,0:T(8,128)(2,1)S(1)} %get-tuple-element.35.coef, bf16[128,32768]{1,0:T(8,128)(2,1)} %src.19, bf16[128,32768]{1,0:T(8,128)(2,1)} %get-tuple-element.32.applied, ...), custom_call_target="tpu_custom_call", output_to_operand_aliasing={{0}: (5, {})} | custom-call | flops 134217728 | bytes 25559048 | tf_op jit(solution)/shard_map/pallas_call | solution.py:22
  280.6 2.4 shard_map.70
  283.0 2.4 shard_map.71
  285.4 1.5 shard_map.73
  (19 shorter events, 0.0 us)
Async XLA Ops:
  8.6 187.3 %collective-permute-start.1 = (bf16[128,12288]{1,0:T(8,128)(2,1)}, bf16[128,12288]{1,0:T(8,128)(2,1)}, u32[]{:S(2)}, u32[]{:S(2)}) collective-permute-start(bf16[128,12288]{1,0:T(8,128)(2,1)} %shard_map.51), channel_id=1, source_target_pairs={{0,1},{1,0},{2,3},{3,2},{4,5},{5,4},{6,7},{7,6},{8,9},{9,8},{10,11... | collective-permute-start | bytes 9437192 | tf_op jit(solution)/shard_map/ppermute | solution.py:401
  14.9 201.8 %collective-permute-start = (bf16[128,4096]{1,0:T(8,128)(2,1)}, bf16[128,4096]{1,0:T(8,128)(2,1)S(1)}, u32[]{:S(2)}, u32[]{:S(2)}) collective-permute-start(bf16[128,4096]{1,0:T(8,128)(2,1)} %shard_map.50), channel_id=1, source_target_pairs={{0,1},{1,0},{2,3},{3,2},{4,5},{5,4},{6,7},{7,6},{8,9},{9,8},{10,11... | collective-permute-start | bytes 3145736 | tf_op jit(solution)/shard_map/ppermute | solution.py:401
  21.3 235.9 %collective-permute-start.8 = (bf16[128,5120]{1,0:T(8,128)(2,1)}, bf16[128,5120]{1,0:T(8,128)(2,1)S(1)}, u32[]{:S(2)}, u32[]{:S(2)}) collective-permute-start(bf16[128,5120]{1,0:T(8,128)(2,1)} %shard_map.61), channel_id=1, source_target_pairs={{0,1},{1,0},{2,3},{3,2},{4,5},{5,4},{6,7},{7,6},{8,9},{9,8},{10,11... | collective-permute-start | bytes 3932168 | tf_op jit(solution)/shard_map/ppermute | solution.py:401
  25.2 117.3 %collective-permute-start.2 = (bf16[128,2048]{1,0:T(8,128)(2,1)}, bf16[128,2048]{1,0:T(8,128)(2,1)S(1)}, u32[]{:S(2)}, u32[]{:S(2)}) collective-permute-start(bf16[128,2048]{1,0:T(8,128)(2,1)} %shard_map.52), channel_id=1, source_target_pairs={{0,1},{1,0},{2,3},{3,2},{4,5},{5,4},{6,7},{7,6},{8,9},{9,8},{10,11... | collective-permute-start | bytes 1572872 | tf_op jit(solution)/shard_map/ppermute | solution.py:401
  28.7 226.5 %collective-permute-start.9 = (bf16[128,4096]{1,0:T(8,128)(2,1)}, bf16[128,4096]{1,0:T(8,128)(2,1)}, u32[]{:S(2)}, u32[]{:S(2)}) collective-permute-start(bf16[128,4096]{1,0:T(8,128)(2,1)} %shard_map.62), channel_id=1, source_target_pairs={{0,1},{1,0},{2,3},{3,2},{4,5},{5,4},{6,7},{7,6},{8,9},{9,8},{10,11... | collective-permute-start | bytes 3145736 | tf_op jit(solution)/shard_map/ppermute | solution.py:401
  142.5 129.9 %collective-permute-start.7 = (bf16[128,2560]{1,0:T(8,128)(2,1)S(1)}, bf16[128,2560]{1,0:T(8,128)(2,1)}, u32[]{:S(2)}, u32[]{:S(2)}) collective-permute-start(bf16[128,2560]{1,0:T(8,128)(2,1)S(1)} %shard_map.60), channel_id=1, source_target_pairs={{0,1},{1,0},{2,3},{3,2},{4,5},{5,4},{6,7},{7,6},{8,9},{9,8},{10,11... | collective-permute-start | bytes 1966088 | tf_op jit(solution)/shard_map/ppermute | solution.py:401
  144.5 51.3 %copy-start = (f32[32768]{0:T(1024)S(1)}, f32[32768]{0:T(1024)}, u32[]{:S(2)}) copy-start(f32[32768]{0:T(1024)} %param.3) | copy-start | bytes 393220
  144.5 51.3 %copy-start.8 = (s32[2]{0:T(128)S(1)}, s32[2]{0:T(128)}, u32[]{:S(2)}) copy-start(s32[2]{0:T(128)} %pad_add_fusion.at) | copy-start | bytes 28
  225.0 0.7 copy-start.6
  226.2 7.8 %collective-permute-start.3 = (f32[128,128]{1,0:T(8,128)}, f32[128,128]{1,0:T(8,128)}, u32[]{:S(2)}, u32[]{:S(2)}) collective-permute-start(f32[128,128]{1,0:T(8,128)} %slice.3), channel_id=1, source_target_pairs={{0,1},{1,0},{2,3},{3,2},{4,5},{5,4},{6,7},{7,6},{8,9},{9,8},{10,11... | collective-permute-start | bytes 196616 | tf_op jit(solution)/shard_map/ppermute | solution.py:419
  227.9 49.9 %collective-permute-start.6 = (bf16[128,1024]{1,0:T(8,128)(2,1)}, bf16[128,1024]{1,0:T(8,128)(2,1)}, u32[]{:S(2)}, u32[]{:S(2)}) collective-permute-start(bf16[128,1024]{1,0:T(8,128)(2,1)} %shard_map.59), channel_id=1, source_target_pairs={{0,1},{1,0},{2,3},{3,2},{4,5},{5,4},{6,7},{7,6},{8,9},{9,8},{10,11... | collective-permute-start | bytes 786440 | tf_op jit(solution)/shard_map/ppermute | solution.py:401
  230.8 0.7 copy-start.2
  232.4 0.7 copy-start.4
  233.1 1.0 copy-start.3
  233.1 1.1 copy-start.1
  233.1 1.1 copy-start.7
  234.0 46.6 %collective-permute-start.5 = (bf16[128,512]{1,0:T(8,128)(2,1)S(1)}, bf16[128,512]{1,0:T(8,128)(2,1)S(1)}, u32[]{:S(2)}, u32[]{:S(2)}) collective-permute-start(bf16[128,512]{1,0:T(8,128)(2,1)S(1)} %copy-done.3), channel_id=1, source_target_pairs={{0,1},{1,0},{2,3},{3,2},{4,5},{5,4},{6,7},{7,6},{8,9},{9,8},{10,11... | collective-permute-start | bytes 393224 | tf_op jit(solution)/shard_map/ppermute | solution.py:401
  250.4 4.7 %copy-start.5 = (bf16[128,512]{1,0:T(8,128)(2,1)S(1)}, bf16[128,512]{1,0:T(8,128)(2,1)}, u32[]{:S(2)}) copy-start(bf16[128,512]{1,0:T(8,128)(2,1)} %copy-done.4) | copy-start | bytes 393220
  255.1 27.9 %collective-permute-start.4 = (bf16[128,512]{1,0:T(8,128)(2,1)S(1)}, bf16[128,512]{1,0:T(8,128)(2,1)S(1)}, u32[]{:S(2)}, u32[]{:S(2)}) collective-permute-start(bf16[128,512]{1,0:T(8,128)(2,1)S(1)} %copy-done.5), channel_id=1, source_target_pairs={{0,1},{1,0},{2,3},{3,2},{4,5},{5,4},{6,7},{7,6},{8,9},{9,8},{10,11... | collective-permute-start | bytes 393224 | tf_op jit(solution)/shard_map/ppermute | solution.py:401
  257.2 28.2 %collective-permute-start.10 = (bf16[128,512]{1,0:T(8,128)(2,1)S(1)}, bf16[128,512]{1,0:T(8,128)(2,1)S(1)}, u32[]{:S(2)}, u32[]{:S(2)}) collective-permute-start(bf16[128,512]{1,0:T(8,128)(2,1)S(1)} %shard_map.72), channel_id=1, source_target_pairs={{0,1},{1,0},{2,3},{3,2},{4,5},{5,4},{6,7},{7,6},{8,9},{9,8},{10,11... | collective-permute-start | bytes 393224 | tf_op jit(solution)/shard_map/ppermute | solution.py:401

commit v4 on v3

--- a/solution.py
+++ b/solution.py
@@ -11,6 +11,7 @@
 ROWS = 16
 WHOLE = 2**20
 PARTS = 2
+NARROW = 2
 F32 = jnp.float32
 BF16 = jnp.bfloat16
 ANY = pl.ANY
@@ -121,11 +122,10 @@
         (side,),
         [plane(-1), plane(0), plane(1), pl.BlockSpec((1, size), lambda i, at: (0, i))],
         [plane(0), pl.BlockSpec((2 * own, own), lambda i, at: (0, 0))],
-        [jax.ShapeDtypeStruct((own, grid), BF16), jax.ShapeDtypeStruct((2 * own, own), F32)],
+        [pltpu.HBM((own, grid), BF16), jax.ShapeDtypeStruct((2 * own, own), F32)],
         (token, orbitals, orbitals, orbitals, potential),
         scratch=[pltpu.VMEM((2 * own, size), BF16)],
         flops=4 * own * own * grid,
-        limit=56,
     )
 
 
@@ -301,66 +301,81 @@
 
 
 def ready_body(at, coef, own_ref, applied, base, copied):
-    own = own_ref.shape[0]
-    copied[...] = own_ref[...]
-    base[...] = applied[...].astype(F32) - jnp.dot(coef[:, :own], own_ref[...], preferred_element_type=F32)
-
-
-def ready(at, coef, orbitals, applied, q0, size, ratio):
+    own, size = own_ref.shape
+    columns = pl.ds(pl.multiple_of(pl.program_id(0) * size, size), size)
+    copied[:, columns] = own_ref[...]
+    base[:, columns] = applied[...].astype(F32) - jnp.dot(coef[:, :own], own_ref[...], preferred_element_type=F32)
+
+
+def ready(at, coef, orbitals, applied, q0, width, size, ratio):
     own, grid = orbitals.shape
     count = grid // size
-    plane = pl.BlockSpec((own, size), lambda i, at: (0, lax.rem((at[0] - 1) * ratio + q0 + count, count)))
+    plane = pl.BlockSpec((own, size), lambda i, at: (0, lax.rem((at[0] - 1) * ratio + q0 + i + count, count)))
     return call(
         ready_body,
-        (1,),
+        (width,),
         [pl.BlockSpec(coef.shape, lambda i, at: (0, 0)), plane, plane],
         [pl.BlockSpec(memory_space=pltpu.VMEM)] * 2,
-        [pltpu.VMEM((own, size), F32), pltpu.VMEM((own, size), BF16)],
+        [pltpu.VMEM((own, width * size), F32), pltpu.VMEM((own, width * size), BF16)],
         (at, coef, orbitals, applied),
     )
 
 
-def finish_body(n, size, count, q0, ratio, at, coef, base, copied, sums, gram, *refs):
+def finish_body(n, size, count, q0, width, offset, ratio, last, at, coef, base, copied, sums, gram, *refs):
     rems, (_, out, margin, rows, block, others, sems) = refs[: n - 1], refs[n - 1 :]
     own = copied.shape[0]
+    here = slice(offset * size, (offset + width) * size)
     if n == 2:
         other = rems[0][...]
     else:
         for j in range(n - 1):
             others[j * own : (j + 1) * own, :] = rems[j][...]
         other = others[...]
-    rows[:, :own] = sums[own:, :]
-    rows[:, own:] = gram[...] + rowdot(copied[...], other)
-    rows[...] = pltpu.roll(rows[...], at[1] * own, 1)
-    first = pltpu.make_async_copy(rows, margin, sems.at[0])
-    first.start()
     mixed = jnp.dot(coef[:, own:], other, preferred_element_type=F32)
-    block[...] = (base[...] - mixed).astype(BF16)
-    column = pl.multiple_of(lax.rem((at[0] - 1) * ratio + q0 + count, count) * size, size)
-    second = pltpu.make_async_copy(block, out.at[:, pl.ds(column, size)], sems.at[1])
-    second.start()
-    first.wait()
-    second.wait()
-
-
-def finish(at, coef, base, copied, sums, rems, carry, q0, size, ratio):
+    block[...] = (base[:, here] - mixed).astype(BF16)
+    copies = []
+    for i in range(width):
+        column = pl.multiple_of(lax.rem((at[0] - 1) * ratio + q0 + i + count, count) * size, size)
+        copies.append(
+            pltpu.make_async_copy(
+                block.at[:, pl.ds(i * size, size)], out.at[:, pl.ds(column, size)], sems.at[i]
+            )
+        )
+        copies[-1].start()
+    total = gram[...] + rowdot(copied[:, here], other)
+    if last:
+        rows[:, :own] = sums[own:, :]
+        rows[:, own:] = total
+        rows[...] = pltpu.roll(rows[...], at[1] * own, 1)
+        copies.append(pltpu.make_async_copy(rows, margin, sems.at[width]))
+        copies[-1].start()
+    else:
+        margin[...] = total
+    for copy in copies:
+        copy.wait()
+
+
+def finish(at, coef, base, copied, sums, rems, carry, q0, width, offset, size, ratio, last):
     out, gram = carry
     own, grid = out.shape
     n = len(rems) + 1
     vmem, free = pl.BlockSpec(memory_space=pltpu.VMEM), pl.BlockSpec(memory_space=ANY)
     held = [pltpu.with_memory_space_constraint(a, pltpu.VMEM) for a in (coef, base, copied, sums, gram, *rems)]
     return call(
-        functools.partial(finish_body, n, size, grid // size, q0, ratio),
+        functools.partial(finish_body, n, size, grid // size, q0, width, offset, ratio, last),
         (1,),
         [vmem] * len(held) + [free],
-        [free, free],
-        [jax.ShapeDtypeStruct(out.shape, BF16), jax.ShapeDtypeStruct((own, n * own), F32)],
+        [free, free if last else vmem],
+        [
+            jax.ShapeDtypeStruct(out.shape, BF16),
+            jax.ShapeDtypeStruct((own, n * own), F32) if last else pltpu.VMEM(gram.shape, F32),
+        ],
         (at, *held, out),
         scratch=[
             pltpu.VMEM((own, n * own), F32),
-            pltpu.VMEM((own, size), BF16),
-            pltpu.VMEM(((n - 1) * own, size), BF16),
-            pltpu.SemaphoreType.DMA((2,)),
+            pltpu.VMEM((own, width * size), BF16),
+            pltpu.VMEM(((n - 1) * own, width * size), BF16),
+            pltpu.SemaphoreType.DMA((width + 1,)),
         ],
         aliases={len(held) + 1: 0},
     )
@@ -419,13 +434,15 @@
         got.append(lax.ppermute(others[j - 1][:, own:], "band", perm))
     chunks += [(*block, sent(len(early) + c, *block)) for c, block in enumerate(late)]
     projected, coef = coefficients(at[1:], sums, mine, got)
+    narrow = [chunk for chunk in chunks if chunk[2] == PARTS and chunk[1] <= NARROW]
+    size, low = grid // (side * PARTS), narrow[0][0]
+    base, copied = ready(at, coef, orbitals, applied, low, side * PARTS - low, size, PARTS)
     carry = None
-    q0, _, ratio, rems = chunks.pop()
-    size = grid // (side * ratio)
-    base, copied = ready(at, coef, orbitals, applied, q0, size, ratio)
-    for first, width, parts, block in chunks:
-        carry = rest(at, coef, orbitals, applied, block, carry, first, width, grid // (side * parts), parts)
-    carry = finish(at, coef, base, copied, sums, rems, carry, q0, size, ratio)
+    for q0, width, ratio, rems in chunks[: -len(narrow)]:
+        carry = rest(at, coef, orbitals, applied, rems, carry, q0, width, grid // (side * ratio), ratio)
+    for q0, width, _, rems in narrow:
+        last = q0 + width == side * PARTS
+        carry = finish(at, coef, base, copied, sums, rems, carry, q0, width, q0 - low, size, PARTS, last)
     residuals, margin = carry
     return margin, projected, residuals
 

time: 288 us -> 286 us (level)
  no operation moved by 1% of the time
where the time goes in v4:
time: 286 us; the launch traced here: 285 us
  Pallas kernels  160 us (56%)
  waiting for transfers between devices  108 us (38%)
  starting transfers between devices  13.4 us (5%)
    pallas_call x25, Pallas kernels, call(): pl.pallas_call(kernel, out_shape=out_shape, grid_spec=pltpu.PrefetchScala...  160 us
    ppermute x10, waiting for transfers between devices, sent(): lax.ppermute(chunk, 'band', [(k, (k - j) % n) for k in range(n)])  108 us
    ppermute x10, starting transfers between devices, sent(): lax.ppermute(chunk, 'band', [(k, (k - j) % n) for k in range(n)])  13.4 us
  transfers between devices with their start and end apart: 11, of which 1 were waited for; matrix products, arithmetic and copies ran while one was open for 0% of the time, Pallas kernels for 53%

profile of v4, /device:TPU:0, one launch (start us, length us, event | category | flops | bytes accessed | tf_op | source)
XLA Modules:
  0.0 284.6 jit_solution(16366592140946284689)
XLA Ops:
  0.6 7.9 %shard_map.51 = bf16[128,12288]{1,0:T(8,128)(2,1)} custom-call(s32[1]{0:T(128)} %bitcast.4.at, bf16[128,32768]{1,0:T(8,128)(2,1)} %src.19), custom_call_target="tpu_custom_call" | custom-call | bytes 8388612 | tf_op jit(solution)/shard_map/pallas_call | solution.py:23
  8.6 3.0 %collective-permute-start.1 = (bf16[128,12288]{1,0:T(8,128)(2,1)}, bf16[128,12288]{1,0:T(8,128)(2,1)}, u32[]{:S(2)}, u32[]{:S(2)}) collective-permute-start(bf16[128,12288]{1,0:T(8,128)(2,1)} %shard_map.51), channel_id=1, source_target_pairs={{0,1},{1,0},{2,3},{3,2},{4,5},{5,4},{6,7},{7,6},{8,9},{9,8},{10,11... | collective-permute-start | bytes 9437192 | tf_op jit(solution)/shard_map/ppermute | solution.py:416
  11.5 3.4 %shard_map.50 = bf16[128,4096]{1,0:T(8,128)(2,1)} custom-call(s32[1]{0:T(128)} %bitcast.3.at, bf16[128,32768]{1,0:T(8,128)(2,1)} %src.19), custom_call_target="tpu_custom_call" | custom-call | bytes 8388612 | tf_op jit(solution)/shard_map/pallas_call | solution.py:23
  14.9 0.0 collective-permute-start
  14.9 6.4 %shard_map.58 = bf16[128,5120]{1,0:T(8,128)(2,1)} custom-call(s32[1]{0:T(128)} %bitcast.7.at, bf16[128,32768]{1,0:T(8,128)(2,1)} %src.19), custom_call_target="tpu_custom_call" | custom-call | bytes 8388612 | tf_op jit(solution)/shard_map/pallas_call | solution.py:23
  21.3 2.0 collective-permute-start.5
  23.3 1.9 shard_map.52
  25.2 0.1 collective-permute-start.2
  25.3 0.0 copy-start
  25.3 3.4 %shard_map.59 = bf16[128,4096]{1,0:T(8,128)(2,1)} custom-call(s32[1]{0:T(128)} %bitcast.8.at, bf16[128,32768]{1,0:T(8,128)(2,1)} %src.19), custom_call_target="tpu_custom_call" | custom-call | bytes 8388612 | tf_op jit(solution)/shard_map/pallas_call | solution.py:23
  28.7 2.0 collective-permute-start.6
  30.7 3.6 %shard_map.57 = bf16[128,2560]{1,0:T(8,128)(2,1)} custom-call(s32[1]{0:T(128)} %bitcast.6.at, bf16[128,32768]{1,0:T(8,128)(2,1)} %src.19), custom_call_target="tpu_custom_call" | custom-call | bytes 8388612 | tf_op jit(solution)/shard_map/pallas_call | solution.py:23
  34.3 0.1 pad_add_fusion.at
  34.4 108.1 %collective-permute-done.2.refs_1_.refs_2_.refs_0_ = bf16[128,2048]{1,0:T(8,128)(2,1)S(1)} collective-permute-done((bf16[128,2048]{1,0:T(8,128)(2,1)}, bf16[128,2048]{1,0:T(8,128)(2,1)S(1)}, u32[]{:S(2)}, u32[]{:S(2)}) %collective-permute-start.2) | collective-permute-done | bytes 524320 | tf_op jit(solution)/shard_map/ppermute | solution.py:416
  142.5 2.0 collective-permute-start.4
  144.5 50.6 %shard_map.49 = (bf16[128,32768]{1,0:T(8,128)(2,1)}, f32[256,128]{1,0:T(8,128)S(1)}) custom-call(s32[2]{0:T(128)S(1)} %pad_add_fusion.at, bf16[128,32768]{1,0:T(8,128)(2,1)} %src.19, bf16[128,32768]{1,0:T(8,128)(2,1)} %src.19, bf16[128,32768]{1,0:T(8,128)(2,1)} %src.19, f32[1,32768]{1,0:T(1,128)S(1)} %bitcast.13), custom_call_target="tpu_custom_call" | custom-call | flops 2147483648 | bytes 25296904 | tf_op jit(solution)/shard_map/pallas_call | solution.py:23
  195.1 20.9 %shard_map.53.refs_3_ = f32[256,256]{1,0:T(8,128)S(1)} custom-call(s32[2]{0:T(128)S(1)} %pad_add_fusion.at, bf16[128,32768]{1,0:T(8,128)(2,1)} %src.19, bf16[128,32768]{1,0:T(8,128)(2,1)} %get-tuple-element.32.applied, f32[1,32768]{1,0:T(1,128)S(1)} %bitcast.14, bf16[128,12288]{1,0:T(8,128)(2,1)} %collective-permute-done.1.refs_0_.refs_1_.refs_2_, ...), custom_call_target="tpu_custom_call" | custom-call | flops 1610612736 | bytes 21102600 | tf_op jit(solution)/shard_map/pallas_call | solution.py:23
  216.0 8.2 %shard_map.54 = (f32[128,256]{1,0:T(8,128)S(1)}, f32[128,256]{1,0:T(8,128)S(1)}) custom-call(s32[2]{0:T(128)S(1)} %pad_add_fusion.at, bf16[128,32768]{1,0:T(8,128)(2,1)} %src.19, bf16[128,32768]{1,0:T(8,128)(2,1)} %get-tuple-element.32.applied, f32[1,32768]{1,0:T(1,128)S(1)} %bitcast.15, bf16[128,4096]{1,0:T(8,128)(2,1)S(1)} %collective-permute-done.refs_0_, ...), custom_call_target="tpu_custom_call" | custom-call | flops 536870912 | bytes 24510472 | tf_op jit(solution)/shard_map/pallas_call | solution.py:23
  224.2 0.0 copy-start.5
  224.2 0.6 copy-done.5
  224.8 0.6 slice.3
  225.5 0.0 collective-permute-start.3
  225.5 1.0 shard_map.66
  226.5 2.1 collective-permute-start.7
  228.6 0.9 shard_map.68
  229.5 0.0 copy-start.1
  229.5 0.6 copy-done.1
  230.2 0.9 shard_map.70
  231.1 0.6 copy-done.3
  231.7 1.0 shard_map.72
  232.7 0.1 collective-permute-start.8
  232.8 1.6 shard_map.55
  234.4 3.1 %shard_map.60 = (bf16[128,32768]{1,0:T(8,128)(2,1)}, f32[128,128]{1,0:T(8,128)S(1)}) custom-call(s32[2]{0:T(128)S(1)} %pad_add_fusion.at, bf16[128,256]{1,0:T(8,128)(2,1)S(1)} %get-tuple-element.35.coef, bf16[128,32768]{1,0:T(8,128)(2,1)} %src.19, bf16[128,32768]{1,0:T(8,128)(2,1)} %get-tuple-element.32.applied, ...), custom_call_target="tpu_custom_call" | custom-call | flops 268435456 | bytes 17367048 | tf_op jit(solution)/shard_map/pallas_call | solution.py:23
  237.6 11.5 %shard_map.61 = (bf16[128,32768]{1,0:T(8,128)(2,1)}, f32[128,128]{1,0:T(8,128)S(1)}) custom-call(s32[2]{0:T(128)S(1)} %pad_add_fusion.at, bf16[128,256]{1,0:T(8,128)(2,1)S(1)} %get-tuple-element.35.coef, bf16[128,32768]{1,0:T(8,128)(2,1)} %src.19, bf16[128,32768]{1,0:T(8,128)(2,1)} %get-tuple-element.32.applied, ...), custom_call_target="tpu_custom_call", output_to_operand_aliasing={{0}: (5, {})} | custom-call | flops 1610612736 | bytes 28442632 | tf_op jit(solution)/shard_map/pallas_call | solution.py:23
  249.1 4.0 %shard_map.56 = (f32[128,2560]{1,0:T(8,128)S(1)}, bf16[128,2560]{1,0:T(8,128)(2,1)S(1)}) custom-call(s32[2]{0:T(128)S(1)} %pad_add_fusion.at, bf16[128,256]{1,0:T(8,128)(2,1)S(1)} %get-tuple-element.35.coef, bf16[128,32768]{1,0:T(8,128)(2,1)} %src.19, bf16[128,32768]{1,0:T(8,128)(2,1)} %get-tuple-element.32.applied), custom_call_target="tpu_custom_call" | custom-call | bytes 16842760 | tf_op jit(solution)/shard_map/pallas_call | solution.py:23
  253.1 4.7 %shard_map.62 = (bf16[128,32768]{1,0:T(8,128)(2,1)}, f32[128,128]{1,0:T(8,128)S(1)}) custom-call(s32[2]{0:T(128)S(1)} %pad_add_fusion.at, bf16[128,256]{1,0:T(8,128)(2,1)S(1)} %get-tuple-element.35.coef, bf16[128,32768]{1,0:T(8,128)(2,1)} %src.19, bf16[128,32768]{1,0:T(8,128)(2,1)} %get-tuple-element.32.applied, ...), custom_call_target="tpu_custom_call", output_to_operand_aliasing={{0}: (5, {})} | custom-call | flops 536870912 | bytes 26345480 | tf_op jit(solution)/shard_map/pallas_call | solution.py:23
  257.9 2.1 collective-permute-start.9
  259.9 0.0 collective-permute-done.5.refs_0_
  259.9 0.1 collective-permute-start.10
  260.0 4.9 %shard_map.63 = (bf16[128,32768]{1,0:T(8,128)(2,1)}, f32[128,128]{1,0:T(8,128)S(1)}) custom-call(s32[2]{0:T(128)S(1)} %pad_add_fusion.at, bf16[128,256]{1,0:T(8,128)(2,1)S(1)} %get-tuple-element.35.coef, bf16[128,32768]{1,0:T(8,128)(2,1)} %src.19, bf16[128,32768]{1,0:T(8,128)(2,1)} %get-tuple-element.32.applied, ...), custom_call_target="tpu_custom_call", output_to_operand_aliasing={{0}: (5, {})} | custom-call | flops 536870912 | bytes 26345480 | tf_op jit(solution)/shard_map/pallas_call | solution.py:23
  264.9 8.5 %shard_map.64 = (bf16[128,32768]{1,0:T(8,128)(2,1)}, f32[128,128]{1,0:T(8,128)S(1)}) custom-call(s32[2]{0:T(128)S(1)} %pad_add_fusion.at, bf16[128,256]{1,0:T(8,128)(2,1)S(1)} %get-tuple-element.35.coef, bf16[128,32768]{1,0:T(8,128)(2,1)} %src.19, bf16[128,32768]{1,0:T(8,128)(2,1)} %get-tuple-element.32.applied, ...), custom_call_target="tpu_custom_call", output_to_operand_aliasing={{0}: (5, {})} | custom-call | flops 671088640 | bytes 26607624 | tf_op jit(solution)/shard_map/pallas_call | solution.py:23
  273.4 5.4 %shard_map.65 = (bf16[128,32768]{1,0:T(8,128)(2,1)}, f32[128,128]{1,0:T(8,128)S(1)}) custom-call(s32[2]{0:T(128)S(1)} %pad_add_fusion.at, bf16[128,256]{1,0:T(8,128)(2,1)S(1)} %get-tuple-element.35.coef, bf16[128,32768]{1,0:T(8,128)(2,1)} %src.19, bf16[128,32768]{1,0:T(8,128)(2,1)} %get-tuple-element.32.applied, ...), custom_call_target="tpu_custom_call", output_to_operand_aliasing={{0}: (5, {})} | custom-call | flops 335544320 | bytes 25952264 | tf_op jit(solution)/shard_map/pallas_call | solution.py:23
  278.8 1.5 shard_map.67
  280.3 1.4 shard_map.69
  281.7 0.0 collective-permute-done.9.refs_0_
  281.7 1.4 shard_map.71
  283.1 0.0 collective-permute-done.10.refs_0_
  283.1 1.5 shard_map.73
  (15 shorter events, 0.0 us)
Async XLA Ops:
  8.6 186.5 %collective-permute-start.1 = (bf16[128,12288]{1,0:T(8,128)(2,1)}, bf16[128,12288]{1,0:T(8,128)(2,1)}, u32[]{:S(2)}, u32[]{:S(2)}) collective-permute-start(bf16[128,12288]{1,0:T(8,128)(2,1)} %shard_map.51), channel_id=1, source_target_pairs={{0,1},{1,0},{2,3},{3,2},{4,5},{5,4},{6,7},{7,6},{8,9},{9,8},{10,11... | collective-permute-start | bytes 9437192 | tf_op jit(solution)/shard_map/ppermute | solution.py:416
  14.9 201.0 %collective-permute-start = (bf16[128,4096]{1,0:T(8,128)(2,1)}, bf16[128,4096]{1,0:T(8,128)(2,1)S(1)}, u32[]{:S(2)}, u32[]{:S(2)}) collective-permute-start(bf16[128,4096]{1,0:T(8,128)(2,1)} %shard_map.50), channel_id=1, source_target_pairs={{0,1},{1,0},{2,3},{3,2},{4,5},{5,4},{6,7},{7,6},{8,9},{9,8},{10,11... | collective-permute-start | bytes 3145736 | tf_op jit(solution)/shard_map/ppermute | solution.py:416
  21.3 238.6 %collective-permute-start.5 = (bf16[128,5120]{1,0:T(8,128)(2,1)}, bf16[128,5120]{1,0:T(8,128)(2,1)S(1)}, u32[]{:S(2)}, u32[]{:S(2)}) collective-permute-start(bf16[128,5120]{1,0:T(8,128)(2,1)} %shard_map.58), channel_id=1, source_target_pairs={{0,1},{1,0},{2,3},{3,2},{4,5},{5,4},{6,7},{7,6},{8,9},{9,8},{10,11... | collective-permute-start | bytes 3932168 | tf_op jit(solution)/shard_map/ppermute | solution.py:416
  25.2 117.3 %collective-permute-start.2 = (bf16[128,2048]{1,0:T(8,128)(2,1)}, bf16[128,2048]{1,0:T(8,128)(2,1)S(1)}, u32[]{:S(2)}, u32[]{:S(2)}) collective-permute-start(bf16[128,2048]{1,0:T(8,128)(2,1)} %shard_map.52), channel_id=1, source_target_pairs={{0,1},{1,0},{2,3},{3,2},{4,5},{5,4},{6,7},{7,6},{8,9},{9,8},{10,11... | collective-permute-start | bytes 1572872 | tf_op jit(solution)/shard_map/ppermute | solution.py:416
  25.3 119.3 %copy-start = (f32[32768]{0:T(1024)S(1)}, f32[32768]{0:T(1024)}, u32[]{:S(2)}) copy-start(f32[32768]{0:T(1024)} %param.3) | copy-start | bytes 393220
  28.7 229.1 %collective-permute-start.6 = (bf16[128,4096]{1,0:T(8,128)(2,1)}, bf16[128,4096]{1,0:T(8,128)(2,1)}, u32[]{:S(2)}, u32[]{:S(2)}) collective-permute-start(bf16[128,4096]{1,0:T(8,128)(2,1)} %shard_map.59), channel_id=1, source_target_pairs={{0,1},{1,0},{2,3},{3,2},{4,5},{5,4},{6,7},{7,6},{8,9},{9,8},{10,11... | collective-permute-start | bytes 3145736 | tf_op jit(solution)/shard_map/ppermute | solution.py:416
  142.5 130.9 %collective-permute-start.4 = (bf16[128,2560]{1,0:T(8,128)(2,1)}, bf16[128,2560]{1,0:T(8,128)(2,1)}, u32[]{:S(2)}, u32[]{:S(2)}) collective-permute-start(bf16[128,2560]{1,0:T(8,128)(2,1)} %shard_map.57), channel_id=1, source_target_pairs={{0,1},{1,0},{2,3},{3,2},{4,5},{5,4},{6,7},{7,6},{8,9},{9,8},{10,11... | collective-permute-start | bytes 1966088 | tf_op jit(solution)/shard_map/ppermute | solution.py:416
  224.2 0.7 copy-start.5
  225.5 7.2 %collective-permute-start.3 = (f32[128,128]{1,0:T(8,128)}, f32[128,128]{1,0:T(8,128)}, u32[]{:S(2)}, u32[]{:S(2)}) collective-permute-start(f32[128,128]{1,0:T(8,128)} %slice.3), channel_id=1, source_target_pairs={{0,1},{1,0},{2,3},{3,2},{4,5},{5,4},{6,7},{7,6},{8,9},{9,8},{10,11... | collective-permute-start | bytes 196616 | tf_op jit(solution)/shard_map/ppermute | solution.py:434
  226.5 52.3 %collective-permute-start.7 = (bf16[128,1024]{1,0:T(8,128)(2,1)S(1)}, bf16[128,1024]{1,0:T(8,128)(2,1)S(1)}, u32[]{:S(2)}, u32[]{:S(2)}) collective-permute-start(bf16[128,1024]{1,0:T(8,128)(2,1)S(1)} %shard_map.66), channel_id=1, source_target_pairs={{0,1},{1,0},{2,3},{3,2},{4,5},{5,4},{6,7},{7,6},{8,9},{9,8},{10,11... | collective-permute-start | bytes 786440 | tf_op jit(solution)/shard_map/ppermute | solution.py:416
  229.5 0.7 copy-start.1
  231.1 0.6 copy-start.3
  231.7 1.0 copy-start.2
  231.7 1.1 copy-start.6
  232.7 47.5 %collective-permute-start.8 = (bf16[128,512]{1,0:T(8,128)(2,1)S(1)}, bf16[128,512]{1,0:T(8,128)(2,1)S(1)}, u32[]{:S(2)}, u32[]{:S(2)}) collective-permute-start(bf16[128,512]{1,0:T(8,128)(2,1)S(1)} %copy-done.2), channel_id=1, source_target_pairs={{0,1},{1,0},{2,3},{3,2},{4,5},{5,4},{6,7},{7,6},{8,9},{9,8},{10,11... | collective-permute-start | bytes 393224 | tf_op jit(solution)/shard_map/ppermute | solution.py:416
  253.1 4.7 %copy-start.4 = (bf16[128,512]{1,0:T(8,128)(2,1)S(1)}, bf16[128,512]{1,0:T(8,128)(2,1)}, u32[]{:S(2)}) copy-start(bf16[128,512]{1,0:T(8,128)(2,1)} %copy-done.3) | copy-start | bytes 393220
  257.9 23.8 %collective-permute-start.9 = (bf16[128,512]{1,0:T(8,128)(2,1)S(1)}, bf16[128,512]{1,0:T(8,128)(2,1)S(1)}, u32[]{:S(2)}, u32[]{:S(2)}) collective-permute-start(bf16[128,512]{1,0:T(8,128)(2,1)S(1)} %copy-done.4), channel_id=1, source_target_pairs={{0,1},{1,0},{2,3},{3,2},{4,5},{5,4},{6,7},{7,6},{8,9},{9,8},{10,11... | collective-permute-start | bytes 393224 | tf_op jit(solution)/shard_map/ppermute | solution.py:416
  259.9 23.2 %collective-permute-start.10 = (bf16[128,512]{1,0:T(8,128)(2,1)S(1)}, bf16[128,512]{1,0:T(8,128)(2,1)S(1)}, u32[]{:S(2)}, u32[]{:S(2)}) collective-permute-start(bf16[128,512]{1,0:T(8,128)(2,1)S(1)} %shard_map.72), channel_id=1, source_target_pairs={{0,1},{1,0},{2,3},{3,2},{4,5},{5,4},{6,7},{7,6},{8,9},{9,8},{10,11... | collective-permute-start | bytes 393224 | tf_op jit(solution)/shard_map/ppermute | solution.py:416

commit v5 on v4

--- a/solution.py
+++ b/solution.py
@@ -17,14 +17,14 @@
 ANY = pl.ANY
 
 
-def call(kernel, grid, in_specs, out_specs, out_shape, args, scratch=(), aliases={}, flops=0, limit=16):
+def call(kernel, grid, in_specs, out_specs, out_shape, args, scratch=(), aliases={}, flops=0, limit=16, scalars=1):
     args = [pltpu.with_memory_space_constraint(a, pltpu.HBM) if a.size >= WHOLE else a for a in args]
     touched = sum(a.size * a.dtype.itemsize for a in args)
     return pl.pallas_call(
         kernel,
         out_shape=out_shape,
         grid_spec=pltpu.PrefetchScalarGridSpec(
-            num_scalar_prefetch=1, grid=grid, in_specs=in_specs, out_specs=out_specs, scratch_shapes=scratch
+            num_scalar_prefetch=scalars, grid=grid, in_specs=in_specs, out_specs=out_specs, scratch_shapes=scratch
         ),
         input_output_aliases=aliases,
         compiler_params=pltpu.CompilerParams(
@@ -47,26 +47,10 @@
     return lax.dot_general(a, b, (((1,), (1,)), ((), ())), preferred_element_type=F32)
 
 
-def pack_body(at, src, dst):
-    dst[...] = src[...]
-
-
-def pack(orbitals, start, width, size):
-    own, count = orbitals.shape[0], orbitals.shape[1] // size
-    return call(
-        pack_body,
-        (width,),
-        [pl.BlockSpec((own, size), lambda i, at: (0, lax.rem(at[0] + i, count)))],
-        pl.BlockSpec((own, size), lambda i, at: (0, i)),
-        jax.ShapeDtypeStruct((own, width * size), BF16),
-        (start, orbitals),
-    )
-
-
-def grab_body(width, size, count, at, src, dst, sems):
-    copies = []
+def pack_body(start, width, size, count, src, dst, sems):
+    first, copies = start(lax.axis_index("band")), []
     for i in range(width):
-        column = pl.multiple_of(lax.rem(at[0] + i, count) * size, size)
+        column = pl.multiple_of(lax.rem(first + i, count) * size, size)
         copies.append(
             pltpu.make_async_copy(src.at[:, pl.ds(column, size)], dst.at[:, pl.ds(i * size, size)], sems.at[i])
         )
@@ -76,16 +60,17 @@
         copy.wait()
 
 
-def grab(orbitals, start, width, size):
+def pack(orbitals, start, width, size):
     own, count = orbitals.shape[0], orbitals.shape[1] // size
     return call(
-        functools.partial(grab_body, width, size, count),
+        functools.partial(pack_body, start, width, size, count),
         (1,),
         [pl.BlockSpec(memory_space=ANY)],
         pl.BlockSpec(memory_space=pltpu.VMEM),
         pltpu.VMEM((own, width * size), BF16),
-        (start, orbitals),
+        (orbitals,),
         scratch=[pltpu.SemaphoreType.DMA((width,))],
+        scalars=0,
     )
 
 
@@ -321,8 +306,9 @@
     )
 
 
-def finish_body(n, size, count, q0, width, offset, ratio, last, at, coef, base, copied, sums, gram, *refs):
+def finish_body(n, size, count, q0, width, offset, ratio, share, last, coef, base, copied, sums, gram, *refs):
     rems, (_, out, margin, rows, block, others, sems) = refs[: n - 1], refs[n - 1 :]
+    me = lax.axis_index("band")
     own = copied.shape[0]
     here = slice(offset * size, (offset + width) * size)
     if n == 2:
@@ -335,7 +321,7 @@
     block[...] = (base[:, here] - mixed).astype(BF16)
     copies = []
     for i in range(width):
-        column = pl.multiple_of(lax.rem((at[0] - 1) * ratio + q0 + i + count, count) * size, size)
+        column = pl.multiple_of(lax.rem((me * share - 1) * ratio + q0 + i + count, count) * size, size)
         copies.append(
             pltpu.make_async_copy(
                 block.at[:, pl.ds(i * size, size)], out.at[:, pl.ds(column, size)], sems.at[i]
@@ -346,7 +332,7 @@
     if last:
         rows[:, :own] = sums[own:, :]
         rows[:, own:] = total
-        rows[...] = pltpu.roll(rows[...], at[1] * own, 1)
+        rows[...] = pltpu.roll(rows[...], me * own, 1)
         copies.append(pltpu.make_async_copy(rows, margin, sems.at[width]))
         copies[-1].start()
     else:
@@ -355,14 +341,14 @@
         copy.wait()
 
 
-def finish(at, coef, base, copied, sums, rems, carry, q0, width, offset, size, ratio, last):
+def finish(share, coef, base, copied, sums, rems, carry, q0, width, offset, size, ratio, last):
     out, gram = carry
     own, grid = out.shape
     n = len(rems) + 1
     vmem, free = pl.BlockSpec(memory_space=pltpu.VMEM), pl.BlockSpec(memory_space=ANY)
     held = [pltpu.with_memory_space_constraint(a, pltpu.VMEM) for a in (coef, base, copied, sums, gram, *rems)]
     return call(
-        functools.partial(finish_body, n, size, grid // size, q0, width, offset, ratio, last),
+        functools.partial(finish_body, n, size, grid // size, q0, width, offset, ratio, share, last),
         (1,),
         [vmem] * len(held) + [free],
         [free, free if last else vmem],
@@ -370,23 +356,16 @@
             jax.ShapeDtypeStruct(out.shape, BF16),
             jax.ShapeDtypeStruct((own, n * own), F32) if last else pltpu.VMEM(gram.shape, F32),
         ],
-        (at, *held, out),
+        (*held, out),
         scratch=[
             pltpu.VMEM((own, n * own), F32),
             pltpu.VMEM((own, width * size), BF16),
             pltpu.VMEM(((n - 1) * own, width * size), BF16),
             pltpu.SemaphoreType.DMA((width + 1,)),
         ],
-        aliases={len(held) + 1: 0},
-    )
-
-
-def cuts(count):
-    out = []
-    while count:
-        out.append(max(1, count // 2))
-        count -= out[-1]
-    return out
+        aliases={len(held): 0},
+        scalars=0,
+    )
 
 
 def plan(n, side):
@@ -394,9 +373,12 @@
     short = max(2, share // 4)
     widths = [2] + ([share - short, short] if share >= 4 else [share])
     widths.append((side - share - 2) // 3)
-    after = cuts(PARTS * (side - sum(widths)))
     early = [(sum(widths[:c]), w, 1) for c, w in enumerate(widths)]
-    late = [(PARTS * sum(widths) + sum(after[:c]), w, PARTS) for c, w in enumerate(after)]
+    done = sum(widths)
+    wide = side - done - 2
+    late = [(done, wide - wide // 2, 1), (side - 2 - wide // 2, wide // 2, 1)]
+    narrow = [NARROW] + [1] * (2 * PARTS - NARROW)
+    late += [(PARTS * (side - 2) + sum(narrow[:c]), w, PARTS) for c, w in enumerate(narrow)]
     return early, late
 
 
@@ -407,18 +389,20 @@
     me = lax.axis_index("band")
     potential = potential.reshape(1, grid)
 
-    def sent(c, q0, width, ratio):
+    def sent(q0, width, ratio):
         got, count = [], side * ratio
         for j in range(1, n):
-            dest = lax.rem(me + n - j, n)
-            start = lax.rem((dest * share - 1) * ratio + q0 + count, count).astype(jnp.int32).reshape(1)
-            chunk = (pack if c else grab)(orbitals, start, width, grid // count)
+
+            def start(me, j=j):
+                return lax.rem((lax.rem(me + n - j, n) * share - 1) * ratio + q0 + count, count)
+
+            chunk = pack(orbitals, start, width, grid // count)
             got.append(lax.ppermute(chunk, "band", [(k, (k - j) % n) for k in range(n)]))
         return got
 
     early, late = plan(n, side)
     at = jnp.stack([me * share, me]).astype(jnp.int32)
-    chunks = [(*block, sent(c, *block)) for c, block in enumerate(early)]
+    chunks = [(*block, sent(*block)) for block in early]
     applied, sums = apply_own(orbitals, potential, at, side)
     before = None
     for c in range(1, len(early) - 1):
@@ -432,7 +416,7 @@
     for j in range(1, n):
         perm = [(k, (k - j) % n) for k in range(n)]
         got.append(lax.ppermute(others[j - 1][:, own:], "band", perm))
-    chunks += [(*block, sent(len(early) + c, *block)) for c, block in enumerate(late)]
+    chunks += [(*block, sent(*block)) for block in late]
     projected, coef = coefficients(at[1:], sums, mine, got)
     narrow = [chunk for chunk in chunks if chunk[2] == PARTS and chunk[1] <= NARROW]
     size, low = grid // (side * PARTS), narrow[0][0]
@@ -442,7 +426,7 @@
         carry = rest(at, coef, orbitals, applied, rems, carry, q0, width, grid // (side * ratio), ratio)
     for q0, width, _, rems in narrow:
         last = q0 + width == side * PARTS
-        carry = finish(at, coef, base, copied, sums, rems, carry, q0, width, q0 - low, size, PARTS, last)
+        carry = finish(share, coef, base, copied, sums, rems, carry, q0, width, q0 - low, size, PARTS, last)
     residuals, margin = carry
     return margin, projected, residuals
 

time: 286 us -> 223 us (0.78)
  waiting for transfers between devices: 108 us -> 71.6 us
  Pallas kernels: 160 us -> 136 us
    ppermute x10 -> x9, waiting for transfers between devices: 108 us -> 67.1 us  [sent(): lax.ppermute(chunk, 'band', [(k, (k - j) % n) for k in range(n)])]
    pallas_call x25 -> x23, Pallas kernels: 160 us -> 136 us  [call(): pl.pallas_call(kernel, out_shape=out_shape, grid_spec=pltpu.PrefetchScala...]
    ppermute x1, waiting for transfers between devices: 0.01 us -> 4.48 us  [shards(): got.append(lax.ppermute(others[j - 1][:, own:], 'band', perm))]
    ppermute x10 -> x9, starting transfers between devices: 13.4 us -> 13.4 us  [sent(): lax.ppermute(chunk, 'band', [(k, (k - j) % n) for k in range(n)])]
  transfers between devices with their start and end apart: 11 -> 10, of which waited for: 1 -> 2; matrix products, arithmetic and copies ran while one was open for 0% -> 0% of each run, Pallas kernels for 53% -> 59%
where the time goes in v5:
time: 223 us; the launch traced here: 222 us
  Pallas kernels  136 us (61%)
  waiting for transfers between devices  71.6 us (32%)
  starting transfers between devices  13.5 us (6%)
    pallas_call x23, Pallas kernels, call(): pl.pallas_call(kernel, out_shape=out_shape, grid_spec=pltpu.PrefetchScala...  136 us
    ppermute x9, waiting for transfers between devices, sent(): lax.ppermute(chunk, 'band', [(k, (k - j) % n) for k in range(n)])  67.1 us
    ppermute x9, starting transfers between devices, sent(): lax.ppermute(chunk, 'band', [(k, (k - j) % n) for k in range(n)])  13.4 us
    ppermute x1, waiting for transfers between devices, shards(): got.append(lax.ppermute(others[j - 1][:, own:], 'band', perm))  4.48 us
  transfers between devices with their start and end apart: 10, of which 2 were waited for; matrix products, arithmetic and copies ran while one was open for 0% of the time, Pallas kernels for 59%

profile of v5, /device:TPU:0, one launch (start us, length us, event | category | flops | bytes accessed | tf_op | source)
XLA Modules:
  0.0 221.7 jit_solution(807427277889930863)
XLA Ops:
  0.6 3.6 %shard_map.51 = bf16[128,12288]{1,0:T(8,128)(2,1)} custom-call(bf16[128,32768]{1,0:T(8,128)(2,1)} %src.17), custom_call_target="tpu_custom_call" | custom-call | bytes 8388608 | tf_op jit(solution)/shard_map/pallas_call | solution.py:23
  4.3 3.0 %collective-permute-start.1 = (bf16[128,12288]{1,0:T(8,128)(2,1)}, bf16[128,12288]{1,0:T(8,128)(2,1)}, u32[]{:S(2)}, u32[]{:S(2)}) collective-permute-start(bf16[128,12288]{1,0:T(8,128)(2,1)} %shard_map.51), channel_id=1, source_target_pairs={{0,1},{1,0},{2,3},{3,2},{4,5},{5,4},{6,7},{7,6},{8,9},{9,8},{10,11... | collective-permute-start | bytes 9437192 | tf_op jit(solution)/shard_map/ppermute | solution.py:400
  7.3 1.0 shard_map.52
  8.3 0.1 collective-permute-start.2
  8.4 2.2 shard_map.50
  10.7 2.1 collective-permute-start
  12.7 2.2 %shard_map.59 = bf16[128,4096]{1,0:T(8,128)(2,1)} custom-call(bf16[128,32768]{1,0:T(8,128)(2,1)} %src.17), custom_call_target="tpu_custom_call" | custom-call | bytes 8388608 | tf_op jit(solution)/shard_map/pallas_call | solution.py:23
  14.9 0.0 copy-start
  15.0 0.1 collective-permute-start.6
  15.1 2.3 %shard_map.58 = bf16[128,4096]{1,0:T(8,128)(2,1)} custom-call(bf16[128,32768]{1,0:T(8,128)(2,1)} %src.17), custom_call_target="tpu_custom_call" | custom-call | bytes 8388608 | tf_op jit(solution)/shard_map/pallas_call | solution.py:23
  17.3 2.1 collective-permute-start.5
  19.4 1.2 shard_map.57
  20.6 67.1 %collective-permute-done.2.refs_1_.refs_2_.refs_0_ = bf16[128,2048]{1,0:T(8,128)(2,1)S(1)} collective-permute-done((bf16[128,2048]{1,0:T(8,128)(2,1)S(1)}, bf16[128,2048]{1,0:T(8,128)(2,1)S(1)}, u32[]{:S(2)}, u32[]{:S(2)}) %collective-permute-start.2) | collective-permute-done | bytes 524320 | tf_op jit(solution)/shard_map/ppermute | solution.py:400
  87.7 2.0 collective-permute-start.4
  89.7 0.1 pad_add_fusion.at
  89.8 0.0 copy-done
  89.8 50.6 %shard_map.49 = (bf16[128,32768]{1,0:T(8,128)(2,1)}, f32[256,128]{1,0:T(8,128)S(1)}) custom-call(s32[2]{0:T(128)S(1)} %pad_add_fusion.at, bf16[128,32768]{1,0:T(8,128)(2,1)} %src.17, bf16[128,32768]{1,0:T(8,128)(2,1)} %src.17, bf16[128,32768]{1,0:T(8,128)(2,1)} %src.17, f32[1,32768]{1,0:T(1,128)S(1)} %bitcast.3), custom_call_target="tpu_custom_call" | custom-call | flops 2147483648 | bytes 25296904 | tf_op jit(solution)/shard_map/pallas_call | solution.py:23
  140.4 0.0 collective-permute-done.1.refs_0_.refs_1_.refs_2_
  140.4 20.9 %shard_map.53.refs_3_ = f32[256,256]{1,0:T(8,128)S(1)} custom-call(s32[2]{0:T(128)S(1)} %pad_add_fusion.at, bf16[128,32768]{1,0:T(8,128)(2,1)} %src.17, bf16[128,32768]{1,0:T(8,128)(2,1)} %get-tuple-element.30.applied, f32[1,32768]{1,0:T(1,128)S(1)} %bitcast.4, bf16[128,12288]{1,0:T(8,128)(2,1)} %collective-permute-done.1.refs_0_.refs_1_.refs_2_, ...), custom_call_target="tpu_custom_call" | custom-call | flops 1610612736 | bytes 21102600 | tf_op jit(solution)/shard_map/pallas_call | solution.py:23
  161.2 0.0 collective-permute-done.refs_0_
  161.3 8.2 %shard_map.54 = (f32[128,256]{1,0:T(8,128)S(1)}, f32[128,256]{1,0:T(8,128)S(1)}) custom-call(s32[2]{0:T(128)S(1)} %pad_add_fusion.at, bf16[128,32768]{1,0:T(8,128)(2,1)} %src.17, bf16[128,32768]{1,0:T(8,128)(2,1)} %get-tuple-element.30.applied, f32[1,32768]{1,0:T(1,128)S(1)} %bitcast.5, bf16[128,4096]{1,0:T(8,128)(2,1)S(1)} %collective-permute-done.refs_0_, ...), custom_call_target="tpu_custom_call" | custom-call | flops 536870912 | bytes 24510472 | tf_op jit(solution)/shard_map/pallas_call | solution.py:23
  169.5 0.1 collective-permute-start.3
  169.6 1.0 shard_map.66
  170.6 2.1 collective-permute-start.7
  172.6 0.9 shard_map.68
  173.6 0.9 shard_map.70
  174.5 4.5 %collective-permute-done.3.refs_0_ = f32[128,128]{1,0:T(8,128)S(1)} collective-permute-done((f32[128,128]{1,0:T(8,128)S(1)}, f32[128,128]{1,0:T(8,128)S(1)}, u32[]{:S(2)}, u32[]{:S(2)}) %collective-permute-start.3) | collective-permute-done | bytes 65568 | tf_op jit(solution)/shard_map/ppermute | solution.py:418
  179.0 2.0 collective-permute-start.8
  181.0 0.8 shard_map.55
  181.8 3.1 %shard_map.60 = (bf16[128,32768]{1,0:T(8,128)(2,1)}, f32[128,128]{1,0:T(8,128)S(1)}) custom-call(s32[2]{0:T(128)S(1)} %pad_add_fusion.at, bf16[128,256]{1,0:T(8,128)(2,1)S(1)} %get-tuple-element.33.coef, bf16[128,32768]{1,0:T(8,128)(2,1)} %src.17, bf16[128,32768]{1,0:T(8,128)(2,1)} %get-tuple-element.30.applied, ...), custom_call_target="tpu_custom_call" | custom-call | flops 268435456 | bytes 17367048 | tf_op jit(solution)/shard_map/pallas_call | solution.py:23
  184.9 11.5 %shard_map.61 = (bf16[128,32768]{1,0:T(8,128)(2,1)}, f32[128,128]{1,0:T(8,128)S(1)}) custom-call(s32[2]{0:T(128)S(1)} %pad_add_fusion.at, bf16[128,256]{1,0:T(8,128)(2,1)S(1)} %get-tuple-element.33.coef, bf16[128,32768]{1,0:T(8,128)(2,1)} %src.17, bf16[128,32768]{1,0:T(8,128)(2,1)} %get-tuple-element.30.applied, ...), custom_call_target="tpu_custom_call", output_to_operand_aliasing={{0}: (5, {})} | custom-call | flops 1610612736 | bytes 28442632 | tf_op jit(solution)/shard_map/pallas_call | solution.py:23
  196.4 3.1 %shard_map.56 = (f32[128,2048]{1,0:T(8,128)S(1)}, bf16[128,2048]{1,0:T(8,128)(2,1)S(1)}) custom-call(s32[2]{0:T(128)S(1)} %pad_add_fusion.at, bf16[128,256]{1,0:T(8,128)(2,1)S(1)} %get-tuple-element.33.coef, bf16[128,32768]{1,0:T(8,128)(2,1)} %src.17, bf16[128,32768]{1,0:T(8,128)(2,1)} %get-tuple-element.30.applied), custom_call_target="tpu_custom_call" | custom-call | bytes 16842760 | tf_op jit(solution)/shard_map/pallas_call | solution.py:23
  199.5 4.7 %shard_map.62 = (bf16[128,32768]{1,0:T(8,128)(2,1)}, f32[128,128]{1,0:T(8,128)S(1)}) custom-call(s32[2]{0:T(128)S(1)} %pad_add_fusion.at, bf16[128,256]{1,0:T(8,128)(2,1)S(1)} %get-tuple-element.33.coef, bf16[128,32768]{1,0:T(8,128)(2,1)} %src.17, bf16[128,32768]{1,0:T(8,128)(2,1)} %get-tuple-element.30.applied, ...), custom_call_target="tpu_custom_call", output_to_operand_aliasing={{0}: (5, {})} | custom-call | flops 536870912 | bytes 26345480 | tf_op jit(solution)/shard_map/pallas_call | solution.py:23
  204.3 0.0 collective-permute-done.6.refs_0_
  204.3 0.0 collective-permute-start.9
  204.3 4.9 %shard_map.63 = (bf16[128,32768]{1,0:T(8,128)(2,1)}, f32[128,128]{1,0:T(8,128)S(1)}) custom-call(s32[2]{0:T(128)S(1)} %pad_add_fusion.at, bf16[128,256]{1,0:T(8,128)(2,1)S(1)} %get-tuple-element.33.coef, bf16[128,32768]{1,0:T(8,128)(2,1)} %src.17, bf16[128,32768]{1,0:T(8,128)(2,1)} %get-tuple-element.30.applied, ...), custom_call_target="tpu_custom_call", output_to_operand_aliasing={{0}: (5, {})} | custom-call | flops 536870912 | bytes 26345480 | tf_op jit(solution)/shard_map/pallas_call | solution.py:23
  209.2 0.0 collective-permute-done.5.refs_0_
  209.2 4.9 %shard_map.64 = (bf16[128,32768]{1,0:T(8,128)(2,1)}, f32[128,128]{1,0:T(8,128)S(1)}) custom-call(s32[2]{0:T(128)S(1)} %pad_add_fusion.at, bf16[128,256]{1,0:T(8,128)(2,1)S(1)} %get-tuple-element.33.coef, bf16[128,32768]{1,0:T(8,128)(2,1)} %src.17, bf16[128,32768]{1,0:T(8,128)(2,1)} %get-tuple-element.30.applied, ...), custom_call_target="tpu_custom_call", output_to_operand_aliasing={{0}: (5, {})} | custom-call | flops 536870912 | bytes 26345480 | tf_op jit(solution)/shard_map/pallas_call | solution.py:23
  214.0 0.0 collective-permute-done.4.refs_0_
  214.1 4.9 %shard_map.65 = (bf16[128,32768]{1,0:T(8,128)(2,1)}, f32[128,128]{1,0:T(8,128)S(1)}) custom-call(s32[2]{0:T(128)S(1)} %pad_add_fusion.at, bf16[128,256]{1,0:T(8,128)(2,1)S(1)} %get-tuple-element.33.coef, bf16[128,32768]{1,0:T(8,128)(2,1)} %src.17, bf16[128,32768]{1,0:T(8,128)(2,1)} %get-tuple-element.30.applied, ...), custom_call_target="tpu_custom_call", output_to_operand_aliasing={{0}: (5, {})} | custom-call | flops 536870912 | bytes 26345480 | tf_op jit(solution)/shard_map/pallas_call | solution.py:23
  218.9 0.0 collective-permute-done.7.refs_0_
  218.9 1.0 shard_map.67
  219.9 0.0 collective-permute-done.8.refs_0_
  219.9 0.9 shard_map.69
  220.8 0.0 collective-permute-done.9.refs_0_
  220.8 1.0 shard_map.71
  (1 shorter events, 0.0 us)
Async XLA Ops:
  4.3 136.1 %collective-permute-start.1 = (bf16[128,12288]{1,0:T(8,128)(2,1)}, bf16[128,12288]{1,0:T(8,128)(2,1)}, u32[]{:S(2)}, u32[]{:S(2)}) collective-permute-start(bf16[128,12288]{1,0:T(8,128)(2,1)} %shard_map.51), channel_id=1, source_target_pairs={{0,1},{1,0},{2,3},{3,2},{4,5},{5,4},{6,7},{7,6},{8,9},{9,8},{10,11... | collective-permute-start | bytes 9437192 | tf_op jit(solution)/shard_map/ppermute | solution.py:400
  8.3 79.3 %collective-permute-start.2 = (bf16[128,2048]{1,0:T(8,128)(2,1)S(1)}, bf16[128,2048]{1,0:T(8,128)(2,1)S(1)}, u32[]{:S(2)}, u32[]{:S(2)}) collective-permute-start(bf16[128,2048]{1,0:T(8,128)(2,1)S(1)} %shard_map.52), channel_id=1, source_target_pairs={{0,1},{1,0},{2,3},{3,2},{4,5},{5,4},{6,7},{7,6},{8,9},{9,8},{10,11... | collective-permute-start | bytes 1572872 | tf_op jit(solution)/shard_map/ppermute | solution.py:400
  10.7 150.6 %collective-permute-start = (bf16[128,4096]{1,0:T(8,128)(2,1)}, bf16[128,4096]{1,0:T(8,128)(2,1)S(1)}, u32[]{:S(2)}, u32[]{:S(2)}) collective-permute-start(bf16[128,4096]{1,0:T(8,128)(2,1)} %shard_map.50), channel_id=1, source_target_pairs={{0,1},{1,0},{2,3},{3,2},{4,5},{5,4},{6,7},{7,6},{8,9},{9,8},{10,11... | collective-permute-start | bytes 3145736 | tf_op jit(solution)/shard_map/ppermute | solution.py:400
  14.9 74.8 %copy-start = (f32[32768]{0:T(1024)S(1)}, f32[32768]{0:T(1024)}, u32[]{:S(2)}) copy-start(f32[32768]{0:T(1024)} %param.3) | copy-start | bytes 393220
  15.0 189.3 %collective-permute-start.6 = (bf16[128,4096]{1,0:T(8,128)(2,1)}, bf16[128,4096]{1,0:T(8,128)(2,1)}, u32[]{:S(2)}, u32[]{:S(2)}) collective-permute-start(bf16[128,4096]{1,0:T(8,128)(2,1)} %shard_map.59), channel_id=1, source_target_pairs={{0,1},{1,0},{2,3},{3,2},{4,5},{5,4},{6,7},{7,6},{8,9},{9,8},{10,11... | collective-permute-start | bytes 3145736 | tf_op jit(solution)/shard_map/ppermute | solution.py:400
  17.3 191.8 %collective-permute-start.5 = (bf16[128,4096]{1,0:T(8,128)(2,1)}, bf16[128,4096]{1,0:T(8,128)(2,1)}, u32[]{:S(2)}, u32[]{:S(2)}) collective-permute-start(bf16[128,4096]{1,0:T(8,128)(2,1)} %shard_map.58), channel_id=1, source_target_pairs={{0,1},{1,0},{2,3},{3,2},{4,5},{5,4},{6,7},{7,6},{8,9},{9,8},{10,11... | collective-permute-start | bytes 3145736 | tf_op jit(solution)/shard_map/ppermute | solution.py:400
  87.7 126.4 %collective-permute-start.4 = (bf16[128,4096]{1,0:T(8,128)(2,1)S(1)}, bf16[128,4096]{1,0:T(8,128)(2,1)}, u32[]{:S(2)}, u32[]{:S(2)}) collective-permute-start(bf16[128,4096]{1,0:T(8,128)(2,1)S(1)} %shard_map.57), channel_id=1, source_target_pairs={{0,1},{1,0},{2,3},{3,2},{4,5},{5,4},{6,7},{7,6},{8,9},{9,8},{10,11... | collective-permute-start | bytes 3145736 | tf_op jit(solution)/shard_map/ppermute | solution.py:400
  169.5 9.5 %collective-permute-start.3 = (f32[128,128]{1,0:T(8,128)S(1)}, f32[128,128]{1,0:T(8,128)S(1)}, u32[]{:S(2)}, u32[]{:S(2)}) collective-permute-start(f32[128,128]{1,0:T(8,128)S(1)} %slice.3), channel_id=1, source_target_pairs={{0,1},{1,0},{2,3},{3,2},{4,5},{5,4},{6,7},{7,6},{8,9},{9,8},{10,11... | collective-permute-start | bytes 196616 | tf_op jit(solution)/shard_map/ppermute | solution.py:418
  170.6 48.4 %collective-permute-start.7 = (bf16[128,1024]{1,0:T(8,128)(2,1)S(1)}, bf16[128,1024]{1,0:T(8,128)(2,1)S(1)}, u32[]{:S(2)}, u32[]{:S(2)}) collective-permute-start(bf16[128,1024]{1,0:T(8,128)(2,1)S(1)} %shard_map.66), channel_id=1, source_target_pairs={{0,1},{1,0},{2,3},{3,2},{4,5},{5,4},{6,7},{7,6},{8,9},{9,8},{10,11... | collective-permute-start | bytes 786440 | tf_op jit(solution)/shard_map/ppermute | solution.py:400
  179.0 40.9 %collective-permute-start.8 = (bf16[128,512]{1,0:T(8,128)(2,1)S(1)}, bf16[128,512]{1,0:T(8,128)(2,1)S(1)}, u32[]{:S(2)}, u32[]{:S(2)}) collective-permute-start(bf16[128,512]{1,0:T(8,128)(2,1)S(1)} %shard_map.68), channel_id=1, source_target_pairs={{0,1},{1,0},{2,3},{3,2},{4,5},{5,4},{6,7},{7,6},{8,9},{9,8},{10,11... | collective-permute-start | bytes 393224 | tf_op jit(solution)/shard_map/ppermute | solution.py:400
  204.3 16.5 %collective-permute-start.9 = (bf16[128,512]{1,0:T(8,128)(2,1)S(1)}, bf16[128,512]{1,0:T(8,128)(2,1)S(1)}, u32[]{:S(2)}, u32[]{:S(2)}) collective-permute-start(bf16[128,512]{1,0:T(8,128)(2,1)S(1)} %shard_map.70), channel_id=1, source_target_pairs={{0,1},{1,0},{2,3},{3,2},{4,5},{5,4},{6,7},{7,6},{8,9},{9,8},{10,11... | collective-permute-start | bytes 393224 | tf_op jit(solution)/shard_map/ppermute | solution.py:400

commit v6 on v5

--- a/solution.py
+++ b/solution.py
@@ -233,55 +233,92 @@
     )
 
 
-def rest_body(n, first, at, coef, own_ref, applied, *refs):
+def rest_body(n, first, width, size, count, ratio, share, q0, coef, own_ref, applied, *refs):
     refs = list(refs)
     rems, refs = refs[: n - 1], refs[n - 1 :]
     if not first:
         before, refs = refs[1], refs[2:]
-    out, gram, every = refs
+    out, gram, mine, held, theirs, every, got, sent = refs
     own = own_ref.shape[0]
-    every[:own, :] = own_ref[...]
-    for j in range(n - 1):
-        every[(j + 1) * own : (j + 2) * own, :] = rems[j][...]
-    mixed = jnp.dot(coef[...], every[...], preferred_element_type=F32)
-    out[...] = (applied[...].astype(F32) - mixed).astype(BF16)
-
-    @pl.when(pl.program_id(0) == 0)
-    def _():
-        gram[...] = jnp.zeros_like(gram) if first else before[...]
-
-    gram[...] += rowdot(own_ref[...], every[own:, :])
-
-
-def rest(at, coef, orbitals, applied, rems, carry, q0, width, size, ratio):
+    me = lax.axis_index("band")
+
+    def place(i):
+        return pl.ds(pl.multiple_of(lax.rem((me * share - 1) * ratio + q0 + i + count, count) * size, size), size)
+
+    def arriving(i):
+        here = pl.ds(pl.multiple_of(i * size, size), size)
+        copies = [
+            pltpu.make_async_copy(own_ref.at[:, place(i)], mine.at[i], got.at[i, n - 1]),
+            pltpu.make_async_copy(applied.at[:, place(i)], held.at[i], got.at[i, n]),
+        ]
+        for j in range(n - 1):
+            rows = pl.ds(j * own, own)
+            copies.append(pltpu.make_async_copy(rems[j].at[:, here], theirs.at[i, rows], got.at[i, j]))
+        return copies
+
+    def leaving(i):
+        return pltpu.make_async_copy(held.at[i], out.at[:, place(i)], sent.at[i])
+
+    def ask(i, _):
+        for copy in arriving(i):
+            copy.start()
+        return 0
+
+    def work(i, _):
+        for copy in arriving(i):
+            copy.wait()
+        every[:own, :] = mine[i]
+        every[own:, :] = theirs[i]
+        mixed = jnp.dot(coef[...], every[...], preferred_element_type=F32)
+        held[i] = (held[i].astype(F32) - mixed).astype(BF16)
+        leaving(i).start()
+        gram[...] += rowdot(mine[i], theirs[i])
+        return 0
+
+    def end(i, _):
+        leaving(i).wait()
+        return 0
+
+    lax.fori_loop(0, width, ask, 0)
+    gram[...] = jnp.zeros_like(gram) if first else before[...]
+    lax.fori_loop(0, width, work, 0)
+    lax.fori_loop(0, width, end, 0)
+
+
+def rest(share, coef, orbitals, applied, rems, carry, q0, width, size, ratio):
     own, grid, n = orbitals.shape[0], orbitals.shape[1], len(rems) + 1
-    total, count = n * own, grid // size
-
-    def plane():
-        return pl.BlockSpec((own, size), lambda i, at: (0, lax.rem((at[0] - 1) * ratio + q0 + i + count, count)))
+    total = n * own
+    free = pl.BlockSpec(memory_space=ANY)
 
     def fixed(shape):
-        return pl.BlockSpec(shape, lambda i, at: (0, 0))
+        return pl.BlockSpec(shape, lambda i: (0, 0))
 
     first = carry is None
-    args = [at, coef, orbitals, applied, *rems]
-    specs = [fixed((own, total)), plane(), plane()]
-    specs += [pl.BlockSpec((own, size), lambda i, at: (0, i))] * (n - 1)
+    args = [coef, orbitals, applied, *rems]
+    specs = [fixed((own, total))] + [free] * (n + 1)
     aliases = {}
     if not first:
         aliases = {len(args): 0}
         args += list(carry)
-        specs += [pl.BlockSpec(memory_space=ANY), fixed((own, total - own))]
-    return call(
-        functools.partial(rest_body, n, first),
-        (width,),
+        specs += [free, fixed((own, total - own))]
+    return call(
+        functools.partial(rest_body, n, first, width, size, grid // size, ratio, share, q0),
+        (1,),
         specs,
-        [plane(), fixed((own, total - own))],
+        [free, fixed((own, total - own))],
         [jax.ShapeDtypeStruct((own, grid), BF16), jax.ShapeDtypeStruct((own, total - own), F32)],
         tuple(args),
-        scratch=[pltpu.VMEM((total, size), BF16)],
+        scratch=[
+            pltpu.VMEM((width, own, size), BF16),
+            pltpu.VMEM((width, own, size), BF16),
+            pltpu.VMEM((width, total - own, size), BF16),
+            pltpu.VMEM((total, size), BF16),
+            pltpu.SemaphoreType.DMA((width, n + 1)),
+            pltpu.SemaphoreType.DMA((width,)),
+        ],
         aliases=aliases,
         flops=4 * own * total * size * width,
+        scalars=0,
     )
 
 
@@ -423,7 +460,7 @@
     base, copied = ready(at, coef, orbitals, applied, low, side * PARTS - low, size, PARTS)
     carry = None
     for q0, width, ratio, rems in chunks[: -len(narrow)]:
-        carry = rest(at, coef, orbitals, applied, rems, carry, q0, width, grid // (side * ratio), ratio)
+        carry = rest(share, coef, orbitals, applied, rems, carry, q0, width, grid // (side * ratio), ratio)
     for q0, width, _, rems in narrow:
         last = q0 + width == side * PARTS
         carry = finish(share, coef, base, copied, sums, rems, carry, q0, width, q0 - low, size, PARTS, last)

time: 223 us -> 209 us (0.937)
  Pallas kernels: 136 us -> 123 us
    pallas_call x23, Pallas kernels: 136 us -> 123 us  [call(): pl.pallas_call(kernel, out_shape=out_shape, grid_spec=pltpu.PrefetchScala...]
  transfers between devices with their start and end apart: 10 -> 10, of which waited for: 2 -> 2; matrix products, arithmetic and copies ran while one was open for 0% -> 0% of each run, Pallas kernels for 59% -> 57%
where the time goes in v6:
time: 209 us
  Pallas kernels  123 us (59%)
  waiting for transfers between devices  71.6 us (34%)
  starting transfers between devices  13.6 us (7%)
    pallas_call x23, Pallas kernels, call(): pl.pallas_call(kernel, out_shape=out_shape, grid_spec=pltpu.PrefetchScala...  123 us
    ppermute x9, waiting for transfers between devices, sent(): lax.ppermute(chunk, 'band', [(k, (k - j) % n) for k in range(n)])  67.1 us
    ppermute x9, starting transfers between devices, sent(): lax.ppermute(chunk, 'band', [(k, (k - j) % n) for k in range(n)])  13.5 us
    ppermute x1, waiting for transfers between devices, shards(): got.append(lax.ppermute(others[j - 1][:, own:], 'band', perm))  4.48 us
  transfers between devices with their start and end apart: 10, of which 2 were waited for; matrix products, arithmetic and copies ran while one was open for 0% of the time, Pallas kernels for 57%

profile of v6, /device:TPU:0, one launch (start us, length us, event | category | flops | bytes accessed | tf_op | source)
XLA Modules:
  0.0 208.7 jit_solution(17031451396237933003)
XLA Ops:
  0.6 3.6 %shard_map.51 = bf16[128,12288]{1,0:T(8,128)(2,1)} custom-call(bf16[128,32768]{1,0:T(8,128)(2,1)} %src.17), custom_call_target="tpu_custom_call" | custom-call | bytes 8388608 | tf_op jit(solution)/shard_map/pallas_call | solution.py:23
  4.3 3.0 %collective-permute-start.1 = (bf16[128,12288]{1,0:T(8,128)(2,1)}, bf16[128,12288]{1,0:T(8,128)(2,1)}, u32[]{:S(2)}, u32[]{:S(2)}) collective-permute-start(bf16[128,12288]{1,0:T(8,128)(2,1)} %shard_map.51), channel_id=1, source_target_pairs={{0,1},{1,0},{2,3},{3,2},{4,5},{5,4},{6,7},{7,6},{8,9},{9,8},{10,11... | collective-permute-start | bytes 9437192 | tf_op jit(solution)/shard_map/ppermute | solution.py:437
  7.3 1.0 shard_map.52
  8.3 0.1 collective-permute-start.2
  8.4 2.2 %shard_map.50 = bf16[128,4096]{1,0:T(8,128)(2,1)} custom-call(bf16[128,32768]{1,0:T(8,128)(2,1)} %src.17), custom_call_target="tpu_custom_call" | custom-call | bytes 8388608 | tf_op jit(solution)/shard_map/pallas_call | solution.py:23
  10.7 2.1 collective-permute-start
  12.7 2.2 %shard_map.59 = bf16[128,4096]{1,0:T(8,128)(2,1)} custom-call(bf16[128,32768]{1,0:T(8,128)(2,1)} %src.17), custom_call_target="tpu_custom_call" | custom-call | bytes 8388608 | tf_op jit(solution)/shard_map/pallas_call | solution.py:23
  14.9 0.0 copy-start
  15.0 0.1 collective-permute-start.6
  15.1 2.3 %shard_map.58 = bf16[128,4096]{1,0:T(8,128)(2,1)} custom-call(bf16[128,32768]{1,0:T(8,128)(2,1)} %src.17), custom_call_target="tpu_custom_call" | custom-call | bytes 8388608 | tf_op jit(solution)/shard_map/pallas_call | solution.py:23
  17.3 2.1 collective-permute-start.5
  19.4 1.2 shard_map.57
  20.6 67.1 %collective-permute-done.2.refs_1_.refs_2_.refs_0_ = bf16[128,2048]{1,0:T(8,128)(2,1)S(1)} collective-permute-done((bf16[128,2048]{1,0:T(8,128)(2,1)S(1)}, bf16[128,2048]{1,0:T(8,128)(2,1)S(1)}, u32[]{:S(2)}, u32[]{:S(2)}) %collective-permute-start.2) | collective-permute-done | bytes 524320 | tf_op jit(solution)/shard_map/ppermute | solution.py:437
  87.7 2.0 collective-permute-start.4
  89.7 0.1 pad_add_fusion.at
  89.8 0.0 copy-done
  89.8 50.6 %shard_map.49 = (bf16[128,32768]{1,0:T(8,128)(2,1)}, f32[256,128]{1,0:T(8,128)S(1)}) custom-call(s32[2]{0:T(128)S(1)} %pad_add_fusion.at, bf16[128,32768]{1,0:T(8,128)(2,1)} %src.17, bf16[128,32768]{1,0:T(8,128)(2,1)} %src.17, bf16[128,32768]{1,0:T(8,128)(2,1)} %src.17, f32[1,32768]{1,0:T(1,128)S(1)} %bitcast.3), custom_call_target="tpu_custom_call" | custom-call | flops 2147483648 | bytes 25296904 | tf_op jit(solution)/shard_map/pallas_call | solution.py:23
  140.4 0.0 collective-permute-done.1.refs_0_.refs_1_.refs_2_
  140.4 20.9 %shard_map.53.refs_3_ = f32[256,256]{1,0:T(8,128)S(1)} custom-call(s32[2]{0:T(128)S(1)} %pad_add_fusion.at, bf16[128,32768]{1,0:T(8,128)(2,1)} %src.17, bf16[128,32768]{1,0:T(8,128)(2,1)} %get-tuple-element.30.applied, f32[1,32768]{1,0:T(1,128)S(1)} %bitcast.4, bf16[128,12288]{1,0:T(8,128)(2,1)} %collective-permute-done.1.refs_0_.refs_1_.refs_2_, ...), custom_call_target="tpu_custom_call" | custom-call | flops 1610612736 | bytes 21102600 | tf_op jit(solution)/shard_map/pallas_call | solution.py:23
  161.2 0.0 collective-permute-done.refs_0_
  161.3 8.2 %shard_map.54 = (f32[128,256]{1,0:T(8,128)S(1)}, f32[128,256]{1,0:T(8,128)S(1)}) custom-call(s32[2]{0:T(128)S(1)} %pad_add_fusion.at, bf16[128,32768]{1,0:T(8,128)(2,1)} %src.17, bf16[128,32768]{1,0:T(8,128)(2,1)} %get-tuple-element.30.applied, f32[1,32768]{1,0:T(1,128)S(1)} %bitcast.5, bf16[128,4096]{1,0:T(8,128)(2,1)S(1)} %collective-permute-done.refs_0_, ...), custom_call_target="tpu_custom_call" | custom-call | flops 536870912 | bytes 24510472 | tf_op jit(solution)/shard_map/pallas_call | solution.py:23
  169.5 0.1 collective-permute-start.3
  169.6 1.0 shard_map.66
  170.6 2.1 collective-permute-start.7
  172.6 0.9 shard_map.68
  173.6 0.9 shard_map.70
  174.5 4.5 %collective-permute-done.3.refs_0_ = f32[128,128]{1,0:T(8,128)S(1)} collective-permute-done((f32[128,128]{1,0:T(8,128)S(1)}, f32[128,128]{1,0:T(8,128)S(1)}, u32[]{:S(2)}, u32[]{:S(2)}) %collective-permute-start.3) | collective-permute-done | bytes 65568 | tf_op jit(solution)/shard_map/ppermute | solution.py:455
  179.0 2.0 collective-permute-start.8
  181.0 0.8 shard_map.55
  181.8 2.4 %shard_map.60 = (bf16[128,32768]{1,0:T(8,128)(2,1)}, f32[128,128]{1,0:T(8,128)S(1)}) custom-call(bf16[128,256]{1,0:T(8,128)(2,1)S(1)} %get-tuple-element.33.coef, bf16[128,32768]{1,0:T(8,128)(2,1)} %src.17, bf16[128,32768]{1,0:T(8,128)(2,1)} %get-tuple-element.30.applied, bf16[128,2048]{1,0:T(8,128)(2,1)S(1)} %collective-permute-done.2.refs_1_.refs_2_.refs_0_), custom_call_target="tpu_custom_call" | custom-call | flops 268435456 | bytes 17367040 | tf_op jit(solution)/shard_map/pallas_call | solution.py:23
  184.1 5.9 %shard_map.61 = (bf16[128,32768]{1,0:T(8,128)(2,1)}, f32[128,128]{1,0:T(8,128)S(1)}) custom-call(bf16[128,256]{1,0:T(8,128)(2,1)S(1)} %get-tuple-element.33.coef, bf16[128,32768]{1,0:T(8,128)(2,1)} %src.17, bf16[128,32768]{1,0:T(8,128)(2,1)} %get-tuple-element.30.applied, ...), custom_call_target="tpu_custom_call", output_to_operand_aliasing={{0}: (4, {})} | custom-call | flops 1610612736 | bytes 28442624 | tf_op jit(solution)/shard_map/pallas_call | solution.py:23
  190.1 3.1 %shard_map.56 = (f32[128,2048]{1,0:T(8,128)S(1)}, bf16[128,2048]{1,0:T(8,128)(2,1)S(1)}) custom-call(s32[2]{0:T(128)S(1)} %pad_add_fusion.at, bf16[128,256]{1,0:T(8,128)(2,1)S(1)} %get-tuple-element.33.coef, bf16[128,32768]{1,0:T(8,128)(2,1)} %src.17, bf16[128,32768]{1,0:T(8,128)(2,1)} %get-tuple-element.30.applied), custom_call_target="tpu_custom_call" | custom-call | bytes 16842760 | tf_op jit(solution)/shard_map/pallas_call | solution.py:23
  193.2 3.1 %shard_map.62 = (bf16[128,32768]{1,0:T(8,128)(2,1)}, f32[128,128]{1,0:T(8,128)S(1)}) custom-call(bf16[128,256]{1,0:T(8,128)(2,1)S(1)} %get-tuple-element.33.coef, bf16[128,32768]{1,0:T(8,128)(2,1)} %src.17, bf16[128,32768]{1,0:T(8,128)(2,1)} %get-tuple-element.30.applied, ...), custom_call_target="tpu_custom_call", output_to_operand_aliasing={{0}: (4, {})} | custom-call | flops 536870912 | bytes 26345472 | tf_op jit(solution)/shard_map/pallas_call | solution.py:23
  196.3 0.0 collective-permute-done.6.refs_0_
  196.3 0.1 collective-permute-start.9
  196.4 3.1 %shard_map.63 = (bf16[128,32768]{1,0:T(8,128)(2,1)}, f32[128,128]{1,0:T(8,128)S(1)}) custom-call(bf16[128,256]{1,0:T(8,128)(2,1)S(1)} %get-tuple-element.33.coef, bf16[128,32768]{1,0:T(8,128)(2,1)} %src.17, bf16[128,32768]{1,0:T(8,128)(2,1)} %get-tuple-element.30.applied, ...), custom_call_target="tpu_custom_call", output_to_operand_aliasing={{0}: (4, {})} | custom-call | flops 536870912 | bytes 26345472 | tf_op jit(solution)/shard_map/pallas_call | solution.py:23
  199.6 0.0 collective-permute-done.5.refs_0_
  199.6 3.2 %shard_map.64 = (bf16[128,32768]{1,0:T(8,128)(2,1)}, f32[128,128]{1,0:T(8,128)S(1)}) custom-call(bf16[128,256]{1,0:T(8,128)(2,1)S(1)} %get-tuple-element.33.coef, bf16[128,32768]{1,0:T(8,128)(2,1)} %src.17, bf16[128,32768]{1,0:T(8,128)(2,1)} %get-tuple-element.30.applied, ...), custom_call_target="tpu_custom_call", output_to_operand_aliasing={{0}: (4, {})} | custom-call | flops 536870912 | bytes 26345472 | tf_op jit(solution)/shard_map/pallas_call | solution.py:23
  202.7 0.0 collective-permute-done.4.refs_0_
  202.7 3.1 %shard_map.65 = (bf16[128,32768]{1,0:T(8,128)(2,1)}, f32[128,128]{1,0:T(8,128)S(1)}) custom-call(bf16[128,256]{1,0:T(8,128)(2,1)S(1)} %get-tuple-element.33.coef, bf16[128,32768]{1,0:T(8,128)(2,1)} %src.17, bf16[128,32768]{1,0:T(8,128)(2,1)} %get-tuple-element.30.applied, ...), custom_call_target="tpu_custom_call", output_to_operand_aliasing={{0}: (4, {})} | custom-call | flops 536870912 | bytes 26345472 | tf_op jit(solution)/shard_map/pallas_call | solution.py:23
  205.9 0.0 collective-permute-done.7.refs_0_
  205.9 0.9 shard_map.67
  206.9 0.0 collective-permute-done.8.refs_0_
  206.9 0.9 shard_map.69
  207.7 0.0 collective-permute-done.9.refs_0_
  207.7 1.0 shard_map.71
  (1 shorter events, 0.0 us)
Async XLA Ops:
  4.3 136.1 %collective-permute-start.1 = (bf16[128,12288]{1,0:T(8,128)(2,1)}, bf16[128,12288]{1,0:T(8,128)(2,1)}, u32[]{:S(2)}, u32[]{:S(2)}) collective-permute-start(bf16[128,12288]{1,0:T(8,128)(2,1)} %shard_map.51), channel_id=1, source_target_pairs={{0,1},{1,0},{2,3},{3,2},{4,5},{5,4},{6,7},{7,6},{8,9},{9,8},{10,11... | collective-permute-start | bytes 9437192 | tf_op jit(solution)/shard_map/ppermute | solution.py:437
  8.3 79.3 %collective-permute-start.2 = (bf16[128,2048]{1,0:T(8,128)(2,1)S(1)}, bf16[128,2048]{1,0:T(8,128)(2,1)S(1)}, u32[]{:S(2)}, u32[]{:S(2)}) collective-permute-start(bf16[128,2048]{1,0:T(8,128)(2,1)S(1)} %shard_map.52), channel_id=1, source_target_pairs={{0,1},{1,0},{2,3},{3,2},{4,5},{5,4},{6,7},{7,6},{8,9},{9,8},{10,11... | collective-permute-start | bytes 1572872 | tf_op jit(solution)/shard_map/ppermute | solution.py:437
  10.7 150.6 %collective-permute-start = (bf16[128,4096]{1,0:T(8,128)(2,1)}, bf16[128,4096]{1,0:T(8,128)(2,1)S(1)}, u32[]{:S(2)}, u32[]{:S(2)}) collective-permute-start(bf16[128,4096]{1,0:T(8,128)(2,1)} %shard_map.50), channel_id=1, source_target_pairs={{0,1},{1,0},{2,3},{3,2},{4,5},{5,4},{6,7},{7,6},{8,9},{9,8},{10,11... | collective-permute-start | bytes 3145736 | tf_op jit(solution)/shard_map/ppermute | solution.py:437
  14.9 74.8 %copy-start = (f32[32768]{0:T(1024)S(1)}, f32[32768]{0:T(1024)}, u32[]{:S(2)}) copy-start(f32[32768]{0:T(1024)} %param.3) | copy-start | bytes 393220
  15.0 181.3 %collective-permute-start.6 = (bf16[128,4096]{1,0:T(8,128)(2,1)}, bf16[128,4096]{1,0:T(8,128)(2,1)}, u32[]{:S(2)}, u32[]{:S(2)}) collective-permute-start(bf16[128,4096]{1,0:T(8,128)(2,1)} %shard_map.59), channel_id=1, source_target_pairs={{0,1},{1,0},{2,3},{3,2},{4,5},{5,4},{6,7},{7,6},{8,9},{9,8},{10,11... | collective-permute-start | bytes 3145736 | tf_op jit(solution)/shard_map/ppermute | solution.py:437
  17.3 182.2 %collective-permute-start.5 = (bf16[128,4096]{1,0:T(8,128)(2,1)}, bf16[128,4096]{1,0:T(8,128)(2,1)}, u32[]{:S(2)}, u32[]{:S(2)}) collective-permute-start(bf16[128,4096]{1,0:T(8,128)(2,1)} %shard_map.58), channel_id=1, source_target_pairs={{0,1},{1,0},{2,3},{3,2},{4,5},{5,4},{6,7},{7,6},{8,9},{9,8},{10,11... | collective-permute-start | bytes 3145736 | tf_op jit(solution)/shard_map/ppermute | solution.py:437
  87.7 115.0 %collective-permute-start.4 = (bf16[128,4096]{1,0:T(8,128)(2,1)S(1)}, bf16[128,4096]{1,0:T(8,128)(2,1)}, u32[]{:S(2)}, u32[]{:S(2)}) collective-permute-start(bf16[128,4096]{1,0:T(8,128)(2,1)S(1)} %shard_map.57), channel_id=1, source_target_pairs={{0,1},{1,0},{2,3},{3,2},{4,5},{5,4},{6,7},{7,6},{8,9},{9,8},{10,11... | collective-permute-start | bytes 3145736 | tf_op jit(solution)/shard_map/ppermute | solution.py:437
  169.5 9.5 %collective-permute-start.3 = (f32[128,128]{1,0:T(8,128)S(1)}, f32[128,128]{1,0:T(8,128)S(1)}, u32[]{:S(2)}, u32[]{:S(2)}) collective-permute-start(f32[128,128]{1,0:T(8,128)S(1)} %slice.3), channel_id=1, source_target_pairs={{0,1},{1,0},{2,3},{3,2},{4,5},{5,4},{6,7},{7,6},{8,9},{9,8},{10,11... | collective-permute-start | bytes 196616 | tf_op jit(solution)/shard_map/ppermute | solution.py:455
  170.6 35.3 %collective-permute-start.7 = (bf16[128,1024]{1,0:T(8,128)(2,1)S(1)}, bf16[128,1024]{1,0:T(8,128)(2,1)S(1)}, u32[]{:S(2)}, u32[]{:S(2)}) collective-permute-start(bf16[128,1024]{1,0:T(8,128)(2,1)S(1)} %shard_map.66), channel_id=1, source_target_pairs={{0,1},{1,0},{2,3},{3,2},{4,5},{5,4},{6,7},{7,6},{8,9},{9,8},{10,11... | collective-permute-start | bytes 786440 | tf_op jit(solution)/shard_map/ppermute | solution.py:437
  179.0 27.9 %collective-permute-start.8 = (bf16[128,512]{1,0:T(8,128)(2,1)S(1)}, bf16[128,512]{1,0:T(8,128)(2,1)S(1)}, u32[]{:S(2)}, u32[]{:S(2)}) collective-permute-start(bf16[128,512]{1,0:T(8,128)(2,1)S(1)} %shard_map.68), channel_id=1, source_target_pairs={{0,1},{1,0},{2,3},{3,2},{4,5},{5,4},{6,7},{7,6},{8,9},{9,8},{10,11... | collective-permute-start | bytes 393224 | tf_op jit(solution)/shard_map/ppermute | solution.py:437
  196.3 11.4 %collective-permute-start.9 = (bf16[128,512]{1,0:T(8,128)(2,1)S(1)}, bf16[128,512]{1,0:T(8,128)(2,1)S(1)}, u32[]{:S(2)}, u32[]{:S(2)}) collective-permute-start(bf16[128,512]{1,0:T(8,128)(2,1)S(1)} %shard_map.70), channel_id=1, source_target_pairs={{0,1},{1,0},{2,3},{3,2},{4,5},{5,4},{6,7},{7,6},{8,9},{9,8},{10,11... | collective-permute-start | bytes 393224 | tf_op jit(solution)/shard_map/ppermute | solution.py:437

commit v7 on v6

--- a/solution.py
+++ b/solution.py
@@ -198,7 +198,7 @@
     )
 
 
-def coef_body(n, at, sums, mine, *refs):
+def coef_body(n, sums, mine, *refs):
     got, (projected, coef, work) = refs[: n - 1], refs[n - 1 :]
     own = mine.shape[0]
     other = mine[:, own:]
@@ -211,15 +211,15 @@
     diagonal = jnp.sum(jnp.where(same, gram, 0.0), axis=1, keepdims=True)
     value = work[...]
     coef[...] = (value / diagonal).astype(BF16)
-    projected[...] = pltpu.roll(value, at[0] * own, 1)
-
-
-def coefficients(at, sums, mine, got):
+    projected[...] = pltpu.roll(value, lax.axis_index("band") * own, 1)
+
+
+def coefficients(sums, mine, got):
     own, total = mine.shape
     n = total // own
 
     def whole(x):
-        return pl.BlockSpec(x.shape, lambda i, at: (0, 0))
+        return pl.BlockSpec(x.shape, lambda i: (0, 0))
 
     shape = jax.ShapeDtypeStruct((own, total), F32)
     return call(
@@ -228,8 +228,9 @@
         [whole(sums), whole(mine)] + [whole(g) for g in got],
         [whole(shape), whole(shape)],
         [shape, jax.ShapeDtypeStruct((own, total), BF16)],
-        (at, sums, mine, *got),
+        (sums, mine, *got),
         scratch=[pltpu.VMEM((own, total), F32)],
+        scalars=0,
     )
 
 
@@ -322,24 +323,36 @@
     )
 
 
-def ready_body(at, coef, own_ref, applied, base, copied):
-    own, size = own_ref.shape
-    columns = pl.ds(pl.multiple_of(pl.program_id(0) * size, size), size)
-    copied[:, columns] = own_ref[...]
-    base[:, columns] = applied[...].astype(F32) - jnp.dot(coef[:, :own], own_ref[...], preferred_element_type=F32)
-
-
-def ready(at, coef, orbitals, applied, q0, width, size, ratio):
+def ready_body(q0, width, size, count, ratio, share, coef, own_ref, applied, base, copied, held, got):
+    own, me = copied.shape[0], lax.axis_index("band")
+    copies = []
+    for i in range(width):
+        place = pl.multiple_of(lax.rem((me * share - 1) * ratio + q0 + i + count, count) * size, size)
+        here, there = pl.ds(i * size, size), pl.ds(place, size)
+        copies.append(pltpu.make_async_copy(own_ref.at[:, there], copied.at[:, here], got.at[2 * i]))
+        copies.append(pltpu.make_async_copy(applied.at[:, there], held.at[:, here], got.at[2 * i + 1]))
+    for copy in copies:
+        copy.start()
+    for i in range(width):
+        copies[2 * i].wait()
+        copies[2 * i + 1].wait()
+        here = slice(i * size, (i + 1) * size)
+        mixed = jnp.dot(coef[:, :own], copied[:, here], preferred_element_type=F32)
+        base[:, here] = held[:, here].astype(F32) - mixed
+
+
+def ready(share, coef, orbitals, applied, q0, width, size, ratio):
     own, grid = orbitals.shape
-    count = grid // size
-    plane = pl.BlockSpec((own, size), lambda i, at: (0, lax.rem((at[0] - 1) * ratio + q0 + i + count, count)))
-    return call(
-        ready_body,
-        (width,),
-        [pl.BlockSpec(coef.shape, lambda i, at: (0, 0)), plane, plane],
+    free = pl.BlockSpec(memory_space=ANY)
+    return call(
+        functools.partial(ready_body, q0, width, size, grid // size, ratio, share),
+        (1,),
+        [pl.BlockSpec(coef.shape, lambda i: (0, 0)), free, free],
         [pl.BlockSpec(memory_space=pltpu.VMEM)] * 2,
         [pltpu.VMEM((own, width * size), F32), pltpu.VMEM((own, width * size), BF16)],
-        (at, coef, orbitals, applied),
+        (coef, orbitals, applied),
+        scratch=[pltpu.VMEM((own, width * size), BF16), pltpu.SemaphoreType.DMA((2 * width,))],
+        scalars=0,
     )
 
 
@@ -454,10 +467,10 @@
         perm = [(k, (k - j) % n) for k in range(n)]
         got.append(lax.ppermute(others[j - 1][:, own:], "band", perm))
     chunks += [(*block, sent(*block)) for block in late]
-    projected, coef = coefficients(at[1:], sums, mine, got)
+    projected, coef = coefficients(sums, mine, got)
     narrow = [chunk for chunk in chunks if chunk[2] == PARTS and chunk[1] <= NARROW]
     size, low = grid // (side * PARTS), narrow[0][0]
-    base, copied = ready(at, coef, orbitals, applied, low, side * PARTS - low, size, PARTS)
+    base, copied = ready(share, coef, orbitals, applied, low, side * PARTS - low, size, PARTS)
     carry = None
     for q0, width, ratio, rems in chunks[: -len(narrow)]:
         carry = rest(share, coef, orbitals, applied, rems, carry, q0, width, grid // (side * ratio), ratio)

time: 209 us -> 208 us (level)
  transfers between devices with their start and end apart: 10 -> 10, of which waited for: 2 -> 2; matrix products, arithmetic and copies ran while one was open for 0% -> 0% of each run, Pallas kernels for 57% -> 56%
where the time goes in v7:
time: 208 us; the launch traced here: 207 us
  Pallas kernels  121 us (58%)
  waiting for transfers between devices  71.6 us (34%)
  starting transfers between devices  13.6 us (7%)
    pallas_call x23, Pallas kernels, call(): pl.pallas_call(kernel, out_shape=out_shape, grid_spec=pltpu.PrefetchScala...  121 us
    ppermute x9, waiting for transfers between devices, sent(): lax.ppermute(chunk, 'band', [(k, (k - j) % n) for k in range(n)])  67.1 us
    ppermute x9, starting transfers between devices, sent(): lax.ppermute(chunk, 'band', [(k, (k - j) % n) for k in range(n)])  13.5 us
    ppermute x1, waiting for transfers between devices, shards(): got.append(lax.ppermute(others[j - 1][:, own:], 'band', perm))  4.48 us
  transfers between devices with their start and end apart: 10, of which 2 were waited for; matrix products, arithmetic and copies ran while one was open for 0% of the time, Pallas kernels for 56%

profile of v7, /device:TPU:0, one launch (start us, length us, event | category | flops | bytes accessed | tf_op | source)
XLA Modules:
  0.0 207.4 jit_solution(83279013260702392)
XLA Ops:
  0.6 3.6 %shard_map.51 = bf16[128,12288]{1,0:T(8,128)(2,1)} custom-call(bf16[128,32768]{1,0:T(8,128)(2,1)} %src.17), custom_call_target="tpu_custom_call" | custom-call | bytes 8388608 | tf_op jit(solution)/shard_map/pallas_call | solution.py:23
  4.3 3.0 %collective-permute-start.1 = (bf16[128,12288]{1,0:T(8,128)(2,1)}, bf16[128,12288]{1,0:T(8,128)(2,1)}, u32[]{:S(2)}, u32[]{:S(2)}) collective-permute-start(bf16[128,12288]{1,0:T(8,128)(2,1)} %shard_map.51), channel_id=1, source_target_pairs={{0,1},{1,0},{2,3},{3,2},{4,5},{5,4},{6,7},{7,6},{8,9},{9,8},{10,11... | collective-permute-start | bytes 9437192 | tf_op jit(solution)/shard_map/ppermute | solution.py:450
  7.3 1.0 shard_map.52
  8.3 0.1 collective-permute-start.2
  8.4 2.2 %shard_map.50 = bf16[128,4096]{1,0:T(8,128)(2,1)} custom-call(bf16[128,32768]{1,0:T(8,128)(2,1)} %src.17), custom_call_target="tpu_custom_call" | custom-call | bytes 8388608 | tf_op jit(solution)/shard_map/pallas_call | solution.py:23
  10.7 2.1 collective-permute-start
  12.7 2.2 %shard_map.59 = bf16[128,4096]{1,0:T(8,128)(2,1)} custom-call(bf16[128,32768]{1,0:T(8,128)(2,1)} %src.17), custom_call_target="tpu_custom_call" | custom-call | bytes 8388608 | tf_op jit(solution)/shard_map/pallas_call | solution.py:23
  14.9 0.0 copy-start
  15.0 0.1 collective-permute-start.6
  15.1 2.3 %shard_map.58 = bf16[128,4096]{1,0:T(8,128)(2,1)} custom-call(bf16[128,32768]{1,0:T(8,128)(2,1)} %src.17), custom_call_target="tpu_custom_call" | custom-call | bytes 8388608 | tf_op jit(solution)/shard_map/pallas_call | solution.py:23
  17.3 2.1 collective-permute-start.5
  19.4 1.2 shard_map.57
  20.6 67.1 %collective-permute-done.2.refs_1_.refs_2_.refs_0_ = bf16[128,2048]{1,0:T(8,128)(2,1)S(1)} collective-permute-done((bf16[128,2048]{1,0:T(8,128)(2,1)S(1)}, bf16[128,2048]{1,0:T(8,128)(2,1)S(1)}, u32[]{:S(2)}, u32[]{:S(2)}) %collective-permute-start.2) | collective-permute-done | bytes 524320 | tf_op jit(solution)/shard_map/ppermute | solution.py:450
  87.7 2.0 collective-permute-start.4
  89.7 0.1 pad_add_fusion.at
  89.8 0.0 copy-done
  89.8 50.6 %shard_map.49 = (bf16[128,32768]{1,0:T(8,128)(2,1)}, f32[256,128]{1,0:T(8,128)S(1)}) custom-call(s32[2]{0:T(128)S(1)} %pad_add_fusion.at, bf16[128,32768]{1,0:T(8,128)(2,1)} %src.17, bf16[128,32768]{1,0:T(8,128)(2,1)} %src.17, bf16[128,32768]{1,0:T(8,128)(2,1)} %src.17, f32[1,32768]{1,0:T(1,128)S(1)} %bitcast.3), custom_call_target="tpu_custom_call" | custom-call | flops 2147483648 | bytes 25296904 | tf_op jit(solution)/shard_map/pallas_call | solution.py:23
  140.4 0.0 collective-permute-done.1.refs_0_.refs_1_.refs_2_
  140.4 20.9 %shard_map.53.refs_3_ = f32[256,256]{1,0:T(8,128)S(1)} custom-call(s32[2]{0:T(128)S(1)} %pad_add_fusion.at, bf16[128,32768]{1,0:T(8,128)(2,1)} %src.17, bf16[128,32768]{1,0:T(8,128)(2,1)} %get-tuple-element.30.applied, f32[1,32768]{1,0:T(1,128)S(1)} %bitcast.4, bf16[128,12288]{1,0:T(8,128)(2,1)} %collective-permute-done.1.refs_0_.refs_1_.refs_2_, ...), custom_call_target="tpu_custom_call" | custom-call | flops 1610612736 | bytes 21102600 | tf_op jit(solution)/shard_map/pallas_call | solution.py:23
  161.2 0.0 collective-permute-done.refs_0_
  161.3 8.2 %shard_map.54 = (f32[128,256]{1,0:T(8,128)S(1)}, f32[128,256]{1,0:T(8,128)S(1)}) custom-call(s32[2]{0:T(128)S(1)} %pad_add_fusion.at, bf16[128,32768]{1,0:T(8,128)(2,1)} %src.17, bf16[128,32768]{1,0:T(8,128)(2,1)} %get-tuple-element.30.applied, f32[1,32768]{1,0:T(1,128)S(1)} %bitcast.5, bf16[128,4096]{1,0:T(8,128)(2,1)S(1)} %collective-permute-done.refs_0_, ...), custom_call_target="tpu_custom_call" | custom-call | flops 536870912 | bytes 24510472 | tf_op jit(solution)/shard_map/pallas_call | solution.py:23
  169.5 0.1 collective-permute-start.3
  169.6 1.0 shard_map.66
  170.6 2.1 collective-permute-start.7
  172.6 0.9 shard_map.68
  173.6 0.9 shard_map.70
  174.5 4.5 %collective-permute-done.3.refs_0_ = f32[128,128]{1,0:T(8,128)S(1)} collective-permute-done((f32[128,128]{1,0:T(8,128)S(1)}, f32[128,128]{1,0:T(8,128)S(1)}, u32[]{:S(2)}, u32[]{:S(2)}) %collective-permute-start.3) | collective-permute-done | bytes 65568 | tf_op jit(solution)/shard_map/ppermute | solution.py:468
  179.0 2.0 collective-permute-start.8
  181.0 0.8 shard_map.55
  181.8 2.4 %shard_map.60 = (bf16[128,32768]{1,0:T(8,128)(2,1)}, f32[128,128]{1,0:T(8,128)S(1)}) custom-call(bf16[128,256]{1,0:T(8,128)(2,1)S(1)} %get-tuple-element.33.coef, bf16[128,32768]{1,0:T(8,128)(2,1)} %src.17, bf16[128,32768]{1,0:T(8,128)(2,1)} %get-tuple-element.30.applied, bf16[128,2048]{1,0:T(8,128)(2,1)S(1)} %collective-permute-done.2.refs_1_.refs_2_.refs_0_), custom_call_target="tpu_custom_call" | custom-call | flops 268435456 | bytes 17367040 | tf_op jit(solution)/shard_map/pallas_call | solution.py:23
  184.1 5.9 %shard_map.61 = (bf16[128,32768]{1,0:T(8,128)(2,1)}, f32[128,128]{1,0:T(8,128)S(1)}) custom-call(bf16[128,256]{1,0:T(8,128)(2,1)S(1)} %get-tuple-element.33.coef, bf16[128,32768]{1,0:T(8,128)(2,1)} %src.17, bf16[128,32768]{1,0:T(8,128)(2,1)} %get-tuple-element.30.applied, ...), custom_call_target="tpu_custom_call", output_to_operand_aliasing={{0}: (4, {})} | custom-call | flops 1610612736 | bytes 28442624 | tf_op jit(solution)/shard_map/pallas_call | solution.py:23
  190.1 1.8 shard_map.56
  191.9 3.1 %shard_map.62 = (bf16[128,32768]{1,0:T(8,128)(2,1)}, f32[128,128]{1,0:T(8,128)S(1)}) custom-call(bf16[128,256]{1,0:T(8,128)(2,1)S(1)} %get-tuple-element.33.coef, bf16[128,32768]{1,0:T(8,128)(2,1)} %src.17, bf16[128,32768]{1,0:T(8,128)(2,1)} %get-tuple-element.30.applied, ...), custom_call_target="tpu_custom_call", output_to_operand_aliasing={{0}: (4, {})} | custom-call | flops 536870912 | bytes 26345472 | tf_op jit(solution)/shard_map/pallas_call | solution.py:23
  195.0 0.0 collective-permute-done.6.refs_0_
  195.0 0.1 collective-permute-start.9
  195.0 3.2 %shard_map.63 = (bf16[128,32768]{1,0:T(8,128)(2,1)}, f32[128,128]{1,0:T(8,128)S(1)}) custom-call(bf16[128,256]{1,0:T(8,128)(2,1)S(1)} %get-tuple-element.33.coef, bf16[128,32768]{1,0:T(8,128)(2,1)} %src.17, bf16[128,32768]{1,0:T(8,128)(2,1)} %get-tuple-element.30.applied, ...), custom_call_target="tpu_custom_call", output_to_operand_aliasing={{0}: (4, {})} | custom-call | flops 536870912 | bytes 26345472 | tf_op jit(solution)/shard_map/pallas_call | solution.py:23
  198.2 0.0 collective-permute-done.5.refs_0_
  198.2 3.2 %shard_map.64 = (bf16[128,32768]{1,0:T(8,128)(2,1)}, f32[128,128]{1,0:T(8,128)S(1)}) custom-call(bf16[128,256]{1,0:T(8,128)(2,1)S(1)} %get-tuple-element.33.coef, bf16[128,32768]{1,0:T(8,128)(2,1)} %src.17, bf16[128,32768]{1,0:T(8,128)(2,1)} %get-tuple-element.30.applied, ...), custom_call_target="tpu_custom_call", output_to_operand_aliasing={{0}: (4, {})} | custom-call | flops 536870912 | bytes 26345472 | tf_op jit(solution)/shard_map/pallas_call | solution.py:23
  201.4 0.0 collective-permute-done.4.refs_0_
  201.4 3.2 %shard_map.65 = (bf16[128,32768]{1,0:T(8,128)(2,1)}, f32[128,128]{1,0:T(8,128)S(1)}) custom-call(bf16[128,256]{1,0:T(8,128)(2,1)S(1)} %get-tuple-element.33.coef, bf16[128,32768]{1,0:T(8,128)(2,1)} %src.17, bf16[128,32768]{1,0:T(8,128)(2,1)} %get-tuple-element.30.applied, ...), custom_call_target="tpu_custom_call", output_to_operand_aliasing={{0}: (4, {})} | custom-call | flops 536870912 | bytes 26345472 | tf_op jit(solution)/shard_map/pallas_call | solution.py:23
  204.6 0.0 collective-permute-done.7.refs_0_
  204.6 0.9 shard_map.67
  205.5 0.0 collective-permute-done.8.refs_0_
  205.5 0.9 shard_map.69
  206.4 0.0 collective-permute-done.9.refs_0_
  206.4 1.0 shard_map.71
  (1 shorter events, 0.0 us)
Async XLA Ops:
  4.3 136.1 %collective-permute-start.1 = (bf16[128,12288]{1,0:T(8,128)(2,1)}, bf16[128,12288]{1,0:T(8,128)(2,1)}, u32[]{:S(2)}, u32[]{:S(2)}) collective-permute-start(bf16[128,12288]{1,0:T(8,128)(2,1)} %shard_map.51), channel_id=1, source_target_pairs={{0,1},{1,0},{2,3},{3,2},{4,5},{5,4},{6,7},{7,6},{8,9},{9,8},{10,11... | collective-permute-start | bytes 9437192 | tf_op jit(solution)/shard_map/ppermute | solution.py:450
  8.3 79.3 %collective-permute-start.2 = (bf16[128,2048]{1,0:T(8,128)(2,1)S(1)}, bf16[128,2048]{1,0:T(8,128)(2,1)S(1)}, u32[]{:S(2)}, u32[]{:S(2)}) collective-permute-start(bf16[128,2048]{1,0:T(8,128)(2,1)S(1)} %shard_map.52), channel_id=1, source_target_pairs={{0,1},{1,0},{2,3},{3,2},{4,5},{5,4},{6,7},{7,6},{8,9},{9,8},{10,11... | collective-permute-start | bytes 1572872 | tf_op jit(solution)/shard_map/ppermute | solution.py:450
  10.7 150.6 %collective-permute-start = (bf16[128,4096]{1,0:T(8,128)(2,1)}, bf16[128,4096]{1,0:T(8,128)(2,1)S(1)}, u32[]{:S(2)}, u32[]{:S(2)}) collective-permute-start(bf16[128,4096]{1,0:T(8,128)(2,1)} %shard_map.50), channel_id=1, source_target_pairs={{0,1},{1,0},{2,3},{3,2},{4,5},{5,4},{6,7},{7,6},{8,9},{9,8},{10,11... | collective-permute-start | bytes 3145736 | tf_op jit(solution)/shard_map/ppermute | solution.py:450
  14.9 74.8 %copy-start = (f32[32768]{0:T(1024)S(1)}, f32[32768]{0:T(1024)}, u32[]{:S(2)}) copy-start(f32[32768]{0:T(1024)} %param.3) | copy-start | bytes 393220
  15.0 180.0 %collective-permute-start.6 = (bf16[128,4096]{1,0:T(8,128)(2,1)}, bf16[128,4096]{1,0:T(8,128)(2,1)}, u32[]{:S(2)}, u32[]{:S(2)}) collective-permute-start(bf16[128,4096]{1,0:T(8,128)(2,1)} %shard_map.59), channel_id=1, source_target_pairs={{0,1},{1,0},{2,3},{3,2},{4,5},{5,4},{6,7},{7,6},{8,9},{9,8},{10,11... | collective-permute-start | bytes 3145736 | tf_op jit(solution)/shard_map/ppermute | solution.py:450
  17.3 180.9 %collective-permute-start.5 = (bf16[128,4096]{1,0:T(8,128)(2,1)}, bf16[128,4096]{1,0:T(8,128)(2,1)}, u32[]{:S(2)}, u32[]{:S(2)}) collective-permute-start(bf16[128,4096]{1,0:T(8,128)(2,1)} %shard_map.58), channel_id=1, source_target_pairs={{0,1},{1,0},{2,3},{3,2},{4,5},{5,4},{6,7},{7,6},{8,9},{9,8},{10,11... | collective-permute-start | bytes 3145736 | tf_op jit(solution)/shard_map/ppermute | solution.py:450
  87.7 113.7 %collective-permute-start.4 = (bf16[128,4096]{1,0:T(8,128)(2,1)S(1)}, bf16[128,4096]{1,0:T(8,128)(2,1)}, u32[]{:S(2)}, u32[]{:S(2)}) collective-permute-start(bf16[128,4096]{1,0:T(8,128)(2,1)S(1)} %shard_map.57), channel_id=1, source_target_pairs={{0,1},{1,0},{2,3},{3,2},{4,5},{5,4},{6,7},{7,6},{8,9},{9,8},{10,11... | collective-permute-start | bytes 3145736 | tf_op jit(solution)/shard_map/ppermute | solution.py:450
  169.5 9.5 %collective-permute-start.3 = (f32[128,128]{1,0:T(8,128)S(1)}, f32[128,128]{1,0:T(8,128)S(1)}, u32[]{:S(2)}, u32[]{:S(2)}) collective-permute-start(f32[128,128]{1,0:T(8,128)S(1)} %slice.3), channel_id=1, source_target_pairs={{0,1},{1,0},{2,3},{3,2},{4,5},{5,4},{6,7},{7,6},{8,9},{9,8},{10,11... | collective-permute-start | bytes 196616 | tf_op jit(solution)/shard_map/ppermute | solution.py:468
  170.6 34.0 %collective-permute-start.7 = (bf16[128,1024]{1,0:T(8,128)(2,1)S(1)}, bf16[128,1024]{1,0:T(8,128)(2,1)S(1)}, u32[]{:S(2)}, u32[]{:S(2)}) collective-permute-start(bf16[128,1024]{1,0:T(8,128)(2,1)S(1)} %shard_map.66), channel_id=1, source_target_pairs={{0,1},{1,0},{2,3},{3,2},{4,5},{5,4},{6,7},{7,6},{8,9},{9,8},{10,11... | collective-permute-start | bytes 786440 | tf_op jit(solution)/shard_map/ppermute | solution.py:450
  179.0 26.6 %collective-permute-start.8 = (bf16[128,512]{1,0:T(8,128)(2,1)S(1)}, bf16[128,512]{1,0:T(8,128)(2,1)S(1)}, u32[]{:S(2)}, u32[]{:S(2)}) collective-permute-start(bf16[128,512]{1,0:T(8,128)(2,1)S(1)} %shard_map.68), channel_id=1, source_target_pairs={{0,1},{1,0},{2,3},{3,2},{4,5},{5,4},{6,7},{7,6},{8,9},{9,8},{10,11... | collective-permute-start | bytes 393224 | tf_op jit(solution)/shard_map/ppermute | solution.py:450
  195.0 11.4 %collective-permute-start.9 = (bf16[128,512]{1,0:T(8,128)(2,1)S(1)}, bf16[128,512]{1,0:T(8,128)(2,1)S(1)}, u32[]{:S(2)}, u32[]{:S(2)}) collective-permute-start(bf16[128,512]{1,0:T(8,128)(2,1)S(1)} %shard_map.70), channel_id=1, source_target_pairs={{0,1},{1,0},{2,3},{3,2},{4,5},{5,4},{6,7},{7,6},{8,9},{9,8},{10,11... | collective-permute-start | bytes 393224 | tf_op jit(solution)/shard_map/ppermute | solution.py:450
